TPU v7x, 256 devices: a whole 4x4x8 slice. The times are simulated.
256 devices in a mesh: leaf: 64 (over z, y, core), sub: 4 (over x).
Axes of the slice: x: 4, y: 4, z: 8, core: 2. Of those that a mesh axis runs over, the one named last changes fastest.
Arguments:
- sources: bfloat16 [524288, 64], P(('leaf', 'sub')), may hold values from -6 to 6
- leaf_basis: bfloat16 [2048, 256, 64], P(('leaf', 'sub')), may hold values from -0.375 to 0.375
- transfer: float32 [2, 64, 64], replicated, may hold values from -0.625 to 0.625
- coupling: float32 [3, 64, 64], replicated, may hold values from -0.5 to 0.5
- near_blocks: bfloat16 [2048, 4, 256, 256], P(('leaf', 'sub')), may hold values from -0.1875 to 0.1875
- near_pattern: int32 [2048, 4], P(('leaf', 'sub')), may hold values from 0 to 2047, as said below
- far_pattern: int32 [4092, 3], replicated, may hold values 0 or 1
Outputs:
- product: bfloat16 [524288, 64], P(('leaf', 'sub'))
Inputs may be any that keep to these rules, and one draw needn't show every extreme that they name: near_pattern[i, 0] = i; every entry j has j // 8 - i // 8 equal to 0, 1, -1, 4 or -4.
All inputs are finite; a program needn't handle non-finite values.
Results may differ from a plain program's by a relative error of at most 0.001.
Values may be sent and summed in bfloat16 or wider, within the bound.
No kernel may reach another device: no remote copies, remote signals or barrier semaphores. Data moves between devices by JAX's collectives and lax.ppermute only.
A program may use at most 64 MiB of HBM per device.

v0:
```python
import jax
import jax.numpy as jnp
from jax import lax
from jax.sharding import PartitionSpec as P

PRECISE = lax.Precision.HIGHEST


def padded(block, sides, width):
    for axis, dim in sides:
        count = lax.axis_size(axis)
        forward = [(i, i + 1) for i in range(count - 1)]
        backward = [(target, source) for source, target in forward]
        low = lax.ppermute(
            lax.slice_in_dim(block, block.shape[dim] - width, None, axis=dim), axis, forward
        )
        high = lax.ppermute(lax.slice_in_dim(block, 0, width, axis=dim), axis, backward)
        block = jnp.concatenate([low, block, high], axis=dim)
    return block


def swapped(array, axis, distance):
    return lax.ppermute(array, axis, [(i, i ^ 1 << distance) for i in range(lax.axis_size(axis))])


def lift_up(level_vals, transfer):
    paired = level_vals.reshape(-1, 2, level_vals.shape[1], level_vals.shape[2])
    left_part = jnp.einsum("jk,pjr->pkr", transfer[0], paired[:, 0], precision=PRECISE)
    right_part = jnp.einsum("jk,pjr->pkr", transfer[1], paired[:, 1], precision=PRECISE)
    return left_part + right_part


def expand_down(parent_field, transfer):
    first_child = jnp.einsum("kj,pjr->pkr", transfer[0], parent_field, precision=PRECISE)
    second_child = jnp.einsum("kj,pjr->pkr", transfer[1], parent_field, precision=PRECISE)
    stacked = jnp.stack([first_child, second_child], 1)
    return stacked.reshape(-1, parent_field.shape[1], parent_field.shape[2])


def couple_level(level_vals, mask_rows, coupling):
    grouped = level_vals.reshape(-1, 4, level_vals.shape[1], level_vals.shape[2])
    summed = jnp.zeros(level_vals.shape, jnp.float32)
    for offset in range(1, 4):
        shifted = jnp.roll(grouped, -offset, axis=1).reshape(level_vals.shape)
        product_term = jnp.einsum("ab,nbr->nar", coupling[offset - 1], shifted, precision=PRECISE)
        weights = mask_rows[:, offset - 1 : offset].astype(jnp.float32)[:, :, None]
        summed = summed + weights * product_term
    return summed


def level_share(whole_group, far_pattern, row_start, first_own, own_count, coupling):
    group_start = first_own // 4 * 4
    mask_rows = lax.dynamic_slice_in_dim(far_pattern, row_start + group_start, 4, 0)
    coupled = couple_level(whole_group, mask_rows, coupling)
    return lax.dynamic_slice_in_dim(coupled, first_own % 4, own_count, 0)


def shards(sources, leaf_basis, transfer, coupling, near_blocks, near_pattern, far_pattern):
    leaf_dev = leaf_basis.shape[0]
    leaf_points = leaf_basis.shape[1]
    rhs_width = sources.shape[1]
    device_total = lax.axis_size(("leaf", "sub"))
    device = lax.axis_index(("leaf", "sub"))
    sub_span = lax.axis_size("sub")
    bit_count = device_total.bit_length() - 1
    rows_dev = leaf_dev * leaf_points
    joined = padded(sources, ((("leaf", "sub"), 0),), rows_dev)
    leafwise = padded(sources, (("leaf", 0),), rows_dev)
    buffer = jnp.concatenate([leafwise[:rows_dev], joined, leafwise[2 * rows_dev :]], 0)
    buffer = buffer.reshape(5 * leaf_dev, leaf_points, rhs_width)
    device_gap = near_pattern // leaf_dev - device
    slot_block = jnp.where(
        device_gap == -sub_span,
        0,
        jnp.where(
            device_gap == -1, 1, jnp.where(device_gap == 0, 2, jnp.where(device_gap == 1, 3, 4))
        ),
    )
    gathered = buffer[slot_block * leaf_dev + near_pattern % leaf_dev]
    near_part = jnp.einsum(
        "lsab,lsbr->lar", near_blocks, gathered, preferred_element_type=jnp.float32
    )
    points = sources.reshape(leaf_dev, leaf_points, rhs_width)
    upward = [jnp.einsum("lpk,lpr->lkr", leaf_basis, points, preferred_element_type=jnp.float32)]
    while upward[-1].shape[0] > 1:
        upward.append(lift_up(upward[-1], transfer))
    local_depth = len(upward) - 1
    total_leaves = leaf_dev * device_total
    top_level = local_depth + bit_count - 2
    row_starts = [0]
    for level_id in range(top_level):
        row_starts.append(row_starts[-1] + (total_leaves >> level_id))
    locals_list = []
    for level_id in range(local_depth - 1):
        level_vals = upward[level_id]
        cluster_count = level_vals.shape[0]
        mask_rows = lax.dynamic_slice_in_dim(
            far_pattern, row_starts[level_id] + device * cluster_count, cluster_count, 0
        )
        locals_list.append(couple_level(level_vals, mask_rows, coupling))
    cross_local = {}
    half_group = upward[local_depth - 1]
    for bit_id in range(bit_count):
        partner_half = swapped(half_group, ("leaf", "sub"), bit_id)
        upper_side = device >> bit_id & 1
        whole_group = jnp.where(
            upper_side == 1,
            jnp.concatenate([partner_half, half_group], 0),
            jnp.concatenate([half_group, partner_half], 0),
        )
        level_id = local_depth - 1 + bit_id
        first_own = device * leaf_dev >> level_id
        own_count = 2 if bit_id == 0 else 1
        cross_local[level_id] = level_share(
            whole_group, far_pattern, row_starts[level_id], first_own, own_count, coupling
        )
        if bit_id + 1 < bit_count:
            own_parent = lift_up(half_group, transfer)
            sibling = lift_up(partner_half, transfer)
            half_group = jnp.where(
                upper_side == 1,
                jnp.concatenate([sibling, own_parent], 0),
                jnp.concatenate([own_parent, sibling], 0),
            )
    field_down = cross_local[top_level]
    for level_id in range(top_level - 1, local_depth - 1, -1):
        position = device * leaf_dev >> level_id & 1
        chosen = lax.dynamic_index_in_dim(transfer, position, 0, keepdims=False)
        field_down = cross_local[level_id] + jnp.einsum(
            "kj,pjr->pkr", chosen, field_down, precision=PRECISE
        )
    field_down = cross_local[local_depth - 1] + expand_down(field_down, transfer)
    for level_id in range(local_depth - 2, -1, -1):
        field_down = locals_list[level_id] + expand_down(field_down, transfer)
    far_part = jnp.einsum(
        "lpk,lkr->lpr", leaf_basis.astype(jnp.float32), field_down, precision=PRECISE
    )
    return (far_part + near_part).reshape(rows_dev, rhs_width).astype(jnp.bfloat16)


def solution(mesh):
    placed = (
        P(("leaf", "sub"), None),
        P(("leaf", "sub"), None, None),
        P(),
        P(),
        P(("leaf", "sub"), None, None, None),
        P(("leaf", "sub"), None),
        P(),
    )
    return jax.shard_map(
        shards, mesh=mesh, in_specs=placed, out_specs=P(("leaf", "sub"), None), check_vma=False
    )
```

profile of v0, /device:TPU:2, one launch (start us, length us, event | category | flops | bytes accessed | tf_op | source)
XLA Modules:
  0.0 104.7 jit_solution(8621229878127772205)
XLA Ops:
  0.0 1.9 %collective-permute-start.8 = (bf16[2048,64]{0,1:T(8,128)(2,1)}, bf16[2048,64]{0,1:T(8,128)(2,1)S(1)}, u32[]{:S(2)}, u32[]{:S(2)}) collective-permute-start(bf16[2048,64]{0,1:T(8,128)(2,1)} %param.7), channel_id=1, source_target_pairs={{0,4},{4,8},{8,12},{12,16},{16,20},{20,24},{24,28},{28,32},{32,36}... | collective-permute-start | bytes 786440 | tf_op jit(solution)/shard_map/ppermute | solution.py:14
  1.9 3.4 %collective-permute-start.9 = (bf16[2048,64]{0,1:T(8,128)(2,1)}, bf16[2048,64]{0,1:T(8,128)(2,1)S(1)}, u32[]{:S(2)}, u32[]{:S(2)}) collective-permute-start(bf16[2048,64]{0,1:T(8,128)(2,1)} %param.7), channel_id=1, source_target_pairs={{0,1},{1,2},{2,3},{3,4},{4,5},{5,6},{6,7},{7,8},{8,9},{9,10},{10,1... | collective-permute-start | bytes 786440 | tf_op jit(solution)/shard_map/ppermute | solution.py:14
  5.3 2.5 %collective-permute-start.10 = (bf16[2048,64]{0,1:T(8,128)(2,1)}, bf16[2048,64]{0,1:T(8,128)(2,1)S(1)}, u32[]{:S(2)}, u32[]{:S(2)}) collective-permute-start(bf16[2048,64]{0,1:T(8,128)(2,1)} %param.7), channel_id=1, source_target_pairs={{1,0},{2,1},{3,2},{4,3},{5,4},{6,5},{7,6},{8,7},{9,8},{10,9},{11,1... | collective-permute-start | bytes 786440 | tf_op jit(solution)/shard_map/ppermute | solution.py:17
  7.8 1.3 %collective-permute-start.11 = (bf16[2048,64]{0,1:T(8,128)(2,1)}, bf16[2048,64]{0,1:T(8,128)(2,1)S(1)}, u32[]{:S(2)}, u32[]{:S(2)}) collective-permute-start(bf16[2048,64]{0,1:T(8,128)(2,1)} %param.7), channel_id=1, source_target_pairs={{4,0},{8,4},{12,8},{16,12},{20,16},{24,20},{28,24},{32,28},{36,32}... | collective-permute-start | bytes 786440 | tf_op jit(solution)/shard_map/ppermute | solution.py:17
  9.1 1.2 %fusion.24 = f32[8,64,64]{2,1,0:T(8,128)S(1)} fusion(bf16[8,256,64]{1,2,0:T(8,128)(2,1)S(1)} %copy-done, bf16[8,8,8,256]{3,2,1,0:T(8,128)(2,1)} %bitcast.672), kind=kOutput, calls=%fused_computation.62 | convolution fusion | flops 16777216 | bytes 655360 | tf_op jit(solution)/shard_map/lpk,lpr->lkr/dot_general | solution.py:84
  10.2 1.1 %fusion.27 = f32[4,64,64]{2,1,0:T(8,128)S(1)} fusion(f32[4,2,64,64]{3,2,1,0:T(8,128)S(1)} %bitcast.661, f32[2,64,64]{2,1,0:T(8,128)} %param.9), kind=kOutput, calls=%fused_computation.71 | convolution fusion | flops 12582912 | bytes 229376 | tf_op jit(solution)/shard_map/jk,pjr->pkr/dot_general | solution.py:28
  11.4 1.1 %convolution_add_fusion.1 = f32[4,64,64]{2,1,0:T(8,128)S(1)} fusion(f32[4,64,64]{2,1,0:T(8,128)S(1)} %fusion.27, f32[4,2,64,64]{3,2,1,0:T(8,128)S(1)} %bitcast.662, f32[2,64,64]{2,1,0:T(8,128)} %param.9), kind=kOutput, calls=%fused_computation.18 | convolution fusion | flops 12599296 | bytes 360448 | tf_op jit(solution)/shard_map/jk,pjr->pkr/dot_general | solution.py:29
  14.2 1.0 constant_dynamic-slice_fusion.8
  15.1 0.8 constant_dynamic-slice_fusion.9
  17.2 1.3 %fusion.5 = f32[8,64,64]{2,1,0:T(8,128)} fusion(f32[8,64,64]{2,1,0:T(8,128)S(1)} %convolution_multiply_fusion.2, f32[8,64,64]{2,1,0:T(8,128)S(1)} %bitcast.675, f32[8]{0:T(128)S(1)} %get-tuple-element.75, f32[3,64,64]{2,1,0:T(8,128)S(1)} %copy-done.2), kind=kOutput, calls=%fused_computation.11 | convolution fusion | flops 25231360 | bytes 688640 | tf_op jit(solution)/shard_map/ab,nbr->nar/dot_general | solution.py:45
  18.5 0.6 dynamic-slice.42
  19.1 0.6 dynamic-slice.40
  19.7 0.6 dynamic-slice.38
  20.4 0.6 dynamic-slice.37
  21.0 0.6 dynamic-slice.36
  22.8 0.7 dynamic-slice.33
  23.4 0.7 dynamic-slice.32
  24.7 0.6 dynamic-slice.30
  25.3 0.6 dynamic-slice.29
  26.5 0.7 dynamic-slice.27
  27.1 0.6 dynamic-slice.26
  27.8 0.6 dynamic-slice.25
  28.4 0.6 dynamic-slice.24
  29.0 0.6 dynamic-slice.23
  29.6 0.6 dynamic-slice.22
  30.3 0.6 dynamic-slice.21
  32.4 2.8 %collective-permute-start.1 = (f32[2,64,64]{1,2,0:T(8,128)S(1)}, f32[2,64,64]{1,2,0:T(8,128)S(1)}, u32[]{:S(2)}, u32[]{:S(2)}) collective-permute-start(f32[2,64,64]{1,2,0:T(8,128)S(1)} %maximum_select_fusion.8), channel_id=1, source_target_pairs={{0,2},{1,3},{2,0},{3,1},{4,6},{5,7},{6,4},{7,5},{8,10},{9,11},{10,... | collective-permute-start | bytes 98312 | tf_op jit(solution)/shard_map/ppermute | solution.py:23
  36.1 2.2 %collective-permute-done.1 = f32[2,64,64]{1,2,0:T(8,128)S(1)} collective-permute-done((f32[2,64,64]{1,2,0:T(8,128)S(1)}, f32[2,64,64]{1,2,0:T(8,128)S(1)}, u32[]{:S(2)}, u32[]{:S(2)}) %collective-permute-start.1) | collective-permute-done | bytes 32800 | tf_op jit(solution)/shard_map/ppermute | solution.py:23
  39.1 2.4 %collective-permute-start.2 = (f32[2,64,64]{1,2,0:T(8,128)S(1)}, f32[2,64,64]{1,2,0:T(8,128)S(1)}, u32[]{:S(2)}, u32[]{:S(2)}) collective-permute-start(f32[2,64,64]{1,2,0:T(8,128)S(1)} %maximum_select_fusion.10), channel_id=1, source_target_pairs={{0,4},{1,5},{2,6},{3,7},{4,0},{5,1},{6,2},{7,3},{8,12},{9,13},{10,... | collective-permute-start | bytes 98312 | tf_op jit(solution)/shard_map/ppermute | solution.py:23
  43.2 3.5 %collective-permute-start.3 = (f32[2,64,64]{1,2,0:T(8,128)S(1)}, f32[2,64,64]{1,2,0:T(8,128)S(1)}, u32[]{:S(2)}, u32[]{:S(2)}) collective-permute-start(f32[2,64,64]{1,2,0:T(8,128)S(1)} %maximum_select_fusion.12), channel_id=1, source_target_pairs={{0,8},{1,9},{2,10},{3,11},{4,12},{5,13},{6,14},{7,15},{8,0},{9,1},... | collective-permute-start | bytes 98312 | tf_op jit(solution)/shard_map/ppermute | solution.py:23
  47.5 1.6 %collective-permute-done.3 = f32[2,64,64]{1,2,0:T(8,128)S(1)} collective-permute-done((f32[2,64,64]{1,2,0:T(8,128)S(1)}, f32[2,64,64]{1,2,0:T(8,128)S(1)}, u32[]{:S(2)}, u32[]{:S(2)}) %collective-permute-start.3) | collective-permute-done | bytes 32800 | tf_op jit(solution)/shard_map/ppermute | solution.py:23
  49.9 3.6 %collective-permute-start.4 = (f32[2,64,64]{1,2,0:T(8,128)S(1)}, f32[2,64,64]{1,2,0:T(8,128)S(1)}, u32[]{:S(2)}, u32[]{:S(2)}) collective-permute-start(f32[2,64,64]{1,2,0:T(8,128)S(1)} %maximum_select_fusion.14), channel_id=1, source_target_pairs={{0,16},{1,17},{2,18},{3,19},{4,20},{5,21},{6,22},{7,23},{8,24},{9,... | collective-permute-start | bytes 98312 | tf_op jit(solution)/shard_map/ppermute | solution.py:23
  54.3 1.5 %collective-permute-done.4 = f32[2,64,64]{1,2,0:T(8,128)S(1)} collective-permute-done((f32[2,64,64]{1,2,0:T(8,128)S(1)}, f32[2,64,64]{1,2,0:T(8,128)S(1)}, u32[]{:S(2)}, u32[]{:S(2)}) %collective-permute-start.4) | collective-permute-done | bytes 32800 | tf_op jit(solution)/shard_map/ppermute | solution.py:23
  56.5 4.6 %collective-permute-start.5 = (f32[2,64,64]{1,2,0:T(8,128)S(1)}, f32[2,64,64]{1,2,0:T(8,128)S(1)}, u32[]{:S(2)}, u32[]{:S(2)}) collective-permute-start(f32[2,64,64]{1,2,0:T(8,128)S(1)} %maximum_select_fusion.16), channel_id=1, source_target_pairs={{0,32},{1,33},{2,34},{3,35},{4,36},{5,37},{6,38},{7,39},{8,40},{9,... | collective-permute-start | bytes 98312 | tf_op jit(solution)/shard_map/ppermute | solution.py:23
  61.9 1.4 %collective-permute-done.5 = f32[2,64,64]{1,2,0:T(8,128)S(1)} collective-permute-done((f32[2,64,64]{1,2,0:T(8,128)S(1)}, f32[2,64,64]{1,2,0:T(8,128)S(1)}, u32[]{:S(2)}, u32[]{:S(2)}) %collective-permute-start.5) | collective-permute-done | bytes 32800 | tf_op jit(solution)/shard_map/ppermute | solution.py:23
  63.8 3.5 %collective-permute-start.6 = (f32[2,64,64]{1,2,0:T(8,128)S(1)}, f32[2,64,64]{1,2,0:T(8,128)S(1)}, u32[]{:S(2)}, u32[]{:S(2)}) collective-permute-start(f32[2,64,64]{1,2,0:T(8,128)S(1)} %maximum_select_fusion.18), channel_id=1, source_target_pairs={{0,64},{1,65},{2,66},{3,67},{4,68},{5,69},{6,70},{7,71},{8,72},{9,... | collective-permute-start | bytes 98312 | tf_op jit(solution)/shard_map/ppermute | solution.py:23
  68.5 1.1 %collective-permute-done.6 = f32[2,64,64]{1,2,0:T(8,128)S(1)} collective-permute-done((f32[2,64,64]{1,2,0:T(8,128)S(1)}, f32[2,64,64]{1,2,0:T(8,128)S(1)}, u32[]{:S(2)}, u32[]{:S(2)}) %collective-permute-start.6) | collective-permute-done | bytes 32800 | tf_op jit(solution)/shard_map/ppermute | solution.py:23
  70.0 8.9 %collective-permute-start.7 = (f32[2,64,64]{1,2,0:T(8,128)S(1)}, f32[2,64,64]{1,2,0:T(8,128)S(1)}, u32[]{:S(2)}, u32[]{:S(2)}) collective-permute-start(f32[2,64,64]{1,2,0:T(8,128)S(1)} %maximum_select_fusion.20), channel_id=1, source_target_pairs={{0,128},{1,129},{2,130},{3,131},{4,132},{5,133},{6,134},{7,135},{8... | collective-permute-start | bytes 98312 | tf_op jit(solution)/shard_map/ppermute | solution.py:23
  79.7 1.4 %collective-permute-done.7 = f32[2,64,64]{1,2,0:T(8,128)S(1)} collective-permute-done((f32[2,64,64]{1,2,0:T(8,128)S(1)}, f32[2,64,64]{1,2,0:T(8,128)S(1)}, u32[]{:S(2)}, u32[]{:S(2)}) %collective-permute-start.7) | collective-permute-done | bytes 32800 | tf_op jit(solution)/shard_map/ppermute | solution.py:23
  82.0 3.9 %fusion.13 = f32[64,64]{0,1:T(8,128)S(1)} fusion(f32[4,64,64]{2,1,0:T(8,128)S(1)} %fusion.103, s32[]{:T(128)S(6)} %select_n.515, f32[4,64,64]{2,1,0:T(8,128)S(1)} %fusion.100, f32[4,64,64]{2,1,0:T(8,128)S(1)} %fusion.97, f32[4,64,64]{2,1,0:T(8,128)S(1)} %fusion.94, s32[]{:T(128)S(6)} %select_n.505, f32[4,64,64]{2,1,0:T(8,128)S(1)} %fusion.91, ...), kind=kOutput, calls=%fused_computation.51 | convolution fusion | flops 3190784 | bytes 245796 | tf_op jit(solution)/shard_map/kj,pjr->pkr/dot_general | solution.py:129
  86.0 2.1 %fusion.15 = f32[64,64]{0,1:T(8,128)S(1)} fusion(f32[64,64]{0,1:T(8,128)S(1)} %fusion.13, f32[4,64,64]{2,1,0:T(8,128)S(1)} %fusion.85, s32[]{:T(128)S(6)} %select_n.495, f32[4,64,64]{2,1,0:T(8,128)S(1)} %fusion.82, f32[4,64,64]{2,1,0:T(8,128)S(1)} %fusion.79, f32[2,64,64]{2,1,0:T(8,128)S(1)} %copy-done.1, s32[]{:T(128)S(6)} %select_n.517, ...), kind=kOutput, calls=%fused_computation.53 | convolution fusion | flops 3170304 | bytes 180244 | tf_op jit(solution)/shard_map/kj,pjr->pkr/dot_general | solution.py:129
  88.1 2.0 %fusion.17 = f32[64,64]{0,1:T(8,128)S(1)} fusion(f32[64,64]{0,1:T(8,128)S(1)} %fusion.15, f32[4,64,64]{2,1,0:T(8,128)S(1)} %fusion.76, s32[]{:T(128)S(6)} %select_n.485, f32[4,64,64]{2,1,0:T(8,128)S(1)} %fusion.73, f32[4,64,64]{2,1,0:T(8,128)S(1)} %fusion.70, f32[2,64,64]{2,1,0:T(8,128)S(1)} %copy-done.1, s32[]{:T(128)S(6)} %select_n.518, ...), kind=kOutput, calls=%fused_computation.55 | convolution fusion | flops 3170304 | bytes 180244 | tf_op jit(solution)/shard_map/kj,pjr->pkr/dot_general | solution.py:129
  90.1 2.1 %fusion.19 = f32[64,64]{0,1:T(8,128)S(1)} fusion(f32[64,64]{0,1:T(8,128)S(1)} %fusion.17, f32[4,64,64]{2,1,0:T(8,128)S(1)} %fusion.67, s32[]{:T(128)S(6)} %select_n.475, f32[4,64,64]{2,1,0:T(8,128)S(1)} %fusion.64, f32[4,64,64]{2,1,0:T(8,128)S(1)} %fusion.61, f32[2,64,64]{2,1,0:T(8,128)S(1)} %copy-done.1, s32[]{:T(128)S(6)} %select_n.519, ...), kind=kOutput, calls=%fused_computation.57 | convolution fusion | flops 3170304 | bytes 180244 | tf_op jit(solution)/shard_map/kj,pjr->pkr/dot_general | solution.py:129
  92.2 2.1 %fusion.21 = f32[64,64]{0,1:T(8,128)S(1)} fusion(f32[64,64]{0,1:T(8,128)S(1)} %fusion.19, f32[4,64,64]{2,1,0:T(8,128)S(1)} %fusion.58, s32[]{:T(128)S(6)} %select_n.465, f32[4,64,64]{2,1,0:T(8,128)S(1)} %fusion.55, f32[4,64,64]{2,1,0:T(8,128)S(1)} %fusion.52, f32[2,64,64]{2,1,0:T(8,128)S(1)} %copy-done.1, s32[]{:T(128)S(6)} %select_n.520, ...), kind=kOutput, calls=%fused_computation.59 | convolution fusion | flops 3170304 | bytes 180244 | tf_op jit(solution)/shard_map/kj,pjr->pkr/dot_general | solution.py:129
  94.3 2.0 %fusion.23 = f32[64,64]{0,1:T(8,128)S(1)} fusion(f32[64,64]{0,1:T(8,128)S(1)} %fusion.21, f32[4,64,64]{2,1,0:T(8,128)S(1)} %fusion.49, s32[]{:T(128)S(6)} %select_n.455, f32[4,64,64]{2,1,0:T(8,128)S(1)} %fusion.46, f32[4,64,64]{2,1,0:T(8,128)S(1)} %fusion.43, f32[2,64,64]{2,1,0:T(8,128)S(1)} %copy-done.1, s32[]{:T(128)S(6)} %select_n.521, ...), kind=kOutput, calls=%fused_computation.61 | convolution fusion | flops 3170304 | bytes 180244 | tf_op jit(solution)/shard_map/kj,pjr->pkr/dot_general | solution.py:129
  98.8 0.6 gather_fusion
  99.4 3.6 %convolution_bitcast_fusion = f32[8,64,256]{2,1,0:T(8,128)S(1)} fusion(bf16[8,4,256,64]{2,3,1,0:T(8,128)(2,1)S(1)} %bitcast.659, bf16[8,4,256,256]{3,2,1,0:T(8,128)(2,1)} %param.11), kind=kOutput, calls=%fused_computation.2 | convolution fusion | flops 268435456 | bytes 5767168 | tf_op jit(solution)/shard_map/lsab,lsbr->lar/dot_general | solution.py:80
  104.0 0.7 copy.47
  (175 shorter events, 19.9 us)
Async XLA Ops:
  0.0 9.1 %copy-start = (bf16[8,256,64]{1,2,0:T(8,128)(2,1)S(1)}, bf16[8,256,64]{1,2,0:T(8,128)(2,1)}, u32[]{:S(2)}) copy-start(bf16[8,256,64]{1,2,0:T(8,128)(2,1)} %param.8) | copy-start | bytes 786436
  0.0 12.5 %copy-start.1 = (f32[2,64,64]{2,1,0:T(8,128)S(1)}, f32[2,64,64]{2,1,0:T(8,128)}, u32[]{:S(2)}) copy-start(f32[2,64,64]{2,1,0:T(8,128)} %param.9) | copy-start | bytes 98308
  0.0 97.2 %collective-permute-start.8 = (bf16[2048,64]{0,1:T(8,128)(2,1)}, bf16[2048,64]{0,1:T(8,128)(2,1)S(1)}, u32[]{:S(2)}, u32[]{:S(2)}) collective-permute-start(bf16[2048,64]{0,1:T(8,128)(2,1)} %param.7), channel_id=1, source_target_pairs={{0,4},{4,8},{8,12},{12,16},{16,20},{20,24},{24,28},{28,32},{32,36}... | collective-permute-start | bytes 786440 | tf_op jit(solution)/shard_map/ppermute | solution.py:14
  1.9 95.6 %collective-permute-start.9 = (bf16[2048,64]{0,1:T(8,128)(2,1)}, bf16[2048,64]{0,1:T(8,128)(2,1)S(1)}, u32[]{:S(2)}, u32[]{:S(2)}) collective-permute-start(bf16[2048,64]{0,1:T(8,128)(2,1)} %param.7), channel_id=1, source_target_pairs={{0,1},{1,2},{2,3},{3,4},{4,5},{5,6},{6,7},{7,8},{8,9},{9,10},{10,1... | collective-permute-start | bytes 786440 | tf_op jit(solution)/shard_map/ppermute | solution.py:14
  5.3 92.9 %collective-permute-start.10 = (bf16[2048,64]{0,1:T(8,128)(2,1)}, bf16[2048,64]{0,1:T(8,128)(2,1)S(1)}, u32[]{:S(2)}, u32[]{:S(2)}) collective-permute-start(bf16[2048,64]{0,1:T(8,128)(2,1)} %param.7), channel_id=1, source_target_pairs={{1,0},{2,1},{3,2},{4,3},{5,4},{6,5},{7,6},{8,7},{9,8},{10,9},{11,1... | collective-permute-start | bytes 786440 | tf_op jit(solution)/shard_map/ppermute | solution.py:17
  7.8 90.5 %collective-permute-start.11 = (bf16[2048,64]{0,1:T(8,128)(2,1)}, bf16[2048,64]{0,1:T(8,128)(2,1)S(1)}, u32[]{:S(2)}, u32[]{:S(2)}) collective-permute-start(bf16[2048,64]{0,1:T(8,128)(2,1)} %param.7), channel_id=1, source_target_pairs={{4,0},{8,4},{12,8},{16,12},{20,16},{24,20},{28,24},{32,28},{36,32}... | collective-permute-start | bytes 786440 | tf_op jit(solution)/shard_map/ppermute | solution.py:17
  12.8 0.7 copy-start.5
  13.0 18.7 %collective-permute-start = (f32[2,64,64]{1,2,0:T(8,128)S(1)}, f32[2,64,64]{1,2,0:T(8,128)S(1)}, u32[]{:S(2)}, u32[]{:S(2)}) collective-permute-start(f32[2,64,64]{1,2,0:T(8,128)S(1)} %bitcast.677), channel_id=1, source_target_pairs={{0,1},{1,0},{2,3},{3,2},{4,5},{5,4},{6,7},{7,6},{8,9},{9,8},{10,11... | collective-permute-start | bytes 98312 | tf_op jit(solution)/shard_map/ppermute | solution.py:23
  13.2 2.8 %copy-start.2 = (f32[3,64,64]{2,1,0:T(8,128)S(1)}, f32[3,64,64]{2,1,0:T(8,128)}, u32[]{:S(2)}) copy-start(f32[3,64,64]{2,1,0:T(8,128)} %param.10) | copy-start | bytes 147460
  32.4 5.9 %collective-permute-start.1 = (f32[2,64,64]{1,2,0:T(8,128)S(1)}, f32[2,64,64]{1,2,0:T(8,128)S(1)}, u32[]{:S(2)}, u32[]{:S(2)}) collective-permute-start(f32[2,64,64]{1,2,0:T(8,128)S(1)} %maximum_select_fusion.8), channel_id=1, source_target_pairs={{0,2},{1,3},{2,0},{3,1},{4,6},{5,7},{6,4},{7,5},{8,10},{9,11},{10,... | collective-permute-start | bytes 98312 | tf_op jit(solution)/shard_map/ppermute | solution.py:23
  39.1 3.3 %collective-permute-start.2 = (f32[2,64,64]{1,2,0:T(8,128)S(1)}, f32[2,64,64]{1,2,0:T(8,128)S(1)}, u32[]{:S(2)}, u32[]{:S(2)}) collective-permute-start(f32[2,64,64]{1,2,0:T(8,128)S(1)} %maximum_select_fusion.10), channel_id=1, source_target_pairs={{0,4},{1,5},{2,6},{3,7},{4,0},{5,1},{6,2},{7,3},{8,12},{9,13},{10,... | collective-permute-start | bytes 98312 | tf_op jit(solution)/shard_map/ppermute | solution.py:23
  43.2 5.9 %collective-permute-start.3 = (f32[2,64,64]{1,2,0:T(8,128)S(1)}, f32[2,64,64]{1,2,0:T(8,128)S(1)}, u32[]{:S(2)}, u32[]{:S(2)}) collective-permute-start(f32[2,64,64]{1,2,0:T(8,128)S(1)} %maximum_select_fusion.12), channel_id=1, source_target_pairs={{0,8},{1,9},{2,10},{3,11},{4,12},{5,13},{6,14},{7,15},{8,0},{9,1},... | collective-permute-start | bytes 98312 | tf_op jit(solution)/shard_map/ppermute | solution.py:23
  49.9 5.9 %collective-permute-start.4 = (f32[2,64,64]{1,2,0:T(8,128)S(1)}, f32[2,64,64]{1,2,0:T(8,128)S(1)}, u32[]{:S(2)}, u32[]{:S(2)}) collective-permute-start(f32[2,64,64]{1,2,0:T(8,128)S(1)} %maximum_select_fusion.14), channel_id=1, source_target_pairs={{0,16},{1,17},{2,18},{3,19},{4,20},{5,21},{6,22},{7,23},{8,24},{9,... | collective-permute-start | bytes 98312 | tf_op jit(solution)/shard_map/ppermute | solution.py:23
  56.5 6.8 %collective-permute-start.5 = (f32[2,64,64]{1,2,0:T(8,128)S(1)}, f32[2,64,64]{1,2,0:T(8,128)S(1)}, u32[]{:S(2)}, u32[]{:S(2)}) collective-permute-start(f32[2,64,64]{1,2,0:T(8,128)S(1)} %maximum_select_fusion.16), channel_id=1, source_target_pairs={{0,32},{1,33},{2,34},{3,35},{4,36},{5,37},{6,38},{7,39},{8,40},{9,... | collective-permute-start | bytes 98312 | tf_op jit(solution)/shard_map/ppermute | solution.py:23
  63.8 5.8 %collective-permute-start.6 = (f32[2,64,64]{1,2,0:T(8,128)S(1)}, f32[2,64,64]{1,2,0:T(8,128)S(1)}, u32[]{:S(2)}, u32[]{:S(2)}) collective-permute-start(f32[2,64,64]{1,2,0:T(8,128)S(1)} %maximum_select_fusion.18), channel_id=1, source_target_pairs={{0,64},{1,65},{2,66},{3,67},{4,68},{5,69},{6,70},{7,71},{8,72},{9,... | collective-permute-start | bytes 98312 | tf_op jit(solution)/shard_map/ppermute | solution.py:23
  70.0 11.2 %collective-permute-start.7 = (f32[2,64,64]{1,2,0:T(8,128)S(1)}, f32[2,64,64]{1,2,0:T(8,128)S(1)}, u32[]{:S(2)}, u32[]{:S(2)}) collective-permute-start(f32[2,64,64]{1,2,0:T(8,128)S(1)} %maximum_select_fusion.20), channel_id=1, source_target_pairs={{0,128},{1,129},{2,130},{3,131},{4,132},{5,133},{6,134},{7,135},{8... | collective-permute-start | bytes 98312 | tf_op jit(solution)/shard_map/ppermute | solution.py:23
  96.7 1.0 copy-start.3
  99.4 3.6 %copy-start.4 = (f32[8,64,64]{2,1,0:T(8,128)S(1)}, f32[8,64,64]{2,1,0:T(8,128)}, u32[]{:S(2)}) copy-start(f32[8,64,64]{2,1,0:T(8,128)} %fusion.5) | copy-start | bytes 393220
where the time goes:
time: 105 us
  starting transfers between devices  38.4 us (37%)
  matrix products  37.3 us (36%)
  local copies, waits for them, and re-layouts  17.6 us (17%)
  waiting for transfers between devices  9.31 us (9%)
  between operations  1.59 us (2%)
    ppermute x8, starting transfers between devices, swapped(): lax.ppermute(array, axis, [(i, i ^ 1 << distance) for i in range(lax.axis...  29.4 us
    dot_general x6, matrix products, shards(): jnp.einsum('kj,pjr->pkr', chosen, field_down, precision=PRECISE)  14.2 us
    dynamic_slice x18, local copies, waits for them, and re-layouts, level_share(): return lax.dynamic_slice_in_dim(coupled, first_own % 4, own_count, 0)  11 us
    dot_general x30, matrix products, couple_level(): jnp.einsum('ab,nbr->nar', coupling[offset - 1], shifted, precision=PRECISE)  9.52 us
    ppermute x8, waiting for transfers between devices, swapped(): lax.ppermute(array, axis, [(i, i ^ 1 << distance) for i in range(lax.axis...  9.3 us
    ppermute x2, starting transfers between devices, padded(): lax.ppermute(lax.slice_in_dim(block, block.shape[dim] - width, None, axis...  5.28 us
    ppermute x2, starting transfers between devices, padded(): lax.ppermute(lax.slice_in_dim(block, 0, width, axis=dim), axis, backward)  3.75 us
    dot_general x16, matrix products, lift_up(): jnp.einsum('jk,pjr->pkr', transfer[0], paired[:, 0], precision=PRECISE)  3.61 us
  transfers between devices with their start and end apart: 12, of which 7 were waited for; matrix products, arithmetic and copies ran while one was open for 47% of the time, Pallas kernels for 0%

commit v1 on v0

v1 whole, which is shorter than its diff:
```python
import jax
import jax.numpy as jnp
from jax import lax
from jax.experimental import pallas as pl
from jax.experimental.pallas import tpu as pltpu
from jax.sharding import Mesh, PartitionSpec as P

AXES = ("z", "y", "c", "x")
F32 = jnp.float32
BF16 = jnp.bfloat16
NN = (((1,), (0,)), ((), ()))
NT = (((1,), (1,)), ((), ()))
VMEM = pl.BlockSpec(memory_space=pltpu.VMEM)
SMEM = pl.BlockSpec(memory_space=pltpu.SMEM)


def split(a):
    high = a.astype(BF16)
    return high, (a - high.astype(F32)).astype(BF16)


def dot(a, b, dims):
    return lax.dot_general(a, b, dims, preferred_element_type=F32)


def dot3(a, b, dims):
    return dot(a[0], b[0], dims) + (dot(a[0], b[1], dims) + dot(a[1], b[0], dims))


def lift(first, second, transfer):
    return dot3(split(first), transfer[0], NN) + dot3(split(second), transfer[1], NN)


def pair_of(first, second):
    return jnp.concatenate([first, second], axis=1)


def device_index():
    z, y, c, x = (lax.axis_index(a) for a in AXES)
    return ((z * lax.axis_size("y") + y) * lax.axis_size("c") + c) * lax.axis_size("x") + x


def swap(array, mask):
    count = 1
    for a in AXES:
        count *= lax.axis_size(a)
    return lax.ppermute(array, AXES, [(i, i ^ mask) for i in range(count)])


def ring(array, step):
    count = 1
    for a in AXES:
        count *= lax.axis_size(a)
    return lax.ppermute(array, AXES, [(i, (i + step) % count) for i in range(count)])


def leaf_kernel(src, basis, transfer, m0, m1, pair2):
    t = [split(transfer[i]) for i in range(2)]
    leaves = basis.shape[0]
    pts = basis.shape[2]
    low = []
    for i in range(leaves):
        v = dot(src[:, i * pts : (i + 1) * pts], basis[i], NT)
        m0[i] = v
        low.append(v)
    mid = [lift(low[2 * i], low[2 * i + 1], t) for i in range(leaves // 2)]
    for i, v in enumerate(mid):
        m1[i] = v
    pair2[...] = pair_of(lift(mid[0], mid[1], t), lift(mid[2], mid[3], t))


def clusters(pairs, out):
    for i, p in enumerate(pairs):
        out[2 * i] = p[:, :64]
        out[2 * i + 1] = p[:, 64:]


def up4_kernel(copies, here, own, p1, p2, p3, transfer, a, b, pair, ordered):
    t = [split(transfer[i]) for i in range(2)]
    for i, ref in enumerate((own, p1, p2, p3)):
        ordered[here[0] ^ i] = ref[...]
    pairs = [ordered[i] for i in range(4)]
    clusters(pairs, a)
    low = [a[i] for i in range(8)]
    mid = [lift(low[2 * i], low[2 * i + 1], t) for i in range(4)]
    for i, v in enumerate(mid):
        b[i] = v
    top = pair_of(lift(mid[0], mid[1], t), lift(mid[2], mid[3], t))
    if copies:
        for i in range(copies):
            pair[i] = top
    else:
        pair[...] = top


def up2_kernel(here, own, p1, transfer, a, pair, ordered):
    t = [split(transfer[i]) for i in range(2)]
    for i, ref in enumerate((own, p1)):
        ordered[here[0] ^ i] = ref[...]
    clusters([ordered[i] for i in range(2)], a)
    pair[...] = pair_of(lift(a[0], a[1], t), lift(a[2], a[3], t))


def near_kernel(place, own, after, before, up, down, blocks, out, held):
    leaves = held.shape[0] // 5
    pts = held.shape[2]

    @pl.when(pl.program_id(0) == 0)
    def _():
        for n, ref in enumerate((own, after, before, up, down)):
            for i in range(leaves):
                held[n * leaves + i] = ref[:, i * pts : (i + 1) * pts]

    leaf = pl.program_id(0)
    total = None
    for s in range(blocks.shape[1]):
        term = dot(held[place[s, leaf]], blocks[0, s], NT)
        total = term if total is None else total + term
    out[...] = total


def couple(weights, sources, coupling):
    total = None
    for w, m, c in zip(weights, sources, coupling):
        term = dot3(split(m * w), c, NT)
        total = term if total is None else total + term
    return total


def last_kernel(me, far, transfer, coupling, basis, m0, m1, m2, m3, m4, m5, m6, g7, near, out, m7, m8, m9):
    t = [split(transfer[i]) for i in range(2)]
    c = [split(coupling[i]) for i in range(3)]
    d = me[0]
    clusters([g7[i] for i in range(8)], m7)
    for i in range(8):
        m8[i] = lift(m7[2 * i], m7[2 * i + 1], t)
    for i in range(4):
        m9[i] = lift(m8[2 * i], m8[2 * i + 1], t)

    total_rows = far.shape[1]
    lane = lax.broadcasted_iota(jnp.int32, (3, 128), 1)

    def weights_of(row):
        base = row // 128 * 128
        chunk = far[:, pl.ds(pl.multiple_of(base, 128), 128)]
        return jnp.sum(jnp.where(lane == row - base, chunk, 0), axis=1, keepdims=True).astype(F32)

    tail = total_rows // 128 * 128
    tail_lane = lax.broadcasted_iota(jnp.int32, (3, total_rows - tail), 1)

    def tail_weights(row):
        return jnp.sum(jnp.where(tail_lane == row - tail, far[:, tail:], 0), axis=1, keepdims=True).astype(F32)

    starts = [0]
    for level in range(9):
        starts.append(starts[-1] + (2048 >> level))

    def local(level, cluster, values, width):
        row = starts[level] + cluster
        w = tail_weights(row) if starts[level] >= tail else weights_of(row)
        at = cluster % width
        group = at // 4 * 4
        sources = [values[group + (at + j) % 4] for j in (1, 2, 3)]
        return couple([w[j : j + 1, :] for j in range(3)], sources, c)

    field = local(9, d >> 6, m9, 4)
    for level, values, width in ((8, m8, 8), (7, m7, 16), (6, m6, 4), (5, m5, 8), (4, m4, 4), (3, m3, 4)):
        cluster = d >> (level - 3)
        child = cluster % 2
        one = split(transfer[child])
        field = local(level, cluster, values, width) + dot3(split(field), one, NT)
    parents = [field]
    for level, values, width, count in ((2, m2, 8, 2), (1, m1, 4, 4), (0, m0, 8, 8)):
        below = []
        for i in range(count):
            if level == 2:
                own = local(level, d * count + i, values, width)
            else:
                row = starts[level] + d * count + i
                w = weights_of(row)
                group = i // 4 * 4
                own = couple([w[j : j + 1, :] for j in range(3)], [values[group + (i + j + 1) % 4] for j in range(3)], c)
            below.append(own + dot3(split(parents[i // 2]), t[i % 2], NT))
        parents = below
    pts = basis.shape[2]
    for i, f in enumerate(parents):
        high, low = split(f)
        part = dot(high, basis[i], NN) + dot(low, basis[i], NN)
        at = slice(i * pts, (i + 1) * pts)
        out[:, at] = (part + near[:, at]).astype(BF16)


def shards(sources, leaf_basis, transfer, coupling, near_blocks, near_pattern, far_pattern):
    leaves, pts, rank = leaf_basis.shape
    rhs = sources.shape[1]
    d = device_index()
    src = sources.T
    basis = jnp.swapaxes(leaf_basis, 1, 2)
    mat = lambda n: jax.ShapeDtypeStruct((n, rhs, rank), F32)
    pair = jax.ShapeDtypeStruct((rhs, 2 * rank), F32)
    params = pltpu.CompilerParams(vmem_limit_bytes=40 * 1024 * 1024)

    after, before = ring(src, -1), ring(src, 1)
    up, down = ring(src, -4), ring(src, 4)

    m0, m1, pair2 = pl.pallas_call(
        leaf_kernel, out_shape=(mat(8), mat(4), pair), in_specs=[VMEM] * 3, out_specs=(VMEM,) * 3,
        name="leaf", compiler_params=params,
    )(src, basis, transfer)

    def up4(own, masks, here, copies):
        got = [swap(own, m) for m in masks]
        top = jax.ShapeDtypeStruct((copies,) + pair.shape, F32) if copies else pair
        return pl.pallas_call(
            lambda *refs: up4_kernel(copies, *refs),
            out_shape=(mat(8), mat(4), top), in_specs=[SMEM] + [VMEM] * 5, out_specs=(VMEM,) * 3,
            scratch_shapes=[pltpu.VMEM((4,) + pair.shape, F32)], name="up4", compiler_params=params,
        )(here.reshape(1), own, *got, transfer)

    m2, m3, pair4 = up4(pair2, (1, 2, 3), lax.axis_index("x"), 0)
    m4, pair5 = pl.pallas_call(
        up2_kernel, out_shape=(mat(4), pair), in_specs=[SMEM] + [VMEM] * 3, out_specs=(VMEM,) * 2,
        scratch_shapes=[pltpu.VMEM((2,) + pair.shape, F32)], name="up2", compiler_params=params,
    )(lax.axis_index("c").reshape(1), pair4, swap(pair4, 4), transfer)
    m5, m6, pair7 = up4(pair5, (8, 16, 24), lax.axis_index("y"), 8)
    g7 = lax.all_to_all(pair7, "z", 0, 0, tiled=True)

    gap = near_pattern.T // leaves - d
    slot = jnp.where(gap == 0, 0, jnp.where(gap == 1, 1, jnp.where(gap == -1, 2, jnp.where(gap == 4, 3, 4))))
    place = slot * leaves + near_pattern.T % leaves
    whole = lambda a: pl.BlockSpec(a.shape, lambda i, *_: (0,) * len(a.shape))
    near = pl.pallas_call(
        near_kernel,
        out_shape=jax.ShapeDtypeStruct((rhs, leaves * pts), F32),
        grid_spec=pltpu.PrefetchScalarGridSpec(
            num_scalar_prefetch=1,
            grid=(leaves,),
            in_specs=[whole(src)] * 5
            + [pl.BlockSpec((1,) + near_blocks.shape[1:], lambda i, *_: (i, 0, 0, 0))],
            out_specs=pl.BlockSpec((rhs, pts), lambda i, *_: (0, i)),
            scratch_shapes=[pltpu.VMEM((5 * leaves, rhs, pts), BF16)],
        ),
        name="near",
        compiler_params=params,
    )(place, src, after, before, up, down, near_blocks)

    product = pl.pallas_call(
        last_kernel,
        out_shape=jax.ShapeDtypeStruct((rhs, leaves * pts), BF16),
        in_specs=[SMEM] + [VMEM] * 13,
        out_specs=VMEM,
        scratch_shapes=[pltpu.VMEM((n, rhs, rank), F32) for n in (16, 8, 4)],
        name="last",
        compiler_params=params,
    )(d.reshape(1), far_pattern.T, transfer, coupling, basis, m0, m1, m2, m3, m4, m5, m6, g7, near)
    return product.T


def solution(mesh):
    leaf, sub = mesh.shape["leaf"], mesh.shape["sub"]
    cut = Mesh(mesh.devices.reshape(leaf // 8, 4, 2, sub), AXES)
    placed = (
        P(AXES, None),
        P(AXES, None, None),
        P(),
        P(),
        P(AXES, None, None, None),
        P(AXES, None),
        P(),
    )
    return jax.shard_map(shards, mesh=cut, in_specs=placed, out_specs=P(AXES, None), check_vma=False)
```

time: 105 us -> 64.4 us (0.61)
  the two profiles are of different devices: /device:TPU:2 before, /device:TPU:127 now
where the time goes in v1:
time: 64.4 us; the launch traced here: 63.9 us
  starting transfers between devices  28.3 us (44%)
  waiting for transfers between devices  15.8 us (25%)
  Pallas kernels  9.67 us (15%)
  local copies, waits for them, and re-layouts  9.29 us (14%)
  other arithmetic  0.7 us (1%)
    ppermute x4, starting transfers between devices, ring(): lax.ppermute(array, AXES, [(i, (i + step) % count) for i in range(count)])  12.3 us
    ppermute x4, waiting for transfers between devices, ring(): lax.ppermute(array, AXES, [(i, (i + step) % count) for i in range(count)])  10.7 us
    unnamed x24, local copies, waits for them, and re-layouts  9.29 us
    ppermute x7, starting transfers between devices, swap(): return lax.ppermute(array, AXES, [(i, i ^ mask) for i in range(count)])  8.89 us
    all_to_all x1, starting transfers between devices, shards(): g7 = lax.all_to_all(pair7, 'z', 0, 0, tiled=True)  7.11 us
    ppermute x7, waiting for transfers between devices, swap(): return lax.ppermute(array, AXES, [(i, i ^ mask) for i in range(count)])  5.05 us
    pallas_call x1, Pallas kernels, shards(): pl.pallas_call(last_kernel, out_shape=jax.ShapeDtypeStruct((rhs, leaves *...  4.07 us
    pallas_call x1, Pallas kernels, shards(): pl.pallas_call(near_kernel, out_shape=jax.ShapeDtypeStruct((rhs, leaves *...  3.01 us
  transfers between devices with their start and end apart: 12, of which 10 were waited for; matrix products, arithmetic and copies ran while one was open for 1% of the time, Pallas kernels for 5%

profile of v1, /device:TPU:127, one launch (start us, length us, event | category | flops | bytes accessed | tf_op | source)
XLA Modules:
  0.0 63.9 jit_solution(3693412325149748077)
XLA Ops:
  0.0 0.8 %copy-done.1 = f32[2,64,64]{2,1,0:T(8,128)S(1)} copy-done((f32[2,64,64]{2,1,0:T(8,128)S(1)}, f32[2,64,64]{2,1,0:T(8,128)}, u32[]{:S(2)}) %copy-start.1) | copy-done | bytes 32792
  0.8 0.9 %copy-done.6 = bf16[2048,64]{0,1:T(8,128)(2,1)S(1)} copy-done((bf16[2048,64]{0,1:T(8,128)(2,1)S(1)}, bf16[2048,64]{0,1:T(8,128)(2,1)}, u32[]{:S(2)}) %copy-start.6) | copy-done | bytes 262168
  1.8 0.0 copy-start.8
  1.8 0.9 %copy-done.8 = bf16[8,256,64]{1,2,0:T(8,128)(2,1)S(1)} copy-done((bf16[8,256,64]{1,2,0:T(8,128)(2,1)S(1)}, bf16[8,256,64]{1,2,0:T(8,128)(2,1)}, u32[]{:S(2)}) %copy-start.8) | copy-done | bytes 262168
  2.7 0.0 copy-start.5
  2.7 0.0 copy-start.9
  2.7 0.0 copy-start.11
  2.7 0.6 leaf.1
  3.3 0.3 collective-permute-start.2
  3.6 2.1 %collective-permute-start.1 = (f32[64,128]{1,0:T(8,128)S(1)}, f32[64,128]{1,0:T(8,128)S(1)}, u32[]{:S(2)}, u32[]{:S(2)}) collective-permute-start(f32[64,128]{1,0:T(8,128)S(1)} %get-tuple-element.18.refs_1_), channel_id=1, source_target_pairs={{0,2},{1,3},{2,0},{3,1},{4,6},{5,7},{6,4},{7,5},{8,10},{9,11},{10,... | collective-permute-start | bytes 98312 | tf_op jit(solution)/shard_map/ppermute | solution.py:47
  5.8 0.9 %collective-permute-start = (f32[64,128]{1,0:T(8,128)S(1)}, f32[64,128]{1,0:T(8,128)S(1)}, u32[]{:S(2)}, u32[]{:S(2)}) collective-permute-start(f32[64,128]{1,0:T(8,128)S(1)} %get-tuple-element.18.refs_1_), channel_id=1, source_target_pairs={{0,1},{1,0},{2,3},{3,2},{4,5},{5,4},{6,7},{7,6},{8,9},{9,8},{10,11... | collective-permute-start | bytes 98312 | tf_op jit(solution)/shard_map/ppermute | solution.py:47
  6.7 0.7 %collective-permute-done.2.refs_4_ = f32[64,128]{1,0:T(8,128)S(1)} collective-permute-done((f32[64,128]{1,0:T(8,128)S(1)}, f32[64,128]{1,0:T(8,128)S(1)}, u32[]{:S(2)}, u32[]{:S(2)}) %collective-permute-start.2) | collective-permute-done | bytes 32800 | tf_op jit(solution)/shard_map/ppermute | solution.py:47
  7.4 0.5 collective-permute-done.1.refs_3_
  7.9 0.9 %collective-permute-done.refs_2_ = f32[64,128]{1,0:T(8,128)S(1)} collective-permute-done((f32[64,128]{1,0:T(8,128)S(1)}, f32[64,128]{1,0:T(8,128)S(1)}, u32[]{:S(2)}, u32[]{:S(2)}) %collective-permute-start) | collective-permute-done | bytes 32800 | tf_op jit(solution)/shard_map/ppermute | solution.py:47
  8.8 0.8 %copy-done.2 = f32[2,64,64]{2,1,0:T(8,128)S(1)} copy-done((f32[2,64,64]{2,1,0:T(8,128)S(1)}, f32[2,64,64]{2,1,0:T(8,128)}, u32[]{:S(2)}) %copy-start.2) | copy-done | bytes 32792
  9.7 0.5 up4.2
  10.2 2.2 %collective-permute-start.3 = (f32[64,128]{1,0:T(8,128)S(1)}, f32[64,128]{1,0:T(8,128)S(1)}, u32[]{:S(2)}, u32[]{:S(2)}) collective-permute-start(f32[64,128]{1,0:T(8,128)S(1)} %get-tuple-element.21.own), channel_id=1, source_target_pairs={{0,4},{1,5},{2,6},{3,7},{4,0},{5,1},{6,2},{7,3},{8,12},{9,13},{10,... | collective-permute-start | bytes 98312 | tf_op jit(solution)/shard_map/ppermute | solution.py:47
  12.4 0.9 %collective-permute-done.3.p1 = f32[64,128]{1,0:T(8,128)S(1)} collective-permute-done((f32[64,128]{1,0:T(8,128)S(1)}, f32[64,128]{1,0:T(8,128)S(1)}, u32[]{:S(2)}, u32[]{:S(2)}) %collective-permute-start.3) | collective-permute-done | bytes 32800 | tf_op jit(solution)/shard_map/ppermute | solution.py:47
  13.2 0.8 %copy-done.3 = f32[2,64,64]{2,1,0:T(8,128)S(1)} copy-done((f32[2,64,64]{2,1,0:T(8,128)S(1)}, f32[2,64,64]{2,1,0:T(8,128)}, u32[]{:S(2)}) %copy-start.3) | copy-done | bytes 32792
  14.1 0.3 up2.1
  14.4 0.1 collective-permute-start.6
  14.5 2.2 %collective-permute-start.5 = (f32[64,128]{1,0:T(8,128)S(1)}, f32[64,128]{1,0:T(8,128)S(1)}, u32[]{:S(2)}, u32[]{:S(2)}) collective-permute-start(f32[64,128]{1,0:T(8,128)S(1)} %get-tuple-element.23.refs_1_), channel_id=1, source_target_pairs={{0,16},{1,17},{2,18},{3,19},{4,20},{5,21},{6,22},{7,23},{8,24},{9,... | collective-permute-start | bytes 98312 | tf_op jit(solution)/shard_map/ppermute | solution.py:47
  16.7 1.0 %collective-permute-start.4 = (f32[64,128]{1,0:T(8,128)S(1)}, f32[64,128]{1,0:T(8,128)S(1)}, u32[]{:S(2)}, u32[]{:S(2)}) collective-permute-start(f32[64,128]{1,0:T(8,128)S(1)} %get-tuple-element.23.refs_1_), channel_id=1, source_target_pairs={{0,8},{1,9},{2,10},{3,11},{4,12},{5,13},{6,14},{7,15},{8,0},{9,1},... | collective-permute-start | bytes 98312 | tf_op jit(solution)/shard_map/ppermute | solution.py:47
  17.7 0.7 %collective-permute-done.6.refs_4_ = f32[64,128]{1,0:T(8,128)S(1)} collective-permute-done((f32[64,128]{1,0:T(8,128)S(1)}, f32[64,128]{1,0:T(8,128)S(1)}, u32[]{:S(2)}, u32[]{:S(2)}) %collective-permute-start.6) | collective-permute-done | bytes 32800 | tf_op jit(solution)/shard_map/ppermute | solution.py:47
  18.5 0.4 collective-permute-done.5.refs_3_
  18.8 0.9 %collective-permute-done.4.refs_2_ = f32[64,128]{1,0:T(8,128)S(1)} collective-permute-done((f32[64,128]{1,0:T(8,128)S(1)}, f32[64,128]{1,0:T(8,128)S(1)}, u32[]{:S(2)}, u32[]{:S(2)}) %collective-permute-start.4) | collective-permute-done | bytes 32800 | tf_op jit(solution)/shard_map/ppermute | solution.py:47
  19.8 0.8 %copy-done.4 = f32[2,64,64]{2,1,0:T(8,128)S(1)} copy-done((f32[2,64,64]{2,1,0:T(8,128)S(1)}, f32[2,64,64]{2,1,0:T(8,128)}, u32[]{:S(2)}) %copy-start.4) | copy-done | bytes 32792
  20.6 1.2 %up4.3 = (f32[8,64,64]{2,1,0:T(8,128)S(1)}, f32[4,64,64]{2,1,0:T(8,128)S(1)}, f32[8,64,128]{2,1,0:T(8,128)}) custom-call(s32[1]{0:T(128)} %bitcast.6.refs_0_, f32[64,128]{1,0:T(8,128)S(1)} %get-tuple-element.23.refs_1_, f32[64,128]{1,0:T(8,128)S(1)} %collective-permute-done.4.refs_2_, f32[64,128]{1,0:T(8,128)S(1)} %collective-permute-done.5.refs_3_, ...), custom_call_target="tpu_custom_call" | custom-call | tf_op jit(solution)/shard_map/up4/pallas_call | solution.py:214
  21.9 7.1 %all-to-all-start = ((f32[8,64,128]{2,1,0:T(8,128)}), f32[8,64,128]{2,1,0:T(8,128)S(1)}, u32[]{:S(2)}, u32[]{:S(2)}) async-start(f32[8,64,128]{2,1,0:T(8,128)} %get-tuple-element.26), calls=%async_computation | async-start | bytes 524288 | tf_op jit(solution)/shard_map/all_to_all | solution.py:226
  29.0 6.0 %collective-permute-start.10 = (bf16[64,2048]{1,0:T(8,128)(2,1)}, bf16[64,2048]{1,0:T(8,128)(2,1)S(1)}, u32[]{:S(2)}, u32[]{:S(2)}) collective-permute-start(bf16[64,2048]{1,0:T(8,128)(2,1)} %bitcast.26), channel_id=1, source_target_pairs={{0,4},{1,5},{2,6},{3,7},{4,8},{5,9},{6,10},{7,11},{8,12},{9,13},{1... | collective-permute-start | bytes 786440 | tf_op jit(solution)/shard_map/ppermute | solution.py:54
  35.0 0.0 collective-permute-start.9
  35.0 6.3 %collective-permute-start.8 = (bf16[64,2048]{1,0:T(8,128)(2,1)}, bf16[64,2048]{1,0:T(8,128)(2,1)S(1)}, u32[]{:S(2)}, u32[]{:S(2)}) collective-permute-start(bf16[64,2048]{1,0:T(8,128)(2,1)} %bitcast.28), channel_id=1, source_target_pairs={{0,1},{1,2},{2,3},{3,4},{4,5},{5,6},{6,7},{7,8},{8,9},{9,10},{10,1... | collective-permute-start | bytes 786440 | tf_op jit(solution)/shard_map/ppermute | solution.py:54
  41.3 0.0 collective-permute-start.7
  41.3 0.7 %fusion.1.place = s32[4,8]{1,0:T(4,128)S(1)} fusion(s32[8,4]{0,1:T(4,128)} %param.12, s32[]{:T(128)} %add.21), kind=kLoop, calls=%fused_computation.6 | loop fusion | flops 960 | bytes 260 | tf_op jit(solution)/shard_map/add | solution.py:230
  42.0 0.0 collective-permute-done.10.down
  42.0 2.3 %collective-permute-done.9.up = bf16[64,2048]{1,0:T(8,128)(2,1)S(1)} collective-permute-done((bf16[64,2048]{1,0:T(8,128)(2,1)}, bf16[64,2048]{1,0:T(8,128)(2,1)S(1)}, u32[]{:S(2)}, u32[]{:S(2)}) %collective-permute-start.9) | collective-permute-done | bytes 262176 | tf_op jit(solution)/shard_map/ppermute | solution.py:54
  44.3 0.6 %collective-permute-done.8.before = bf16[64,2048]{1,0:T(8,128)(2,1)S(1)} collective-permute-done((bf16[64,2048]{1,0:T(8,128)(2,1)}, bf16[64,2048]{1,0:T(8,128)(2,1)S(1)}, u32[]{:S(2)}, u32[]{:S(2)}) %collective-permute-start.8) | collective-permute-done | bytes 262176 | tf_op jit(solution)/shard_map/ppermute | solution.py:54
  44.9 7.8 %collective-permute-done.7.after = bf16[64,2048]{1,0:T(8,128)(2,1)S(1)} collective-permute-done((bf16[64,2048]{1,0:T(8,128)(2,1)}, bf16[64,2048]{1,0:T(8,128)(2,1)S(1)}, u32[]{:S(2)}, u32[]{:S(2)}) %collective-permute-start.7) | collective-permute-done | bytes 262176 | tf_op jit(solution)/shard_map/ppermute | solution.py:54
  52.7 2.2 %copy-done = bf16[8,4,256,256]{3,2,1,0:T(8,128)(2,1)S(1)} copy-done((bf16[8,4,256,256]{3,2,1,0:T(8,128)(2,1)S(1)}, bf16[8,4,256,256]{3,2,1,0:T(8,128)(2,1)}, u32[]{:S(2)}) %copy-start) | copy-done | bytes 4194328
  54.9 0.9 %copy-done.7 = bf16[2048,64]{0,1:T(8,128)(2,1)S(1)} copy-done((bf16[2048,64]{0,1:T(8,128)(2,1)S(1)}, bf16[2048,64]{0,1:T(8,128)(2,1)}, u32[]{:S(2)}) %copy-start.7) | copy-done | bytes 262168
  55.9 3.0 %near.1 = f32[64,2048]{1,0:T(8,128)S(1)} custom-call(s32[4,8]{1,0:T(4,128)S(1)} %fusion.1.place, bf16[64,2048]{1,0:T(8,128)(2,1)S(1)} %bitcast.31, bf16[64,2048]{1,0:T(8,128)(2,1)S(1)} %collective-permute-done.7.after, bf16[64,2048]{1,0:T(8,128)(2,1)S(1)} %collective-permute-done.8.before, bf16[64,2048]{1,0:T(8,128)(2,1)S(1)} %collective-permute-done.9.up, ...), custom_call_target="tpu_custom_call" | custom-call | tf_op jit(solution)/shard_map/near/pallas_call | solution.py:232
  58.9 0.0 all-to-all-done.g7
  58.9 0.0 copy-done.5
  58.9 0.0 copy-done.9
  58.9 0.0 copy-done.11
  58.9 0.0 copy-start.10
  58.9 0.9 %copy-done.10 = f32[3,64,64]{2,1,0:T(8,128)S(1)} copy-done((f32[3,64,64]{2,1,0:T(8,128)S(1)}, f32[3,64,64]{2,1,0:T(8,128)}, u32[]{:S(2)}) %copy-start.10) | copy-done | bytes 49176
  59.8 4.1 %last.1 = bf16[64,2048]{1,0:T(8,128)(2,1)} custom-call(s32[1]{0:T(128)} %bitcast.me, s32[3,4092]{1,0:T(4,128)S(1)} %bitcast.34, f32[2,64,64]{2,1,0:T(8,128)S(1)} %copy-done.5, f32[3,64,64]{2,1,0:T(8,128)S(1)} %copy-done.10, bf16[8,64,256]{2,1,0:T(8,128)(2,1)S(1)} %bitcast.33, f32[8,64,64]{2,1,0:T(8,128)S(1)} %get-tuple-element.16.m0, ...), custom_call_target="tpu_custom_call" | custom-call | tf_op jit(solution)/shard_map/last/pallas_call | solution.py:247
  (7 shorter events, 0.0 us)
Async XLA Ops:
  0.0 0.8 %copy-start.1 = (f32[2,64,64]{2,1,0:T(8,128)S(1)}, f32[2,64,64]{2,1,0:T(8,128)}, u32[]{:S(2)}) copy-start(f32[2,64,64]{2,1,0:T(8,128)} %transfer.5) | copy-start | bytes 98308
  0.8 0.9 %copy-start.6 = (bf16[2048,64]{0,1:T(8,128)(2,1)S(1)}, bf16[2048,64]{0,1:T(8,128)(2,1)}, u32[]{:S(2)}) copy-start(bf16[2048,64]{0,1:T(8,128)(2,1)} %param.7) | copy-start | bytes 786436
  1.8 0.9 %copy-start.8 = (bf16[8,256,64]{1,2,0:T(8,128)(2,1)S(1)}, bf16[8,256,64]{1,2,0:T(8,128)(2,1)}, u32[]{:S(2)}) copy-start(bf16[8,256,64]{1,2,0:T(8,128)(2,1)} %param.8) | copy-start | bytes 786436
  2.7 56.2 %copy-start.5 = (f32[2,64,64]{2,1,0:T(8,128)S(1)}, f32[2,64,64]{2,1,0:T(8,128)}, u32[]{:S(2)}) copy-start(f32[2,64,64]{2,1,0:T(8,128)} %transfer.5) | copy-start | bytes 98308
  2.7 56.2 %copy-start.9 = (bf16[8,256,64]{1,2,0:T(8,128)(2,1)S(1)}, bf16[8,256,64]{1,2,0:T(8,128)(2,1)}, u32[]{:S(2)}) copy-start(bf16[8,256,64]{1,2,0:T(8,128)(2,1)} %param.8) | copy-start | bytes 786436
  2.7 56.2 %copy-start.11 = (s32[4092,3]{0,1:T(4,128)S(1)}, s32[4092,3]{0,1:T(4,128)}, u32[]{:S(2)}) copy-start(s32[4092,3]{0,1:T(4,128)} %param.13) | copy-start | bytes 147316
  3.3 4.1 %collective-permute-start.2 = (f32[64,128]{1,0:T(8,128)S(1)}, f32[64,128]{1,0:T(8,128)S(1)}, u32[]{:S(2)}, u32[]{:S(2)}) collective-permute-start(f32[64,128]{1,0:T(8,128)S(1)} %get-tuple-element.18.refs_1_), channel_id=1, source_target_pairs={{0,3},{1,2},{2,1},{3,0},{4,7},{5,6},{6,5},{7,4},{8,11},{9,10},{10,... | collective-permute-start | bytes 98312 | tf_op jit(solution)/shard_map/ppermute | solution.py:47
  3.6 4.3 %collective-permute-start.1 = (f32[64,128]{1,0:T(8,128)S(1)}, f32[64,128]{1,0:T(8,128)S(1)}, u32[]{:S(2)}, u32[]{:S(2)}) collective-permute-start(f32[64,128]{1,0:T(8,128)S(1)} %get-tuple-element.18.refs_1_), channel_id=1, source_target_pairs={{0,2},{1,3},{2,0},{3,1},{4,6},{5,7},{6,4},{7,5},{8,10},{9,11},{10,... | collective-permute-start | bytes 98312 | tf_op jit(solution)/shard_map/ppermute | solution.py:47
  5.8 3.1 %collective-permute-start = (f32[64,128]{1,0:T(8,128)S(1)}, f32[64,128]{1,0:T(8,128)S(1)}, u32[]{:S(2)}, u32[]{:S(2)}) collective-permute-start(f32[64,128]{1,0:T(8,128)S(1)} %get-tuple-element.18.refs_1_), channel_id=1, source_target_pairs={{0,1},{1,0},{2,3},{3,2},{4,5},{5,4},{6,7},{7,6},{8,9},{9,8},{10,11... | collective-permute-start | bytes 98312 | tf_op jit(solution)/shard_map/ppermute | solution.py:47
  8.8 0.8 %copy-start.2 = (f32[2,64,64]{2,1,0:T(8,128)S(1)}, f32[2,64,64]{2,1,0:T(8,128)}, u32[]{:S(2)}) copy-start(f32[2,64,64]{2,1,0:T(8,128)} %transfer.5) | copy-start | bytes 98308
  10.2 3.0 %collective-permute-start.3 = (f32[64,128]{1,0:T(8,128)S(1)}, f32[64,128]{1,0:T(8,128)S(1)}, u32[]{:S(2)}, u32[]{:S(2)}) collective-permute-start(f32[64,128]{1,0:T(8,128)S(1)} %get-tuple-element.21.own), channel_id=1, source_target_pairs={{0,4},{1,5},{2,6},{3,7},{4,0},{5,1},{6,2},{7,3},{8,12},{9,13},{10,... | collective-permute-start | bytes 98312 | tf_op jit(solution)/shard_map/ppermute | solution.py:47
  13.2 0.8 %copy-start.3 = (f32[2,64,64]{2,1,0:T(8,128)S(1)}, f32[2,64,64]{2,1,0:T(8,128)}, u32[]{:S(2)}) copy-start(f32[2,64,64]{2,1,0:T(8,128)} %transfer.5) | copy-start | bytes 98308
  14.4 4.1 %collective-permute-start.6 = (f32[64,128]{1,0:T(8,128)S(1)}, f32[64,128]{1,0:T(8,128)S(1)}, u32[]{:S(2)}, u32[]{:S(2)}) collective-permute-start(f32[64,128]{1,0:T(8,128)S(1)} %get-tuple-element.23.refs_1_), channel_id=1, source_target_pairs={{0,24},{1,25},{2,26},{3,27},{4,28},{5,29},{6,30},{7,31},{8,16},{9,... | collective-permute-start | bytes 98312 | tf_op jit(solution)/shard_map/ppermute | solution.py:47
  14.5 4.4 %collective-permute-start.5 = (f32[64,128]{1,0:T(8,128)S(1)}, f32[64,128]{1,0:T(8,128)S(1)}, u32[]{:S(2)}, u32[]{:S(2)}) collective-permute-start(f32[64,128]{1,0:T(8,128)S(1)} %get-tuple-element.23.refs_1_), channel_id=1, source_target_pairs={{0,16},{1,17},{2,18},{3,19},{4,20},{5,21},{6,22},{7,23},{8,24},{9,... | collective-permute-start | bytes 98312 | tf_op jit(solution)/shard_map/ppermute | solution.py:47
  16.7 3.1 %collective-permute-start.4 = (f32[64,128]{1,0:T(8,128)S(1)}, f32[64,128]{1,0:T(8,128)S(1)}, u32[]{:S(2)}, u32[]{:S(2)}) collective-permute-start(f32[64,128]{1,0:T(8,128)S(1)} %get-tuple-element.23.refs_1_), channel_id=1, source_target_pairs={{0,8},{1,9},{2,10},{3,11},{4,12},{5,13},{6,14},{7,15},{8,0},{9,1},... | collective-permute-start | bytes 98312 | tf_op jit(solution)/shard_map/ppermute | solution.py:47
  19.8 0.8 %copy-start.4 = (f32[2,64,64]{2,1,0:T(8,128)S(1)}, f32[2,64,64]{2,1,0:T(8,128)}, u32[]{:S(2)}) copy-start(f32[2,64,64]{2,1,0:T(8,128)} %transfer.5) | copy-start | bytes 98308
  21.9 37.0 %all-to-all-start = ((f32[8,64,128]{2,1,0:T(8,128)}), f32[8,64,128]{2,1,0:T(8,128)S(1)}, u32[]{:S(2)}, u32[]{:S(2)}) async-start(f32[8,64,128]{2,1,0:T(8,128)} %get-tuple-element.26), calls=%async_computation | async-start | bytes 524288 | tf_op jit(solution)/shard_map/all_to_all | solution.py:226
  29.0 13.0 %collective-permute-start.10 = (bf16[64,2048]{1,0:T(8,128)(2,1)}, bf16[64,2048]{1,0:T(8,128)(2,1)S(1)}, u32[]{:S(2)}, u32[]{:S(2)}) collective-permute-start(bf16[64,2048]{1,0:T(8,128)(2,1)} %bitcast.26), channel_id=1, source_target_pairs={{0,4},{1,5},{2,6},{3,7},{4,8},{5,9},{6,10},{7,11},{8,12},{9,13},{1... | collective-permute-start | bytes 786440 | tf_op jit(solution)/shard_map/ppermute | solution.py:54
  35.0 9.3 %collective-permute-start.9 = (bf16[64,2048]{1,0:T(8,128)(2,1)}, bf16[64,2048]{1,0:T(8,128)(2,1)S(1)}, u32[]{:S(2)}, u32[]{:S(2)}) collective-permute-start(bf16[64,2048]{1,0:T(8,128)(2,1)} %bitcast.27), channel_id=1, source_target_pairs={{0,252},{1,253},{2,254},{3,255},{4,0},{5,1},{6,2},{7,3},{8,4},{9,5... | collective-permute-start | bytes 786440 | tf_op jit(solution)/shard_map/ppermute | solution.py:54
  35.0 10.0 %collective-permute-start.8 = (bf16[64,2048]{1,0:T(8,128)(2,1)}, bf16[64,2048]{1,0:T(8,128)(2,1)S(1)}, u32[]{:S(2)}, u32[]{:S(2)}) collective-permute-start(bf16[64,2048]{1,0:T(8,128)(2,1)} %bitcast.28), channel_id=1, source_target_pairs={{0,1},{1,2},{2,3},{3,4},{4,5},{5,6},{6,7},{7,8},{8,9},{9,10},{10,1... | collective-permute-start | bytes 786440 | tf_op jit(solution)/shard_map/ppermute | solution.py:54
  41.3 11.4 %collective-permute-start.7 = (bf16[64,2048]{1,0:T(8,128)(2,1)}, bf16[64,2048]{1,0:T(8,128)(2,1)S(1)}, u32[]{:S(2)}, u32[]{:S(2)}) collective-permute-start(bf16[64,2048]{1,0:T(8,128)(2,1)} %bitcast.29), channel_id=1, source_target_pairs={{0,255},{1,0},{2,1},{3,2},{4,3},{5,4},{6,5},{7,6},{8,7},{9,8},{10,... | collective-permute-start | bytes 786440 | tf_op jit(solution)/shard_map/ppermute | solution.py:54
  52.7 2.2 %copy-start = (bf16[8,4,256,256]{3,2,1,0:T(8,128)(2,1)S(1)}, bf16[8,4,256,256]{3,2,1,0:T(8,128)(2,1)}, u32[]{:S(2)}) copy-start(bf16[8,4,256,256]{3,2,1,0:T(8,128)(2,1)} %blocks.1) | copy-start | bytes 12582916
  54.9 0.9 %copy-start.7 = (bf16[2048,64]{0,1:T(8,128)(2,1)S(1)}, bf16[2048,64]{0,1:T(8,128)(2,1)}, u32[]{:S(2)}) copy-start(bf16[2048,64]{0,1:T(8,128)(2,1)} %param.7) | copy-start | bytes 786436
  58.9 0.9 %copy-start.10 = (f32[3,64,64]{2,1,0:T(8,128)S(1)}, f32[3,64,64]{2,1,0:T(8,128)}, u32[]{:S(2)}) copy-start(f32[3,64,64]{2,1,0:T(8,128)} %coupling.1) | copy-start | bytes 147460

commit v2 on v1

v2 whole, which is shorter than its diff:
```python
import jax
import jax.numpy as jnp
from jax import lax
from jax.experimental import pallas as pl
from jax.experimental.pallas import tpu as pltpu
from jax.sharding import Mesh, PartitionSpec as P

AXES = ("z", "y", "c", "x")
F32 = jnp.float32
BF16 = jnp.bfloat16
NN = (((1,), (0,)), ((), ()))
NT = (((1,), (1,)), ((), ()))
VMEM = pl.BlockSpec(memory_space=pltpu.VMEM)
SMEM = pl.BlockSpec(memory_space=pltpu.SMEM)
HBM = pl.BlockSpec(memory_space=pltpu.HBM)
PARAMS = pltpu.CompilerParams(vmem_limit_bytes=40 * 1024 * 1024)


def in_hbm(array):
    return pltpu.with_memory_space_constraint(array, pltpu.HBM)


def split(a):
    high = a.astype(BF16)
    return high, (a - high.astype(F32)).astype(BF16)


def dot(a, b, dims):
    return lax.dot_general(a, b, dims, preferred_element_type=F32)


def dot3(a, b, dims):
    return dot(a[0], b[0], dims) + (dot(a[0], b[1], dims) + dot(a[1], b[0], dims))


def lift(first, second, transfer):
    return dot3(split(first), transfer[0], NN) + dot3(split(second), transfer[1], NN)


def pair_of(first, second):
    return jnp.concatenate([first, second], axis=1)


def device_index():
    z, y, c, x = (lax.axis_index(a) for a in AXES)
    return ((z * lax.axis_size("y") + y) * lax.axis_size("c") + c) * lax.axis_size("x") + x


def device_count():
    count = 1
    for a in AXES:
        count *= lax.axis_size(a)
    return count


def swap(array, mask):
    return lax.ppermute(array, AXES, [(i, i ^ mask) for i in range(device_count())])


def across(device, step, count):
    return (device + jnp.where(device & step, step, count - step)) % count


def swap_across(array, step):
    n = device_count()
    pairs = [(i, (i + (step if i & step else n - step)) % n) for i in range(n)]
    return lax.ppermute(array, AXES, pairs)


def leaf_kernel(src_in, basis_in, transfer_in, coupling_in, far_in, src, basis, coupling, far, tsplit, m0, m1, pair2, raw, sems):
    copies = [
        pltpu.make_async_copy(a, b, sems.at[i])
        for i, (a, b) in enumerate(
            ((src_in, src), (basis_in, basis), (transfer_in, raw), (coupling_in, coupling), (far_in, far))
        )
    ]
    for copy in copies:
        copy.start()
    for copy in copies[:3]:
        copy.wait()
    t = [split(raw[i]) for i in range(2)]
    for i in range(2):
        tsplit[2 * i], tsplit[2 * i + 1] = t[i]
    leaves, _, pts = basis.shape
    low = []
    for i in range(leaves):
        v = dot(src[:, i * pts : (i + 1) * pts], basis[i], NT)
        m0[i] = v
        low.append(v)
    mid = [lift(low[2 * i], low[2 * i + 1], t) for i in range(leaves // 2)]
    for i, v in enumerate(mid):
        m1[i] = v
    pair2[...] = pair_of(lift(mid[0], mid[1], t), lift(mid[2], mid[3], t))
    for copy in copies[3:]:
        copy.wait()


def transfers(tsplit):
    return [(tsplit[0], tsplit[1]), (tsplit[2], tsplit[3])]


def clusters(pairs, out):
    for i, p in enumerate(pairs):
        out[2 * i] = p[:, :64]
        out[2 * i + 1] = p[:, 64:]


def up4_kernel(copies, axis, refs):
    own, p1, p2, p3, tsplit = refs[:5]
    a, b, pair, ordered = refs[-4:]
    t = transfers(tsplit)
    here = lax.axis_index(axis)
    for i, ref in enumerate((own, p1, p2, p3)):
        ordered[here ^ i] = ref[...]
    clusters([ordered[i] for i in range(4)], a)
    low = [a[i] for i in range(8)]
    mid = [lift(low[2 * i], low[2 * i + 1], t) for i in range(4)]
    for i, v in enumerate(mid):
        b[i] = v
    top = pair_of(lift(mid[0], mid[1], t), lift(mid[2], mid[3], t))
    if copies:
        for i in range(copies):
            pair[i] = top
    else:
        pair[...] = top


def up2_kernel(axis, refs):
    own, p1, tsplit = refs[:3]
    a, pair, ordered = refs[-3:]
    t = transfers(tsplit)
    here = lax.axis_index(axis)
    for i, ref in enumerate((own, p1)):
        ordered[here ^ i] = ref[...]
    clusters([ordered[i] for i in range(2)], a)
    pair[...] = pair_of(lift(a[0], a[1], t), lift(a[2], a[3], t))


def near_kernel(pattern_in, own, core, side, cross4, cross1, blocks_in, out, held, blocks, pattern, sems, sem):
    leaves, slots, pts = blocks_in.shape[:3]
    pattern_copy = pltpu.make_async_copy(pattern_in, pattern, sem)
    pattern_copy.start()
    copies = [pltpu.make_async_copy(blocks_in.at[i], blocks.at[i], sems.at[i]) for i in range(leaves)]
    for copy in copies:
        copy.start()
    for n, ref in enumerate((own, core, side, cross4, cross1)):
        for i in range(leaves):
            held[n * leaves + i] = ref[:, i * pts : (i + 1) * pts]
    pattern_copy.wait()
    me = device_index()
    n = device_count()
    others = [me, me ^ 4, me ^ 1, across(me, 4, n)]
    for i in range(leaves):
        copies[i].wait()
        total = None
        for s in range(slots):
            j = pattern[s, i]
            device = j // leaves
            slot = jnp.int32(4)
            for k, other in enumerate(others):
                slot = jnp.where(device == other, k, slot)
            term = dot(held[slot * leaves + j % leaves], blocks[i, s], NT)
            total = term if total is None else total + term
        out[:, i * pts : (i + 1) * pts] = total


def start_of(level):
    return sum(2048 >> l for l in range(level))


def weights_of(far, level, cluster):
    row = start_of(level) + cluster
    total = far.shape[1]
    tail = total // 128 * 128
    if start_of(level) >= tail:
        chunk, base = far[:, tail:], tail
    else:
        base = row // 128 * 128
        chunk = far[:, pl.ds(pl.multiple_of(base, 128), 128)]
    lane = lax.broadcasted_iota(jnp.int32, chunk.shape, 1)
    w = jnp.sum(jnp.where(lane == row - base, chunk, 0), axis=1, keepdims=True).astype(F32)
    return [w[j : j + 1, :] for j in range(3)]


def couple(weights, sources, coupling):
    total = None
    for w, m, c in zip(weights, sources, coupling):
        term = dot3(split(m * w), c, NT)
        total = term if total is None else total + term
    return total


def local(far, c, level, cluster, values, width):
    at = cluster % width
    group = at // 4 * 4
    return couple(weights_of(far, level, cluster), [values[group + (at + j) % 4] for j in (1, 2, 3)], c)


def low_kernel(far, coupling, m0, m1, loc0, loc1):
    c = [split(coupling[i]) for i in range(3)]
    d = device_index()
    for level, values, out in ((0, m0, loc0), (1, m1, loc1)):
        count = values.shape[0]
        for i in range(count):
            w = weights_of(far, level, d * count + i)
            out[i] = couple(w, [values[i // 4 * 4 + (i + j) % 4] for j in (1, 2, 3)], c)


def low2_kernel(far, coupling, m2, behind, loc2):
    c = [split(coupling[i]) for i in range(3)]
    d = device_index()
    for i in range(2):
        loc2[i] = local(far, c, 2, d * 2 + i, m2, 8)


def mid_kernel(far, coupling, tsplit, basis, loc0, loc1, loc2, m3, m4, m5, m6, near, part, ghigh, glow):
    c = [split(coupling[i]) for i in range(3)]
    t = transfers(tsplit)
    d = device_index()
    rows = lax.broadcasted_iota(jnp.int32, (64, 64), 0)
    cols = lax.broadcasted_iota(jnp.int32, (64, 64), 1)
    chain = jnp.where(rows == cols, 1.0, 0.0).astype(F32)
    field = None
    for level, values, width in ((6, m6, 4), (5, m5, 8), (4, m4, 4), (3, m3, 4)):
        cluster = d >> (level - 3)
        child = cluster % 2
        one = (tsplit[2 * child], tsplit[2 * child + 1])
        own = local(far, c, level, cluster, values, width)
        if field is None:
            chain = dot3(split(chain), one, NT)
            field = own
        else:
            both = dot3(split(jnp.concatenate([field, chain], 0)), one, NT)
            field, chain = own + both[:64], both[64:]
    parents = [(field, chain)]
    for level, count in ((2, 2), (1, 4), (0, 8)):
        below = []
        for i in range(count):
            own = (loc0, loc1, loc2)[level][i]
            both = dot3(split(jnp.concatenate(parents[i // 2], 0)), t[i % 2], NT)
            below.append((own + both[:64], both[64:]))
        parents = below
    pts = basis.shape[2]
    for i, both in enumerate(parents):
        high, low = split(jnp.concatenate(both, 0))
        whole = dot(high, basis[i], NN) + dot(low, basis[i], NN)
        at = slice(i * pts, (i + 1) * pts)
        part[:, at] = whole[:64] + near[:, at]
        ghigh[:, at], glow[:, at] = split(whole[64:])


def last_kernel(far, coupling, tsplit, g7, part, ghigh, glow, out, m7, m8, m9):
    c = [split(coupling[i]) for i in range(3)]
    t = transfers(tsplit)
    d = device_index()
    clusters([g7[i] for i in range(8)], m7)
    for i in range(8):
        m8[i] = lift(m7[2 * i], m7[2 * i + 1], t)
    for i in range(4):
        m9[i] = lift(m8[2 * i], m8[2 * i + 1], t)
    field = local(far, c, 9, d >> 6, m9, 4)
    for level, values, width in ((8, m8, 8), (7, m7, 16)):
        cluster = d >> (level - 3)
        child = cluster % 2
        one = (tsplit[2 * child], tsplit[2 * child + 1])
        field = local(far, c, level, cluster, values, width) + dot3(split(field), one, NT)
    high, low = split(field)
    step = 256
    for at in range(0, out.shape[1], step):
        at = slice(at, at + step)
        far_part = dot(high, ghigh[:, at], NN) + (dot(high, glow[:, at], NN) + dot(low, ghigh[:, at], NN))
        out[:, at] = (far_part + part[:, at]).astype(BF16)


def shards(sources, leaf_basis, transfer, coupling, near_blocks, near_pattern, far_pattern):
    leaves, pts, rank = leaf_basis.shape
    rhs = sources.shape[1]
    points = leaves * pts
    src_in = sources.T
    basis_in = jnp.swapaxes(leaf_basis, 1, 2)
    far_in = far_pattern.T
    of = jax.ShapeDtypeStruct
    mat = lambda n: of((n, rhs, rank), F32)
    pair = of((rhs, 2 * rank), F32)

    src, basis, coup, far, tsplit, m0, m1, pair2 = pl.pallas_call(
        leaf_kernel,
        out_shape=(
            of(src_in.shape, BF16), of(basis_in.shape, BF16), of(coupling.shape, F32), of(far_in.shape, jnp.int32),
            of((4, rank, rank), BF16), mat(8), mat(4), pair,
        ),
        in_specs=[HBM] * 5, out_specs=(VMEM,) * 8,
        scratch_shapes=[pltpu.VMEM(transfer.shape, F32), pltpu.SemaphoreType.DMA((5,))],
        name="leaf", compiler_params=PARAMS,
    )(*[in_hbm(a) for a in (src_in, basis_in, transfer, coupling, far_in)])

    def up4(own, masks, axis, copies, *behind):
        got = [swap(own, m) for m in masks]
        top = of((copies,) + pair.shape, F32) if copies else pair
        return pl.pallas_call(
            lambda *refs: up4_kernel(copies, axis, refs),
            out_shape=(mat(8), mat(4), top), in_specs=[VMEM] * (5 + len(behind)), out_specs=(VMEM,) * 3,
            scratch_shapes=[pltpu.VMEM((4,) + pair.shape, F32)], name="up4", compiler_params=PARAMS,
        )(own, *got, tsplit, *behind)

    def up2(own, mask, axis, *behind):
        return pl.pallas_call(
            lambda *refs: up2_kernel(axis, refs),
            out_shape=(mat(4), pair), in_specs=[VMEM] * (3 + len(behind)), out_specs=(VMEM,) * 2,
            scratch_shapes=[pltpu.VMEM((2,) + pair.shape, F32)], name="up2", compiler_params=PARAMS,
        )(own, swap(own, mask), tsplit, *behind)

    def later(array, other):
        return lax.optimization_barrier((array, other))[0]

    loc0, loc1 = pl.pallas_call(
        low_kernel, out_shape=(mat(8), mat(4)), in_specs=[VMEM] * 4, out_specs=(VMEM,) * 2,
        name="low", compiler_params=PARAMS,
    )(far, coup, m0, m1)
    cross1 = swap_across(later(src, loc0), 1)
    m2, m3, pair4 = up4(pair2, (1, 2, 3), "x", 0, loc0)
    cross4 = swap_across(later(src, pair4), 4)
    m4, pair5 = up2(pair4, 4, "c", loc0)
    loc2 = pl.pallas_call(
        low2_kernel, out_shape=mat(2), in_specs=[VMEM] * 4, out_specs=VMEM,
        name="low2", compiler_params=PARAMS,
    )(far, coup, m2, pair5)
    src3 = later(src, loc2)
    core, side = swap(src3, 4), swap(src3, 1)

    near = pl.pallas_call(
        near_kernel,
        out_shape=of((rhs, points), F32),
        in_specs=[HBM] + [VMEM] * 5 + [HBM], out_specs=VMEM,
        scratch_shapes=[
            pltpu.VMEM((5 * leaves, rhs, pts), BF16),
            pltpu.VMEM(near_blocks.shape, BF16),
            pltpu.SMEM(near_pattern.shape[::-1], jnp.int32),
            pltpu.SemaphoreType.DMA((leaves,)),
            pltpu.SemaphoreType.DMA,
        ],
        name="near", compiler_params=PARAMS,
    )(in_hbm(near_pattern.T), src, core, side, cross4, cross1, in_hbm(near_blocks))

    m5, m6, pair7 = up4(pair5, (8, 16, 24), "y", 8, loc2, cross4, cross1)
    g7 = lax.all_to_all(pair7, "z", 0, 0, tiled=True)

    part, ghigh, glow = pl.pallas_call(
        mid_kernel,
        out_shape=(of((rhs, points), F32), of((rhs, points), BF16), of((rhs, points), BF16)),
        in_specs=[VMEM] * 12, out_specs=(VMEM,) * 3,
        name="mid", compiler_params=PARAMS,
    )(far, coup, tsplit, basis, loc0, loc1, loc2, m3, m4, m5, m6, near)

    product = pl.pallas_call(
        last_kernel,
        out_shape=of((rhs, points), BF16),
        in_specs=[VMEM] * 7, out_specs=VMEM,
        scratch_shapes=[pltpu.VMEM((n, rhs, rank), F32) for n in (16, 8, 4)],
        name="last", compiler_params=PARAMS,
    )(far, coup, tsplit, g7, part, ghigh, glow)
    return product.T


def solution(mesh):
    leaf, sub = mesh.shape["leaf"], mesh.shape["sub"]
    cut = Mesh(mesh.devices.reshape(leaf // 8, 4, 2, sub), AXES)
    placed = (
        P(AXES, None),
        P(AXES, None, None),
        P(),
        P(),
        P(AXES, None, None, None),
        P(AXES, None),
        P(),
    )
    return jax.shard_map(shards, mesh=cut, in_specs=placed, out_specs=P(AXES, None), check_vma=False)
```

time: 64.4 us -> 49 us (0.76)
  the two profiles are of different devices: /device:TPU:127 before, /device:TPU:1 now
where the time goes in v2:
time: 49 us; the launch traced here: 48.8 us
  starting transfers between devices  24.3 us (50%)
  Pallas kernels  13.6 us (28%)
  waiting for transfers between devices  10.7 us (22%)
    ppermute x9, starting transfers between devices, swap(): lax.ppermute(array, AXES, [(i, i ^ mask) for i in range(device_count())])  15 us
    ppermute x9, waiting for transfers between devices, swap(): lax.ppermute(array, AXES, [(i, i ^ mask) for i in range(device_count())])  10.7 us
    ppermute x2, starting transfers between devices, swap_across(): return lax.ppermute(array, AXES, pairs)  5.82 us
    pallas_call x1, Pallas kernels, shards(): pl.pallas_call(near_kernel, out_shape=of((rhs, points), F32), in_specs=[H...  4.36 us
    all_to_all x1, starting transfers between devices, shards(): g7 = lax.all_to_all(pair7, 'z', 0, 0, tiled=True)  3.47 us
    pallas_call x1, Pallas kernels, shards(): pl.pallas_call(last_kernel, out_shape=of((rhs, points), BF16), in_specs=[...  2.24 us
    pallas_call x1, Pallas kernels, shards(): pl.pallas_call(mid_kernel, out_shape=(of((rhs, points), F32), of((rhs, po...  1.78 us
    pallas_call x2, Pallas kernels, up4(): pl.pallas_call(lambda *refs: up4_kernel(copies, axis, refs), out_shape=(m...  1.75 us
  transfers between devices with their start and end apart: 12, of which 3 were waited for; matrix products, arithmetic and copies ran while one was open for 0% of the time, Pallas kernels for 17%

profile of v2, /device:TPU:1, one launch (start us, length us, event | category | flops | bytes accessed | tf_op | source)
XLA Modules:
  0.0 48.8 jit_solution(17415123278480826714)
XLA Ops:
  0.0 1.7 %leaf.1 = (bf16[64,2048]{1,0:T(8,128)(2,1)S(1)}, bf16[8,64,256]{2,1,0:T(8,128)(2,1)S(1)}, f32[3,64,64]{2,1,0:T(8,128)S(1)}, s32[3,4092]{1,0:T(4,128)S(1)}, bf16[...) custom-call(bf16[64,2048]{1,0:T(8,128)(2,1)} %bitcast.5, ...), custom_call_target="tpu_custom_call" | custom-call | tf_op jit(solution)/shard_map/leaf/pallas_call | solution.py:286
  1.7 3.4 %collective-permute-start.2 = (f32[64,128]{1,0:T(8,128)S(1)}, f32[64,128]{1,0:T(8,128)S(1)}, u32[]{:S(2)}, u32[]{:S(2)}) collective-permute-start(f32[64,128]{1,0:T(8,128)S(1)} %get-tuple-element.32.refs_0_), channel_id=1, source_target_pairs={{0,3},{1,2},{2,1},{3,0},{4,7},{5,6},{6,5},{7,4},{8,11},{9,10},{10,... | collective-permute-start | bytes 98312 | tf_op jit(solution)/shard_map/ppermute | solution.py:57
  5.1 0.5 %collective-permute-start.1 = (f32[64,128]{1,0:T(8,128)S(1)}, f32[64,128]{1,0:T(8,128)S(1)}, u32[]{:S(2)}, u32[]{:S(2)}) collective-permute-start(f32[64,128]{1,0:T(8,128)S(1)} %get-tuple-element.32.refs_0_), channel_id=1, source_target_pairs={{0,2},{1,3},{2,0},{3,1},{4,6},{5,7},{6,4},{7,5},{8,10},{9,11},{10,... | collective-permute-start | bytes 98312 | tf_op jit(solution)/shard_map/ppermute | solution.py:57
  5.6 0.2 collective-permute-start
  5.8 1.1 %low.1 = (f32[8,64,64]{2,1,0:T(8,128)S(1)}, f32[4,64,64]{2,1,0:T(8,128)S(1)}) custom-call(s32[3,4092]{1,0:T(4,128)S(1)} %get-tuple-element.29.far, f32[3,64,64]{2,1,0:T(8,128)S(1)} %get-tuple-element.30.coupling, f32[8,64,64]{2,1,0:T(8,128)S(1)} %get-tuple-element.33.m0, f32[4,64,64]{2,1,0:T(8,128)S(1)} %get-tuple-element.34.m1), custom_call_target="tpu_custom_call" | custom-call | tf_op jit(solution)/shard_map/low/pallas_call | solution.py:316
  6.9 4.1 %collective-permute-start.8 = (bf16[64,2048]{1,0:T(8,128)(2,1)S(1)}, bf16[64,2048]{1,0:T(8,128)(2,1)S(1)}, u32[]{:S(2)}, u32[]{:S(2)}) collective-permute-start(bf16[64,2048]{1,0:T(8,128)(2,1)S(1)} %get-tuple-element.49.own), channel_id=1, source_target_pairs={{0,255},{1,2},{2,1},{3,4},{4,3},{5,6},{6,5},{7,8},{8,7},{9,10},{10... | collective-permute-start | bytes 786440 | tf_op jit(solution)/shard_map/ppermute | solution.py:67
  11.0 0.0 collective-permute-done.2.refs_3_
  11.0 0.0 collective-permute-done.1.refs_2_
  11.0 0.0 collective-permute-done.refs_1_
  11.0 0.5 up4.2
  11.5 1.8 %collective-permute-start.7 = (bf16[64,2048]{1,0:T(8,128)(2,1)S(1)}, bf16[64,2048]{1,0:T(8,128)(2,1)S(1)}, u32[]{:S(2)}, u32[]{:S(2)}) collective-permute-start(bf16[64,2048]{1,0:T(8,128)(2,1)S(1)} %get-tuple-element.49.own), channel_id=1, source_target_pairs={{0,252},{1,253},{2,254},{3,255},{4,8},{5,9},{6,10},{7,11},{8,4},{9... | collective-permute-start | bytes 786440 | tf_op jit(solution)/shard_map/ppermute | solution.py:67
  13.3 6.8 %collective-permute-start.3 = (f32[64,128]{1,0:T(8,128)S(1)}, f32[64,128]{1,0:T(8,128)S(1)}, u32[]{:S(2)}, u32[]{:S(2)}) collective-permute-start(f32[64,128]{1,0:T(8,128)S(1)} %get-tuple-element.36.refs_0_), channel_id=1, source_target_pairs={{0,4},{1,5},{2,6},{3,7},{4,0},{5,1},{6,2},{7,3},{8,12},{9,13},{10,... | collective-permute-start | bytes 98312 | tf_op jit(solution)/shard_map/ppermute | solution.py:57
  20.0 0.9 %collective-permute-done.3.refs_1_ = f32[64,128]{1,0:T(8,128)S(1)} collective-permute-done((f32[64,128]{1,0:T(8,128)S(1)}, f32[64,128]{1,0:T(8,128)S(1)}, u32[]{:S(2)}, u32[]{:S(2)}) %collective-permute-start.3) | collective-permute-done | bytes 32800 | tf_op jit(solution)/shard_map/ppermute | solution.py:57
  20.9 0.3 up2.1
  21.2 0.1 collective-permute-start.6
  21.3 0.1 collective-permute-start.5
  21.4 3.1 %collective-permute-start.4 = (f32[64,128]{1,0:T(8,128)S(1)}, f32[64,128]{1,0:T(8,128)S(1)}, u32[]{:S(2)}, u32[]{:S(2)}) collective-permute-start(f32[64,128]{1,0:T(8,128)S(1)} %get-tuple-element.37.behind.refs_0_), channel_id=1, source_target_pairs={{0,8},{1,9},{2,10},{3,11},{4,12},{5,13},{6,14},{7,15},{8,0},{9,1},... | collective-permute-start | bytes 98312 | tf_op jit(solution)/shard_map/ppermute | solution.py:57
  24.6 0.4 low2.1.refs_5_.loc2
  24.9 3.5 %collective-permute-done.6.refs_3_ = f32[64,128]{1,0:T(8,128)S(1)} collective-permute-done((f32[64,128]{1,0:T(8,128)S(1)}, f32[64,128]{1,0:T(8,128)S(1)}, u32[]{:S(2)}, u32[]{:S(2)}) %collective-permute-start.6) | collective-permute-done | bytes 32800 | tf_op jit(solution)/shard_map/ppermute | solution.py:57
  28.4 0.0 collective-permute-done.5.refs_2_
  28.4 0.0 collective-permute-done.4.refs_1_
  28.4 0.0 collective-permute-done.8.refs_7_.cross1
  28.4 0.0 collective-permute-done.7.refs_6_.cross4
  28.4 1.3 %up4.3 = (f32[8,64,64]{2,1,0:T(8,128)S(1)}, f32[4,64,64]{2,1,0:T(8,128)S(1)}, f32[8,64,128]{2,1,0:T(8,128)}) custom-call(f32[64,128]{1,0:T(8,128)S(1)} %get-tuple-element.37.behind.refs_0_, f32[64,128]{1,0:T(8,128)S(1)} %collective-permute-done.4.refs_1_, f32[64,128]{1,0:T(8,128)S(1)} %collective-permute-done.5.refs_2_, ...), custom_call_target="tpu_custom_call" | custom-call | tf_op jit(solution)/shard_map/up4/pallas_call | solution.py:300
  29.7 3.5 %all-to-all-start = ((f32[8,64,128]{2,1,0:T(8,128)}), f32[8,64,128]{2,1,0:T(8,128)S(1)}, u32[]{:S(2)}, u32[]{:S(2)}) async-start(f32[8,64,128]{2,1,0:T(8,128)} %get-tuple-element.42), calls=%async_computation | async-start | bytes 524288 | tf_op jit(solution)/shard_map/all_to_all | solution.py:346
  33.2 0.1 collective-permute-start.10
  33.2 0.8 %collective-permute-start.9 = (bf16[64,2048]{1,0:T(8,128)(2,1)S(1)}, bf16[64,2048]{1,0:T(8,128)(2,1)S(1)}, u32[]{:S(2)}, u32[]{:S(2)}) collective-permute-start(bf16[64,2048]{1,0:T(8,128)(2,1)S(1)} %get-tuple-element.49.own), channel_id=1, source_target_pairs={{0,4},{1,5},{2,6},{3,7},{4,0},{5,1},{6,2},{7,3},{8,12},{9,13},{10,... | collective-permute-start | bytes 786440 | tf_op jit(solution)/shard_map/ppermute | solution.py:57
  34.0 6.4 %collective-permute-done.10.side = bf16[64,2048]{1,0:T(8,128)(2,1)S(1)} collective-permute-done((bf16[64,2048]{1,0:T(8,128)(2,1)S(1)}, bf16[64,2048]{1,0:T(8,128)(2,1)S(1)}, u32[]{:S(2)}, u32[]{:S(2)}) %collective-permute-start.10) | collective-permute-done | bytes 262176 | tf_op jit(solution)/shard_map/ppermute | solution.py:57
  40.4 0.0 collective-permute-done.9.core
  40.4 4.4 %near.1 = f32[64,2048]{1,0:T(8,128)S(1)} custom-call(s32[4,8]{1,0:T(4,128)} %bitcast.8, bf16[64,2048]{1,0:T(8,128)(2,1)S(1)} %get-tuple-element.49.own, bf16[64,2048]{1,0:T(8,128)(2,1)S(1)} %collective-permute-done.9.core, bf16[64,2048]{1,0:T(8,128)(2,1)S(1)} %collective-permute-done.10.side, bf16[64,2048]{1,0:T(8,128)(2,1)S(1)} %collective-permute-done.7.refs_6_.cross4, ...), custom_call_target="tpu_custom_call" | custom-call | tf_op jit(solution)/shard_map/near/pallas_call | solution.py:331
  44.7 1.8 %mid.1 = (f32[64,2048]{1,0:T(8,128)S(1)}, bf16[64,2048]{1,0:T(8,128)(2,1)S(1)}, bf16[64,2048]{1,0:T(8,128)(2,1)S(1)}) custom-call(s32[3,4092]{1,0:T(4,128)S(1)} %get-tuple-element.29.far, f32[3,64,64]{2,1,0:T(8,128)S(1)} %get-tuple-element.30.coupling, bf16[4,64,64]{2,1,0:T(8,128)(2,1)S(1)} %get-tuple-element.31.refs_4_.refs_2_.tsplit, ...), custom_call_target="tpu_custom_call" | custom-call | tf_op jit(solution)/shard_map/mid/pallas_call | solution.py:348
  46.5 0.0 all-to-all-done.g7
  46.5 2.2 %last.1 = bf16[64,2048]{1,0:T(8,128)(2,1)} custom-call(s32[3,4092]{1,0:T(4,128)S(1)} %get-tuple-element.29.far, f32[3,64,64]{2,1,0:T(8,128)S(1)} %get-tuple-element.30.coupling, bf16[4,64,64]{2,1,0:T(8,128)(2,1)S(1)} %get-tuple-element.31.refs_4_.refs_2_.tsplit, f32[8,64,128]{2,1,0:T(8,128)S(1)} %all-to-all-done.g7, f32[64,2048]{1,0:T(8,128)S(1)} %get-tuple-element.50.part, ...), custom_call_target="tpu_custom_call" | custom-call | tf_op jit(solution)/shard_map/last/pallas_call | solution.py:355
Async XLA Ops:
  1.7 9.3 %collective-permute-start.2 = (f32[64,128]{1,0:T(8,128)S(1)}, f32[64,128]{1,0:T(8,128)S(1)}, u32[]{:S(2)}, u32[]{:S(2)}) collective-permute-start(f32[64,128]{1,0:T(8,128)S(1)} %get-tuple-element.32.refs_0_), channel_id=1, source_target_pairs={{0,3},{1,2},{2,1},{3,0},{4,7},{5,6},{6,5},{7,4},{8,11},{9,10},{10,... | collective-permute-start | bytes 98312 | tf_op jit(solution)/shard_map/ppermute | solution.py:57
  5.1 5.9 %collective-permute-start.1 = (f32[64,128]{1,0:T(8,128)S(1)}, f32[64,128]{1,0:T(8,128)S(1)}, u32[]{:S(2)}, u32[]{:S(2)}) collective-permute-start(f32[64,128]{1,0:T(8,128)S(1)} %get-tuple-element.32.refs_0_), channel_id=1, source_target_pairs={{0,2},{1,3},{2,0},{3,1},{4,6},{5,7},{6,4},{7,5},{8,10},{9,11},{10,... | collective-permute-start | bytes 98312 | tf_op jit(solution)/shard_map/ppermute | solution.py:57
  5.6 5.4 %collective-permute-start = (f32[64,128]{1,0:T(8,128)S(1)}, f32[64,128]{1,0:T(8,128)S(1)}, u32[]{:S(2)}, u32[]{:S(2)}) collective-permute-start(f32[64,128]{1,0:T(8,128)S(1)} %get-tuple-element.32.refs_0_), channel_id=1, source_target_pairs={{0,1},{1,0},{2,3},{3,2},{4,5},{5,4},{6,7},{7,6},{8,9},{9,8},{10,11... | collective-permute-start | bytes 98312 | tf_op jit(solution)/shard_map/ppermute | solution.py:57
  6.9 21.5 %collective-permute-start.8 = (bf16[64,2048]{1,0:T(8,128)(2,1)S(1)}, bf16[64,2048]{1,0:T(8,128)(2,1)S(1)}, u32[]{:S(2)}, u32[]{:S(2)}) collective-permute-start(bf16[64,2048]{1,0:T(8,128)(2,1)S(1)} %get-tuple-element.49.own), channel_id=1, source_target_pairs={{0,255},{1,2},{2,1},{3,4},{4,3},{5,6},{6,5},{7,8},{8,7},{9,10},{10... | collective-permute-start | bytes 786440 | tf_op jit(solution)/shard_map/ppermute | solution.py:67
  11.5 16.9 %collective-permute-start.7 = (bf16[64,2048]{1,0:T(8,128)(2,1)S(1)}, bf16[64,2048]{1,0:T(8,128)(2,1)S(1)}, u32[]{:S(2)}, u32[]{:S(2)}) collective-permute-start(bf16[64,2048]{1,0:T(8,128)(2,1)S(1)} %get-tuple-element.49.own), channel_id=1, source_target_pairs={{0,252},{1,253},{2,254},{3,255},{4,8},{5,9},{6,10},{7,11},{8,4},{9... | collective-permute-start | bytes 786440 | tf_op jit(solution)/shard_map/ppermute | solution.py:67
  13.3 7.6 %collective-permute-start.3 = (f32[64,128]{1,0:T(8,128)S(1)}, f32[64,128]{1,0:T(8,128)S(1)}, u32[]{:S(2)}, u32[]{:S(2)}) collective-permute-start(f32[64,128]{1,0:T(8,128)S(1)} %get-tuple-element.36.refs_0_), channel_id=1, source_target_pairs={{0,4},{1,5},{2,6},{3,7},{4,0},{5,1},{6,2},{7,3},{8,12},{9,13},{10,... | collective-permute-start | bytes 98312 | tf_op jit(solution)/shard_map/ppermute | solution.py:57
  21.2 7.2 %collective-permute-start.6 = (f32[64,128]{1,0:T(8,128)S(1)}, f32[64,128]{1,0:T(8,128)S(1)}, u32[]{:S(2)}, u32[]{:S(2)}) collective-permute-start(f32[64,128]{1,0:T(8,128)S(1)} %get-tuple-element.37.behind.refs_0_), channel_id=1, source_target_pairs={{0,24},{1,25},{2,26},{3,27},{4,28},{5,29},{6,30},{7,31},{8,16},{9,... | collective-permute-start | bytes 98312 | tf_op jit(solution)/shard_map/ppermute | solution.py:57
  21.3 7.1 %collective-permute-start.5 = (f32[64,128]{1,0:T(8,128)S(1)}, f32[64,128]{1,0:T(8,128)S(1)}, u32[]{:S(2)}, u32[]{:S(2)}) collective-permute-start(f32[64,128]{1,0:T(8,128)S(1)} %get-tuple-element.37.behind.refs_0_), channel_id=1, source_target_pairs={{0,16},{1,17},{2,18},{3,19},{4,20},{5,21},{6,22},{7,23},{8,24},{9,... | collective-permute-start | bytes 98312 | tf_op jit(solution)/shard_map/ppermute | solution.py:57
  21.4 7.0 %collective-permute-start.4 = (f32[64,128]{1,0:T(8,128)S(1)}, f32[64,128]{1,0:T(8,128)S(1)}, u32[]{:S(2)}, u32[]{:S(2)}) collective-permute-start(f32[64,128]{1,0:T(8,128)S(1)} %get-tuple-element.37.behind.refs_0_), channel_id=1, source_target_pairs={{0,8},{1,9},{2,10},{3,11},{4,12},{5,13},{6,14},{7,15},{8,0},{9,1},... | collective-permute-start | bytes 98312 | tf_op jit(solution)/shard_map/ppermute | solution.py:57
  29.7 16.8 %all-to-all-start = ((f32[8,64,128]{2,1,0:T(8,128)}), f32[8,64,128]{2,1,0:T(8,128)S(1)}, u32[]{:S(2)}, u32[]{:S(2)}) async-start(f32[8,64,128]{2,1,0:T(8,128)} %get-tuple-element.42), calls=%async_computation | async-start | bytes 524288 | tf_op jit(solution)/shard_map/all_to_all | solution.py:346
  33.2 7.2 %collective-permute-start.10 = (bf16[64,2048]{1,0:T(8,128)(2,1)S(1)}, bf16[64,2048]{1,0:T(8,128)(2,1)S(1)}, u32[]{:S(2)}, u32[]{:S(2)}) collective-permute-start(bf16[64,2048]{1,0:T(8,128)(2,1)S(1)} %get-tuple-element.49.own), channel_id=1, source_target_pairs={{0,1},{1,0},{2,3},{3,2},{4,5},{5,4},{6,7},{7,6},{8,9},{9,8},{10,11... | collective-permute-start | bytes 786440 | tf_op jit(solution)/shard_map/ppermute | solution.py:57
  33.2 7.1 %collective-permute-start.9 = (bf16[64,2048]{1,0:T(8,128)(2,1)S(1)}, bf16[64,2048]{1,0:T(8,128)(2,1)S(1)}, u32[]{:S(2)}, u32[]{:S(2)}) collective-permute-start(bf16[64,2048]{1,0:T(8,128)(2,1)S(1)} %get-tuple-element.49.own), channel_id=1, source_target_pairs={{0,4},{1,5},{2,6},{3,7},{4,0},{5,1},{6,2},{7,3},{8,12},{9,13},{10,... | collective-permute-start | bytes 786440 | tf_op jit(solution)/shard_map/ppermute | solution.py:57

commit v3 on v2

--- a/solution.py
+++ b/solution.py
@@ -13,7 +13,7 @@
 VMEM = pl.BlockSpec(memory_space=pltpu.VMEM)
 SMEM = pl.BlockSpec(memory_space=pltpu.SMEM)
 HBM = pl.BlockSpec(memory_space=pltpu.HBM)
-PARAMS = pltpu.CompilerParams(vmem_limit_bytes=40 * 1024 * 1024)
+PARAMS = pltpu.CompilerParams(vmem_limit_bytes=4 * 1024 * 1024)
 
 
 def in_hbm(array):
@@ -67,7 +67,7 @@
     return lax.ppermute(array, AXES, pairs)
 
 
-def leaf_kernel(src_in, basis_in, transfer_in, coupling_in, far_in, src, basis, coupling, far, tsplit, m0, m1, pair2, raw, sems):
+def leaf_kernel(src_in, basis_in, transfer_in, coupling_in, far_in, src, coupling, far, tsplit, m0, m1, pair2, basis, raw, sems):
     copies = [
         pltpu.make_async_copy(a, b, sems.at[i])
         for i, (a, b) in enumerate(
@@ -107,16 +107,16 @@
 
 def up4_kernel(copies, axis, refs):
     own, p1, p2, p3, tsplit = refs[:5]
-    a, b, pair, ordered = refs[-4:]
+    ab, pair, ordered = refs[-3:]
     t = transfers(tsplit)
     here = lax.axis_index(axis)
     for i, ref in enumerate((own, p1, p2, p3)):
         ordered[here ^ i] = ref[...]
-    clusters([ordered[i] for i in range(4)], a)
-    low = [a[i] for i in range(8)]
+    clusters([ordered[i] for i in range(4)], ab)
+    low = [ab[i] for i in range(8)]
     mid = [lift(low[2 * i], low[2 * i + 1], t) for i in range(4)]
     for i, v in enumerate(mid):
-        b[i] = v
+        ab[8 + i] = v
     top = pair_of(lift(mid[0], mid[1], t), lift(mid[2], mid[3], t))
     if copies:
         for i in range(copies):
@@ -134,34 +134,6 @@
         ordered[here ^ i] = ref[...]
     clusters([ordered[i] for i in range(2)], a)
     pair[...] = pair_of(lift(a[0], a[1], t), lift(a[2], a[3], t))
-
-
-def near_kernel(pattern_in, own, core, side, cross4, cross1, blocks_in, out, held, blocks, pattern, sems, sem):
-    leaves, slots, pts = blocks_in.shape[:3]
-    pattern_copy = pltpu.make_async_copy(pattern_in, pattern, sem)
-    pattern_copy.start()
-    copies = [pltpu.make_async_copy(blocks_in.at[i], blocks.at[i], sems.at[i]) for i in range(leaves)]
-    for copy in copies:
-        copy.start()
-    for n, ref in enumerate((own, core, side, cross4, cross1)):
-        for i in range(leaves):
-            held[n * leaves + i] = ref[:, i * pts : (i + 1) * pts]
-    pattern_copy.wait()
-    me = device_index()
-    n = device_count()
-    others = [me, me ^ 4, me ^ 1, across(me, 4, n)]
-    for i in range(leaves):
-        copies[i].wait()
-        total = None
-        for s in range(slots):
-            j = pattern[s, i]
-            device = j // leaves
-            slot = jnp.int32(4)
-            for k, other in enumerate(others):
-                slot = jnp.where(device == other, k, slot)
-            term = dot(held[slot * leaves + j % leaves], blocks[i, s], NT)
-            total = term if total is None else total + term
-        out[:, i * pts : (i + 1) * pts] = total
 
 
 def start_of(level):
@@ -190,30 +162,48 @@
     return total
 
 
-def local(far, c, level, cluster, values, width):
+def local(far, c, level, cluster, values, width, first=0):
     at = cluster % width
-    group = at // 4 * 4
+    group = at // 4 * 4 + first
     return couple(weights_of(far, level, cluster), [values[group + (at + j) % 4] for j in (1, 2, 3)], c)
 
 
-def low_kernel(far, coupling, m0, m1, loc0, loc1):
+def low_kernel(far, coupling, m1, loc_a):
     c = [split(coupling[i]) for i in range(3)]
     d = device_index()
-    for level, values, out in ((0, m0, loc0), (1, m1, loc1)):
-        count = values.shape[0]
-        for i in range(count):
-            w = weights_of(far, level, d * count + i)
-            out[i] = couple(w, [values[i // 4 * 4 + (i + j) % 4] for j in (1, 2, 3)], c)
-
-
-def low2_kernel(far, coupling, m2, behind, loc2):
+    for i in range(4):
+        w = weights_of(far, 1, d * 4 + i)
+        loc_a[i] = couple(w, [m1[(i + j) % 4] for j in (1, 2, 3)], c)
+
+
+def low2_kernel(far, coupling, m0, m23, m4, behind, loc_b):
     c = [split(coupling[i]) for i in range(3)]
     d = device_index()
+    for i in range(8):
+        w = weights_of(far, 0, d * 8 + i)
+        loc_b[4 + i] = couple(w, [m0[i // 4 * 4 + (i + j) % 4] for j in (1, 2, 3)], c)
     for i in range(2):
-        loc2[i] = local(far, c, 2, d * 2 + i, m2, 8)
-
-
-def mid_kernel(far, coupling, tsplit, basis, loc0, loc1, loc2, m3, m4, m5, m6, near, part, ghigh, glow):
+        loc_b[i] = local(far, c, 2, d * 2 + i, m23, 8)
+    loc_b[2] = local(far, c, 3, d, m23, 4, 8)
+    loc_b[3] = local(far, c, 4, d >> 1, m4, 4)
+
+
+def mid_kernel(far, coupling, tsplit, loc_a, loc_b, m56, core, side, cross4, cross1,
+               src_in, basis_in, pattern_in, blocks_in, part, g, held, basis, blocks, pattern, sems, own_sems, pair_sems):
+    leaves, slots, pts = blocks_in.shape[:3]
+    own_copies = [
+        pltpu.make_async_copy(src_in.at[:, i * pts : (i + 1) * pts], held.at[i], own_sems.at[i]) for i in range(leaves)
+    ]
+    for copy in own_copies:
+        copy.start()
+    basis_copy = pltpu.make_async_copy(basis_in, basis, pair_sems.at[0])
+    basis_copy.start()
+    pattern_copy = pltpu.make_async_copy(pattern_in, pattern, pair_sems.at[1])
+    pattern_copy.start()
+    copies = [pltpu.make_async_copy(blocks_in.at[i], blocks.at[i], sems.at[i]) for i in range(leaves)]
+    for copy in copies:
+        copy.start()
+
     c = [split(coupling[i]) for i in range(3)]
     t = transfers(tsplit)
     d = device_index()
@@ -221,35 +211,51 @@
     cols = lax.broadcasted_iota(jnp.int32, (64, 64), 1)
     chain = jnp.where(rows == cols, 1.0, 0.0).astype(F32)
     field = None
-    for level, values, width in ((6, m6, 4), (5, m5, 8), (4, m4, 4), (3, m3, 4)):
+    for level, width, first in ((6, 4, 8), (5, 8, 0), (4, 0, 0), (3, 0, 0)):
         cluster = d >> (level - 3)
         child = cluster % 2
         one = (tsplit[2 * child], tsplit[2 * child + 1])
-        own = local(far, c, level, cluster, values, width)
+        here = local(far, c, level, cluster, m56, width, first) if width else loc_b[level - 1]
         if field is None:
             chain = dot3(split(chain), one, NT)
-            field = own
+            field = here
         else:
             both = dot3(split(jnp.concatenate([field, chain], 0)), one, NT)
-            field, chain = own + both[:64], both[64:]
+            field, chain = here + both[:64], both[64:]
     parents = [(field, chain)]
-    for level, count in ((2, 2), (1, 4), (0, 8)):
+    for locs, first, count in ((loc_b, 0, 2), (loc_a, 0, 4), (loc_b, 4, 8)):
         below = []
         for i in range(count):
-            own = (loc0, loc1, loc2)[level][i]
             both = dot3(split(jnp.concatenate(parents[i // 2], 0)), t[i % 2], NT)
-            below.append((own + both[:64], both[64:]))
+            below.append((locs[first + i] + both[:64], both[64:]))
         parents = below
-    pts = basis.shape[2]
+
+    for n, ref in enumerate((core, side, cross4, cross1)):
+        for i in range(leaves):
+            held[(n + 1) * leaves + i] = ref[:, i * pts : (i + 1) * pts]
+    for copy in own_copies:
+        copy.wait()
+    basis_copy.wait()
+    pattern_copy.wait()
+    others = [d, d ^ 4, d ^ 1, across(d, 4, device_count())]
     for i, both in enumerate(parents):
+        at = slice(i * pts, (i + 1) * pts)
         high, low = split(jnp.concatenate(both, 0))
         whole = dot(high, basis[i], NN) + dot(low, basis[i], NN)
-        at = slice(i * pts, (i + 1) * pts)
-        part[:, at] = whole[:64] + near[:, at]
-        ghigh[:, at], glow[:, at] = split(whole[64:])
-
-
-def last_kernel(far, coupling, tsplit, g7, part, ghigh, glow, out, m7, m8, m9):
+        g[0, :, at], g[1, :, at] = split(whole[64:])
+        copies[i].wait()
+        total = whole[:64]
+        for s in range(slots):
+            j = pattern[s, i]
+            device = j // leaves
+            slot = jnp.int32(4)
+            for k, other in enumerate(others):
+                slot = jnp.where(device == other, k, slot)
+            total = total + dot(held[slot * leaves + j % leaves], blocks[i, s], NT)
+        part[:, at] = total
+
+
+def last_kernel(far, coupling, tsplit, g7, part, g, out, m7, m8, m9):
     c = [split(coupling[i]) for i in range(3)]
     t = transfers(tsplit)
     d = device_index()
@@ -268,7 +274,7 @@
     step = 256
     for at in range(0, out.shape[1], step):
         at = slice(at, at + step)
-        far_part = dot(high, ghigh[:, at], NN) + (dot(high, glow[:, at], NN) + dot(low, ghigh[:, at], NN))
+        far_part = dot(high, g[0, :, at], NN) + (dot(high, g[1, :, at], NN) + dot(low, g[0, :, at], NN))
         out[:, at] = (far_part + part[:, at]).astype(BF16)
 
 
@@ -283,14 +289,14 @@
     mat = lambda n: of((n, rhs, rank), F32)
     pair = of((rhs, 2 * rank), F32)
 
-    src, basis, coup, far, tsplit, m0, m1, pair2 = pl.pallas_call(
+    src, coup, far, tsplit, m0, m1, pair2 = pl.pallas_call(
         leaf_kernel,
         out_shape=(
-            of(src_in.shape, BF16), of(basis_in.shape, BF16), of(coupling.shape, F32), of(far_in.shape, jnp.int32),
+            of(src_in.shape, BF16), of(coupling.shape, F32), of(far_in.shape, jnp.int32),
             of((4, rank, rank), BF16), mat(8), mat(4), pair,
         ),
-        in_specs=[HBM] * 5, out_specs=(VMEM,) * 8,
-        scratch_shapes=[pltpu.VMEM(transfer.shape, F32), pltpu.SemaphoreType.DMA((5,))],
+        in_specs=[HBM] * 5, out_specs=(VMEM,) * 7,
+        scratch_shapes=[pltpu.VMEM(basis_in.shape, BF16), pltpu.VMEM(transfer.shape, F32), pltpu.SemaphoreType.DMA((5,))],
         name="leaf", compiler_params=PARAMS,
     )(*[in_hbm(a) for a in (src_in, basis_in, transfer, coupling, far_in)])
 
@@ -299,7 +305,7 @@
         top = of((copies,) + pair.shape, F32) if copies else pair
         return pl.pallas_call(
             lambda *refs: up4_kernel(copies, axis, refs),
-            out_shape=(mat(8), mat(4), top), in_specs=[VMEM] * (5 + len(behind)), out_specs=(VMEM,) * 3,
+            out_shape=(mat(12), top), in_specs=[VMEM] * (5 + len(behind)), out_specs=(VMEM,) * 2,
             scratch_shapes=[pltpu.VMEM((4,) + pair.shape, F32)], name="up4", compiler_params=PARAMS,
         )(own, *got, tsplit, *behind)
 
@@ -313,52 +319,48 @@
     def later(array, other):
         return lax.optimization_barrier((array, other))[0]
 
-    loc0, loc1 = pl.pallas_call(
-        low_kernel, out_shape=(mat(8), mat(4)), in_specs=[VMEM] * 4, out_specs=(VMEM,) * 2,
+    loc_a = pl.pallas_call(
+        low_kernel, out_shape=mat(4), in_specs=[VMEM] * 3, out_specs=VMEM,
         name="low", compiler_params=PARAMS,
-    )(far, coup, m0, m1)
-    cross1 = swap_across(later(src, loc0), 1)
-    m2, m3, pair4 = up4(pair2, (1, 2, 3), "x", 0, loc0)
-    cross4 = swap_across(later(src, pair4), 4)
-    m4, pair5 = up2(pair4, 4, "c", loc0)
-    loc2 = pl.pallas_call(
-        low2_kernel, out_shape=mat(2), in_specs=[VMEM] * 4, out_specs=VMEM,
+    )(far, coup, m1)
+    s2 = later(src, loc_a)
+    core, cross4 = swap(s2, 4), swap_across(s2, 4)
+    m23, pair4 = up4(pair2, (1, 2, 3), "x", 0, loc_a)
+    s3 = later(src, pair4)
+    side, cross1 = swap(s3, 1), swap_across(s3, 1)
+    m4, pair5 = up2(pair4, 4, "c", cross4, core)
+    loc_b = pl.pallas_call(
+        low2_kernel, out_shape=mat(12), in_specs=[VMEM] * 6, out_specs=VMEM,
         name="low2", compiler_params=PARAMS,
-    )(far, coup, m2, pair5)
-    src3 = later(src, loc2)
-    core, side = swap(src3, 4), swap(src3, 1)
-
-    near = pl.pallas_call(
-        near_kernel,
-        out_shape=of((rhs, points), F32),
-        in_specs=[HBM] + [VMEM] * 5 + [HBM], out_specs=VMEM,
+    )(far, coup, m0, m23, m4, pair5)
+
+    m56, pair7 = up4(pair5, (8, 16, 24), "y", 8, loc_b, cross1, side)
+    g7 = lax.all_to_all(pair7, "z", 0, 0, tiled=True)
+
+    part, g = pl.pallas_call(
+        mid_kernel,
+        out_shape=(of((rhs, points), F32), of((2, rhs, points), BF16)),
+        in_specs=[VMEM] * 10 + [HBM] * 4, out_specs=(VMEM,) * 2,
         scratch_shapes=[
             pltpu.VMEM((5 * leaves, rhs, pts), BF16),
+            pltpu.VMEM(basis_in.shape, BF16),
             pltpu.VMEM(near_blocks.shape, BF16),
             pltpu.SMEM(near_pattern.shape[::-1], jnp.int32),
             pltpu.SemaphoreType.DMA((leaves,)),
-            pltpu.SemaphoreType.DMA,
+            pltpu.SemaphoreType.DMA((leaves,)),
+            pltpu.SemaphoreType.DMA((2,)),
         ],
-        name="near", compiler_params=PARAMS,
-    )(in_hbm(near_pattern.T), src, core, side, cross4, cross1, in_hbm(near_blocks))
-
-    m5, m6, pair7 = up4(pair5, (8, 16, 24), "y", 8, loc2, cross4, cross1)
-    g7 = lax.all_to_all(pair7, "z", 0, 0, tiled=True)
-
-    part, ghigh, glow = pl.pallas_call(
-        mid_kernel,
-        out_shape=(of((rhs, points), F32), of((rhs, points), BF16), of((rhs, points), BF16)),
-        in_specs=[VMEM] * 12, out_specs=(VMEM,) * 3,
-        name="mid", compiler_params=PARAMS,
-    )(far, coup, tsplit, basis, loc0, loc1, loc2, m3, m4, m5, m6, near)
+        name="mid", compiler_params=pltpu.CompilerParams(vmem_limit_bytes=8 * 1024 * 1024),
+    )(far, coup, tsplit, loc_a, loc_b, m56, core, side, cross4, cross1,
+      in_hbm(src_in), in_hbm(basis_in), in_hbm(near_pattern.T), in_hbm(near_blocks))
 
     product = pl.pallas_call(
         last_kernel,
         out_shape=of((rhs, points), BF16),
-        in_specs=[VMEM] * 7, out_specs=VMEM,
+        in_specs=[VMEM] * 6, out_specs=VMEM,
         scratch_shapes=[pltpu.VMEM((n, rhs, rank), F32) for n in (16, 8, 4)],
         name="last", compiler_params=PARAMS,
-    )(far, coup, tsplit, g7, part, ghigh, glow)
+    )(far, coup, tsplit, g7, part, g)
     return product.T
 
 

time: 49 us -> 48.1 us (0.982)
  waiting for transfers between devices: 10.7 us -> 6.65 us
  starting transfers between devices: 24.3 us -> 26.5 us
  Pallas kernels: 13.6 us -> 14.7 us
    ppermute x9, waiting for transfers between devices: 10.7 us -> 2.93 us  [swap(): lax.ppermute(array, AXES, [(i, i ^ mask) for i in range(device_count())])]
    all_to_all x1, waiting for transfers between devices: 0.01 us -> 3.72 us  [shards(): g7 = lax.all_to_all(pair7, 'z', 0, 0, tiled=True)]
    all_to_all x1, starting transfers between devices: 3.47 us -> 5.31 us  [shards(): g7 = lax.all_to_all(pair7, 'z', 0, 0, tiled=True)]
    pallas_call x5 -> x4, Pallas kernels: 9.33 us -> 10.4 us  [the longest x1 7.02 us: shards(): pl.pallas_call(mid_kernel, out_shape=(of((rhs, points), F32), of((2, rhs,...]
    ppermute x9, starting transfers between devices: 15 us -> 15.7 us  [swap(): lax.ppermute(array, AXES, [(i, i ^ mask) for i in range(device_count())])]
  transfers between devices with their start and end apart: 12 -> 12, of which waited for: 3 -> 3; matrix products, arithmetic and copies ran while one was open for 0% -> 0% of each run, Pallas kernels for 17% -> 20%
where the time goes in v3:
time: 48.1 us; the launch traced here: 47.9 us
  starting transfers between devices  26.5 us (55%)
  Pallas kernels  14.7 us (31%)
  waiting for transfers between devices  6.65 us (14%)
    ppermute x9, starting transfers between devices, swap(): lax.ppermute(array, AXES, [(i, i ^ mask) for i in range(device_count())])  15.7 us
    pallas_call x1, Pallas kernels, shards(): pl.pallas_call(mid_kernel, out_shape=(of((rhs, points), F32), of((2, rhs,...  7.02 us
    ppermute x2, starting transfers between devices, swap_across(): return lax.ppermute(array, AXES, pairs)  5.41 us
    all_to_all x1, starting transfers between devices, shards(): g7 = lax.all_to_all(pair7, 'z', 0, 0, tiled=True)  5.31 us
    all_to_all x1, waiting for transfers between devices, shards(): g7 = lax.all_to_all(pair7, 'z', 0, 0, tiled=True)  3.72 us
    ppermute x9, waiting for transfers between devices, swap(): lax.ppermute(array, AXES, [(i, i ^ mask) for i in range(device_count())])  2.93 us
    pallas_call x1, Pallas kernels, shards(): pl.pallas_call(last_kernel, out_shape=of((rhs, points), BF16), in_specs=[...  2.24 us
    pallas_call x2, Pallas kernels, up4(): pl.pallas_call(lambda *refs: up4_kernel(copies, axis, refs), out_shape=(m...  1.74 us
  transfers between devices with their start and end apart: 12, of which 3 were waited for; matrix products, arithmetic and copies ran while one was open for 0% of the time, Pallas kernels for 20%

profile of v3, /device:TPU:1, one launch (start us, length us, event | category | flops | bytes accessed | tf_op | source)
XLA Modules:
  0.0 47.9 jit_solution(6597719596599492442)
XLA Ops:
  0.0 1.7 %leaf.1 = (bf16[64,2048]{1,0:T(8,128)(2,1)S(1)}, f32[3,64,64]{2,1,0:T(8,128)S(1)}, s32[3,4092]{1,0:T(4,128)S(1)}, bf16[4,64,64]{2,1,0:T(8,128)(2,1)S(1)}, f32[8,...) custom-call(bf16[64,2048]{1,0:T(8,128)(2,1)} %bitcast.5, bf16[8,64,256]{2,1,0:T(8,128)(2,1)} %bitcast.7, ...), custom_call_target="tpu_custom_call" | custom-call | tf_op jit(solution)/shard_map/leaf/pallas_call | solution.py:292
  1.7 2.1 %collective-permute-start = (f32[64,128]{1,0:T(8,128)S(1)}, f32[64,128]{1,0:T(8,128)S(1)}, u32[]{:S(2)}, u32[]{:S(2)}) collective-permute-start(f32[64,128]{1,0:T(8,128)S(1)} %get-tuple-element.25.refs_0_), channel_id=1, source_target_pairs={{0,1},{1,0},{2,3},{3,2},{4,5},{5,4},{6,7},{7,6},{8,9},{9,8},{10,11... | collective-permute-start | bytes 98312 | tf_op jit(solution)/shard_map/ppermute | solution.py:57
  3.8 2.5 %collective-permute-start.1 = (f32[64,128]{1,0:T(8,128)S(1)}, f32[64,128]{1,0:T(8,128)S(1)}, u32[]{:S(2)}, u32[]{:S(2)}) collective-permute-start(f32[64,128]{1,0:T(8,128)S(1)} %get-tuple-element.25.refs_0_), channel_id=1, source_target_pairs={{0,2},{1,3},{2,0},{3,1},{4,6},{5,7},{6,4},{7,5},{8,10},{9,11},{10,... | collective-permute-start | bytes 98312 | tf_op jit(solution)/shard_map/ppermute | solution.py:57
  6.3 0.0 collective-permute-start.2
  6.3 0.5 %low.1.refs_5_.loc_a = f32[4,64,64]{2,1,0:T(8,128)S(1)} custom-call(s32[3,4092]{1,0:T(4,128)S(1)} %get-tuple-element.22.far, f32[3,64,64]{2,1,0:T(8,128)S(1)} %get-tuple-element.23.coupling, f32[4,64,64]{2,1,0:T(8,128)S(1)} %get-tuple-element.26.m1), custom_call_target="tpu_custom_call" | custom-call | tf_op jit(solution)/shard_map/low/pallas_call | solution.py:322
  6.9 2.9 %collective-permute-start.4 = (bf16[64,2048]{1,0:T(8,128)(2,1)S(1)}, bf16[64,2048]{1,0:T(8,128)(2,1)S(1)}, u32[]{:S(2)}, u32[]{:S(2)}) collective-permute-start(bf16[64,2048]{1,0:T(8,128)(2,1)S(1)} %get-tuple-element.34), channel_id=1, source_target_pairs={{0,252},{1,253},{2,254},{3,255},{4,8},{5,9},{6,10},{7,11},{8,4},{9... | collective-permute-start | bytes 786440 | tf_op jit(solution)/shard_map/ppermute | solution.py:67
  9.8 5.7 %collective-permute-start.5 = (bf16[64,2048]{1,0:T(8,128)(2,1)S(1)}, bf16[64,2048]{1,0:T(8,128)(2,1)S(1)}, u32[]{:S(2)}, u32[]{:S(2)}) collective-permute-start(bf16[64,2048]{1,0:T(8,128)(2,1)S(1)} %get-tuple-element.34), channel_id=1, source_target_pairs={{0,4},{1,5},{2,6},{3,7},{4,0},{5,1},{6,2},{7,3},{8,12},{9,13},{10,... | collective-permute-start | bytes 786440 | tf_op jit(solution)/shard_map/ppermute | solution.py:57
  15.5 0.0 collective-permute-done.refs_1_
  15.5 0.0 collective-permute-done.1.refs_2_
  15.5 0.0 collective-permute-done.2.refs_3_
  15.5 0.5 %up4.2 = (f32[12,64,64]{2,1,0:T(8,128)S(1)}, f32[64,128]{1,0:T(8,128)S(1)}) custom-call(f32[64,128]{1,0:T(8,128)S(1)} %get-tuple-element.25.refs_0_, f32[64,128]{1,0:T(8,128)S(1)} %collective-permute-done.refs_1_, f32[64,128]{1,0:T(8,128)S(1)} %collective-permute-done.1.refs_2_, f32[64,128]{1,0:T(8,128)S(1)} %collective-permute-done.2.refs_3_, ...), custom_call_target="tpu_custom_call" | custom-call | tf_op jit(solution)/shard_map/up4/pallas_call | solution.py:306
  16.1 2.5 %collective-permute-start.9 = (bf16[64,2048]{1,0:T(8,128)(2,1)S(1)}, bf16[64,2048]{1,0:T(8,128)(2,1)S(1)}, u32[]{:S(2)}, u32[]{:S(2)}) collective-permute-start(bf16[64,2048]{1,0:T(8,128)(2,1)S(1)} %get-tuple-element.34), channel_id=1, source_target_pairs={{0,255},{1,2},{2,1},{3,4},{4,3},{5,6},{6,5},{7,8},{8,7},{9,10},{10... | collective-permute-start | bytes 786440 | tf_op jit(solution)/shard_map/ppermute | solution.py:67
  18.5 0.0 collective-permute-start.10
  18.5 1.4 %collective-permute-start.3 = (f32[64,128]{1,0:T(8,128)S(1)}, f32[64,128]{1,0:T(8,128)S(1)}, u32[]{:S(2)}, u32[]{:S(2)}) collective-permute-start(f32[64,128]{1,0:T(8,128)S(1)} %get-tuple-element.27.refs_0_), channel_id=1, source_target_pairs={{0,4},{1,5},{2,6},{3,7},{4,0},{5,1},{6,2},{7,3},{8,12},{9,13},{10,... | collective-permute-start | bytes 98312 | tf_op jit(solution)/shard_map/ppermute | solution.py:57
  20.0 0.9 %collective-permute-done.3.refs_1_ = f32[64,128]{1,0:T(8,128)S(1)} collective-permute-done((f32[64,128]{1,0:T(8,128)S(1)}, f32[64,128]{1,0:T(8,128)S(1)}, u32[]{:S(2)}, u32[]{:S(2)}) %collective-permute-start.3) | collective-permute-done | bytes 32800 | tf_op jit(solution)/shard_map/ppermute | solution.py:57
  20.8 0.0 collective-permute-done.4.refs_3_.cross4
  20.8 0.0 collective-permute-done.5.refs_4_.core
  20.8 0.3 up2.1
  21.2 0.3 collective-permute-start.6
  21.5 0.0 collective-permute-start.7
  21.5 3.6 %collective-permute-start.8 = (f32[64,128]{1,0:T(8,128)S(1)}, f32[64,128]{1,0:T(8,128)S(1)}, u32[]{:S(2)}, u32[]{:S(2)}) collective-permute-start(f32[64,128]{1,0:T(8,128)S(1)} %get-tuple-element.30.behind.refs_0_), channel_id=1, source_target_pairs={{0,24},{1,25},{2,26},{3,27},{4,28},{5,29},{6,30},{7,31},{8,16},{9,... | collective-permute-start | bytes 98312 | tf_op jit(solution)/shard_map/ppermute | solution.py:57
  25.1 1.1 %low2.1.refs_5_.loc_b = f32[12,64,64]{2,1,0:T(8,128)S(1)} custom-call(s32[3,4092]{1,0:T(4,128)S(1)} %get-tuple-element.22.far, f32[3,64,64]{2,1,0:T(8,128)S(1)} %get-tuple-element.23.coupling, f32[8,64,64]{2,1,0:T(8,128)S(1)} %get-tuple-element.31.m0, f32[12,64,64]{2,1,0:T(8,128)S(1)} %get-tuple-element.32.m23, f32[4,64,64]{2,1,0:T(8,128)S(1)} %get-tuple-element.33.m4, ...), custom_call_target="tpu_custom_call" | custom-call | tf_op jit(solution)/shard_map/low2/pallas_call | solution.py:332
  26.2 0.0 collective-permute-done.6.refs_1_
  26.2 0.0 collective-permute-done.7.refs_2_
  26.3 2.0 %collective-permute-done.8.refs_3_ = f32[64,128]{1,0:T(8,128)S(1)} collective-permute-done((f32[64,128]{1,0:T(8,128)S(1)}, f32[64,128]{1,0:T(8,128)S(1)}, u32[]{:S(2)}, u32[]{:S(2)}) %collective-permute-start.8) | collective-permute-done | bytes 32800 | tf_op jit(solution)/shard_map/ppermute | solution.py:57
  28.3 0.0 collective-permute-done.9.refs_6_.cross1
  28.3 0.0 collective-permute-done.10.refs_7_.side
  28.3 1.3 %up4.3 = (f32[12,64,64]{2,1,0:T(8,128)S(1)}, f32[8,64,128]{2,1,0:T(8,128)}) custom-call(f32[64,128]{1,0:T(8,128)S(1)} %get-tuple-element.30.behind.refs_0_, f32[64,128]{1,0:T(8,128)S(1)} %collective-permute-done.6.refs_1_, f32[64,128]{1,0:T(8,128)S(1)} %collective-permute-done.7.refs_2_, f32[64,128]{1,0:T(8,128)S(1)} %collective-permute-done.8.refs_3_, ...), custom_call_target="tpu_custom_call" | custom-call | tf_op jit(solution)/shard_map/up4/pallas_call | solution.py:306
  29.6 5.3 %all-to-all-start = ((f32[8,64,128]{2,1,0:T(8,128)}), f32[8,64,128]{2,1,0:T(8,128)S(1)}, u32[]{:S(2)}, u32[]{:S(2)}) async-start(f32[8,64,128]{2,1,0:T(8,128)} %get-tuple-element.35), calls=%async_computation | async-start | bytes 524288 | tf_op jit(solution)/shard_map/all_to_all | solution.py:338
  34.9 7.0 %mid.1 = (f32[64,2048]{1,0:T(8,128)S(1)}, bf16[2,64,2048]{2,1,0:T(8,128)(2,1)S(1)}) custom-call(s32[3,4092]{1,0:T(4,128)S(1)} %get-tuple-element.22.far, f32[3,64,64]{2,1,0:T(8,128)S(1)} %get-tuple-element.23.coupling, bf16[4,64,64]{2,1,0:T(8,128)(2,1)S(1)} %get-tuple-element.24.refs_4_.refs_2_.tsplit, f32[4,64,64]{2,1,0:T(8,128)S(1)} %low.1.refs_5_.loc_a, ...), custom_call_target="tpu_custom_call" | custom-call | tf_op jit(solution)/shard_map/mid/pallas_call | solution.py:340
  41.9 3.7 %all-to-all-done.g7 = f32[8,64,128]{2,1,0:T(8,128)S(1)} async-done(((f32[8,64,128]{2,1,0:T(8,128)}), f32[8,64,128]{2,1,0:T(8,128)S(1)}, u32[]{:S(2)}, u32[]{:S(2)}) %all-to-all-start) | async-done | bytes 262176 | tf_op jit(solution)/shard_map/all_to_all | solution.py:338
  45.6 2.2 %last.1 = bf16[64,2048]{1,0:T(8,128)(2,1)} custom-call(s32[3,4092]{1,0:T(4,128)S(1)} %get-tuple-element.22.far, f32[3,64,64]{2,1,0:T(8,128)S(1)} %get-tuple-element.23.coupling, bf16[4,64,64]{2,1,0:T(8,128)(2,1)S(1)} %get-tuple-element.24.refs_4_.refs_2_.tsplit, f32[8,64,128]{2,1,0:T(8,128)S(1)} %all-to-all-done.g7, f32[64,2048]{1,0:T(8,128)S(1)} %get-tuple-element.37.part, ...), custom_call_target="tpu_custom_call" | custom-call | tf_op jit(solution)/shard_map/last/pallas_call | solution.py:357
Async XLA Ops:
  1.7 13.8 %collective-permute-start = (f32[64,128]{1,0:T(8,128)S(1)}, f32[64,128]{1,0:T(8,128)S(1)}, u32[]{:S(2)}, u32[]{:S(2)}) collective-permute-start(f32[64,128]{1,0:T(8,128)S(1)} %get-tuple-element.25.refs_0_), channel_id=1, source_target_pairs={{0,1},{1,0},{2,3},{3,2},{4,5},{5,4},{6,7},{7,6},{8,9},{9,8},{10,11... | collective-permute-start | bytes 98312 | tf_op jit(solution)/shard_map/ppermute | solution.py:57
  3.8 11.7 %collective-permute-start.1 = (f32[64,128]{1,0:T(8,128)S(1)}, f32[64,128]{1,0:T(8,128)S(1)}, u32[]{:S(2)}, u32[]{:S(2)}) collective-permute-start(f32[64,128]{1,0:T(8,128)S(1)} %get-tuple-element.25.refs_0_), channel_id=1, source_target_pairs={{0,2},{1,3},{2,0},{3,1},{4,6},{5,7},{6,4},{7,5},{8,10},{9,11},{10,... | collective-permute-start | bytes 98312 | tf_op jit(solution)/shard_map/ppermute | solution.py:57
  6.3 9.2 %collective-permute-start.2 = (f32[64,128]{1,0:T(8,128)S(1)}, f32[64,128]{1,0:T(8,128)S(1)}, u32[]{:S(2)}, u32[]{:S(2)}) collective-permute-start(f32[64,128]{1,0:T(8,128)S(1)} %get-tuple-element.25.refs_0_), channel_id=1, source_target_pairs={{0,3},{1,2},{2,1},{3,0},{4,7},{5,6},{6,5},{7,4},{8,11},{9,10},{10,... | collective-permute-start | bytes 98312 | tf_op jit(solution)/shard_map/ppermute | solution.py:57
  6.9 14.0 %collective-permute-start.4 = (bf16[64,2048]{1,0:T(8,128)(2,1)S(1)}, bf16[64,2048]{1,0:T(8,128)(2,1)S(1)}, u32[]{:S(2)}, u32[]{:S(2)}) collective-permute-start(bf16[64,2048]{1,0:T(8,128)(2,1)S(1)} %get-tuple-element.34), channel_id=1, source_target_pairs={{0,252},{1,253},{2,254},{3,255},{4,8},{5,9},{6,10},{7,11},{8,4},{9... | collective-permute-start | bytes 786440 | tf_op jit(solution)/shard_map/ppermute | solution.py:67
  9.8 11.0 %collective-permute-start.5 = (bf16[64,2048]{1,0:T(8,128)(2,1)S(1)}, bf16[64,2048]{1,0:T(8,128)(2,1)S(1)}, u32[]{:S(2)}, u32[]{:S(2)}) collective-permute-start(bf16[64,2048]{1,0:T(8,128)(2,1)S(1)} %get-tuple-element.34), channel_id=1, source_target_pairs={{0,4},{1,5},{2,6},{3,7},{4,0},{5,1},{6,2},{7,3},{8,12},{9,13},{10,... | collective-permute-start | bytes 786440 | tf_op jit(solution)/shard_map/ppermute | solution.py:57
  16.1 12.2 %collective-permute-start.9 = (bf16[64,2048]{1,0:T(8,128)(2,1)S(1)}, bf16[64,2048]{1,0:T(8,128)(2,1)S(1)}, u32[]{:S(2)}, u32[]{:S(2)}) collective-permute-start(bf16[64,2048]{1,0:T(8,128)(2,1)S(1)} %get-tuple-element.34), channel_id=1, source_target_pairs={{0,255},{1,2},{2,1},{3,4},{4,3},{5,6},{6,5},{7,8},{8,7},{9,10},{10... | collective-permute-start | bytes 786440 | tf_op jit(solution)/shard_map/ppermute | solution.py:67
  18.5 9.8 %collective-permute-start.10 = (bf16[64,2048]{1,0:T(8,128)(2,1)S(1)}, bf16[64,2048]{1,0:T(8,128)(2,1)S(1)}, u32[]{:S(2)}, u32[]{:S(2)}) collective-permute-start(bf16[64,2048]{1,0:T(8,128)(2,1)S(1)} %get-tuple-element.34), channel_id=1, source_target_pairs={{0,1},{1,0},{2,3},{3,2},{4,5},{5,4},{6,7},{7,6},{8,9},{9,8},{10,11... | collective-permute-start | bytes 786440 | tf_op jit(solution)/shard_map/ppermute | solution.py:57
  18.5 2.3 %collective-permute-start.3 = (f32[64,128]{1,0:T(8,128)S(1)}, f32[64,128]{1,0:T(8,128)S(1)}, u32[]{:S(2)}, u32[]{:S(2)}) collective-permute-start(f32[64,128]{1,0:T(8,128)S(1)} %get-tuple-element.27.refs_0_), channel_id=1, source_target_pairs={{0,4},{1,5},{2,6},{3,7},{4,0},{5,1},{6,2},{7,3},{8,12},{9,13},{10,... | collective-permute-start | bytes 98312 | tf_op jit(solution)/shard_map/ppermute | solution.py:57
  21.2 5.1 %collective-permute-start.6 = (f32[64,128]{1,0:T(8,128)S(1)}, f32[64,128]{1,0:T(8,128)S(1)}, u32[]{:S(2)}, u32[]{:S(2)}) collective-permute-start(f32[64,128]{1,0:T(8,128)S(1)} %get-tuple-element.30.behind.refs_0_), channel_id=1, source_target_pairs={{0,8},{1,9},{2,10},{3,11},{4,12},{5,13},{6,14},{7,15},{8,0},{9,1},... | collective-permute-start | bytes 98312 | tf_op jit(solution)/shard_map/ppermute | solution.py:57
  21.5 4.8 %collective-permute-start.7 = (f32[64,128]{1,0:T(8,128)S(1)}, f32[64,128]{1,0:T(8,128)S(1)}, u32[]{:S(2)}, u32[]{:S(2)}) collective-permute-start(f32[64,128]{1,0:T(8,128)S(1)} %get-tuple-element.30.behind.refs_0_), channel_id=1, source_target_pairs={{0,16},{1,17},{2,18},{3,19},{4,20},{5,21},{6,22},{7,23},{8,24},{9,... | collective-permute-start | bytes 98312 | tf_op jit(solution)/shard_map/ppermute | solution.py:57
  21.5 6.8 %collective-permute-start.8 = (f32[64,128]{1,0:T(8,128)S(1)}, f32[64,128]{1,0:T(8,128)S(1)}, u32[]{:S(2)}, u32[]{:S(2)}) collective-permute-start(f32[64,128]{1,0:T(8,128)S(1)} %get-tuple-element.30.behind.refs_0_), channel_id=1, source_target_pairs={{0,24},{1,25},{2,26},{3,27},{4,28},{5,29},{6,30},{7,31},{8,16},{9,... | collective-permute-start | bytes 98312 | tf_op jit(solution)/shard_map/ppermute | solution.py:57
  29.6 16.1 %all-to-all-start = ((f32[8,64,128]{2,1,0:T(8,128)}), f32[8,64,128]{2,1,0:T(8,128)S(1)}, u32[]{:S(2)}, u32[]{:S(2)}) async-start(f32[8,64,128]{2,1,0:T(8,128)} %get-tuple-element.35), calls=%async_computation | async-start | bytes 524288 | tf_op jit(solution)/shard_map/all_to_all | solution.py:338

commit v4 on v3

--- a/solution.py
+++ b/solution.py
@@ -65,6 +65,12 @@
     n = device_count()
     pairs = [(i, (i + (step if i & step else n - step)) % n) for i in range(n)]
     return lax.ppermute(array, AXES, pairs)
+
+
+def shift(array):
+    n, span = device_count(), lax.axis_size("x")
+    step = lambda i: -1 if i // span % 2 else 1
+    return lax.ppermute(array, AXES, [(i, i // span * span + (i + step(i)) % span) for i in range(n)])
 
 
 def leaf_kernel(src_in, basis_in, transfer_in, coupling_in, far_in, src, coupling, far, tsplit, m0, m1, pair2, basis, raw, sems):
@@ -126,14 +132,26 @@
 
 
 def up2_kernel(axis, refs):
-    own, p1, tsplit = refs[:3]
-    a, pair, ordered = refs[-3:]
+    own, p1, tsplit, src, core, cross4 = refs[:6]
+    a, pair, both, ordered = refs[-4:]
     t = transfers(tsplit)
     here = lax.axis_index(axis)
     for i, ref in enumerate((own, p1)):
         ordered[here ^ i] = ref[...]
     clusters([ordered[i] for i in range(2)], a)
     pair[...] = pair_of(lift(a[0], a[1], t), lift(a[2], a[3], t))
+    c, x = lax.axis_index("c"), lax.axis_index("x")
+    end = x == jnp.where(c == 0, lax.axis_size("x") - 1, 0)
+
+    @pl.when(end)
+    def _():
+        both[0] = cross4[...]
+        both[1] = src[...]
+
+    @pl.when(jnp.logical_not(end))
+    def _():
+        both[0] = src[...]
+        both[1] = core[...]
 
 
 def start_of(level):
@@ -188,14 +206,11 @@
     loc_b[3] = local(far, c, 4, d >> 1, m4, 4)
 
 
-def mid_kernel(far, coupling, tsplit, loc_a, loc_b, m56, core, side, cross4, cross1,
-               src_in, basis_in, pattern_in, blocks_in, part, g, held, basis, blocks, pattern, sems, own_sems, pair_sems):
+def mid_kernel(far, coupling, tsplit, loc_a, loc_b, m56, core, cross4, shifted, other,
+               src_in, basis_in, pattern_in, blocks_in, part, g, held, own, basis, blocks, pattern, sems, pair_sems):
     leaves, slots, pts = blocks_in.shape[:3]
-    own_copies = [
-        pltpu.make_async_copy(src_in.at[:, i * pts : (i + 1) * pts], held.at[i], own_sems.at[i]) for i in range(leaves)
-    ]
-    for copy in own_copies:
-        copy.start()
+    own_copy = pltpu.make_async_copy(src_in, own, pair_sems.at[2])
+    own_copy.start()
     basis_copy = pltpu.make_async_copy(basis_in, basis, pair_sems.at[0])
     basis_copy.start()
     pattern_copy = pltpu.make_async_copy(pattern_in, pattern, pair_sems.at[1])
@@ -230,14 +245,15 @@
             below.append((locs[first + i] + both[:64], both[64:]))
         parents = below
 
-    for n, ref in enumerate((core, side, cross4, cross1)):
+    for n, ref in enumerate((core, cross4, shifted.at[0], other)):
         for i in range(leaves):
             held[(n + 1) * leaves + i] = ref[:, i * pts : (i + 1) * pts]
-    for copy in own_copies:
-        copy.wait()
+    own_copy.wait()
+    for i in range(leaves):
+        held[i] = own[:, i * pts : (i + 1) * pts]
     basis_copy.wait()
     pattern_copy.wait()
-    others = [d, d ^ 4, d ^ 1, across(d, 4, device_count())]
+    others = [d, d ^ 4, across(d, 4, device_count()), d + jnp.where(lax.axis_index("c") == 0, -1, 1)]
     for i, both in enumerate(parents):
         at = slice(i * pts, (i + 1) * pts)
         high, low = split(jnp.concatenate(both, 0))
@@ -309,33 +325,29 @@
             scratch_shapes=[pltpu.VMEM((4,) + pair.shape, F32)], name="up4", compiler_params=PARAMS,
         )(own, *got, tsplit, *behind)
 
-    def up2(own, mask, axis, *behind):
+    def up2(own, mask, axis, *sources):
         return pl.pallas_call(
             lambda *refs: up2_kernel(axis, refs),
-            out_shape=(mat(4), pair), in_specs=[VMEM] * (3 + len(behind)), out_specs=(VMEM,) * 2,
+            out_shape=(mat(4), pair, of((2,) + src_in.shape, BF16)), in_specs=[VMEM] * 6, out_specs=(VMEM,) * 3,
             scratch_shapes=[pltpu.VMEM((2,) + pair.shape, F32)], name="up2", compiler_params=PARAMS,
-        )(own, swap(own, mask), tsplit, *behind)
-
-    def later(array, other):
-        return lax.optimization_barrier((array, other))[0]
+        )(own, swap(own, mask), tsplit, *sources)
 
     loc_a = pl.pallas_call(
         low_kernel, out_shape=mat(4), in_specs=[VMEM] * 3, out_specs=VMEM,
         name="low", compiler_params=PARAMS,
     )(far, coup, m1)
-    s2 = later(src, loc_a)
-    core, cross4 = swap(s2, 4), swap_across(s2, 4)
+    core, cross4 = swap(src, 4), swap_across(src, 4)
     m23, pair4 = up4(pair2, (1, 2, 3), "x", 0, loc_a)
-    s3 = later(src, pair4)
-    side, cross1 = swap(s3, 1), swap_across(s3, 1)
-    m4, pair5 = up2(pair4, 4, "c", cross4, core)
+    m4, pair5, both = up2(pair4, 4, "c", src, core, cross4)
     loc_b = pl.pallas_call(
         low2_kernel, out_shape=mat(12), in_specs=[VMEM] * 6, out_specs=VMEM,
         name="low2", compiler_params=PARAMS,
     )(far, coup, m0, m23, m4, pair5)
 
-    m56, pair7 = up4(pair5, (8, 16, 24), "y", 8, loc_b, cross1, side)
+    shifted = shift(both)
+    m56, pair7 = up4(pair5, (8, 16, 24), "y", 8, loc_b)
     g7 = lax.all_to_all(pair7, "z", 0, 0, tiled=True)
+    other = swap(shifted[1], 4)
 
     part, g = pl.pallas_call(
         mid_kernel,
@@ -343,15 +355,15 @@
         in_specs=[VMEM] * 10 + [HBM] * 4, out_specs=(VMEM,) * 2,
         scratch_shapes=[
             pltpu.VMEM((5 * leaves, rhs, pts), BF16),
+            pltpu.VMEM(src_in.shape, BF16),
             pltpu.VMEM(basis_in.shape, BF16),
             pltpu.VMEM(near_blocks.shape, BF16),
             pltpu.SMEM(near_pattern.shape[::-1], jnp.int32),
             pltpu.SemaphoreType.DMA((leaves,)),
-            pltpu.SemaphoreType.DMA((leaves,)),
-            pltpu.SemaphoreType.DMA((2,)),
+            pltpu.SemaphoreType.DMA((3,)),
         ],
         name="mid", compiler_params=pltpu.CompilerParams(vmem_limit_bytes=8 * 1024 * 1024),
-    )(far, coup, tsplit, loc_a, loc_b, m56, core, side, cross4, cross1,
+    )(far, coup, tsplit, loc_a, loc_b, m56, core, cross4, shifted, other,
       in_hbm(src_in), in_hbm(basis_in), in_hbm(near_pattern.T), in_hbm(near_blocks))
 
     product = pl.pallas_call(

time: 48.1 us -> 45.9 us (0.954)
  starting transfers between devices: 26.5 us -> 22.7 us
  waiting for transfers between devices: 6.65 us -> 8.76 us
  Pallas kernels: 14.7 us -> 14 us
    ppermute x9, waiting for transfers between devices: 2.93 us -> 6.23 us  [swap(): lax.ppermute(array, AXES, [(i, i ^ mask) for i in range(device_count())])]
    ppermute x2 -> x1, starting transfers between devices: 5.41 us -> 2.78 us  [swap_across(): return lax.ppermute(array, AXES, pairs)]
    all_to_all x1, starting transfers between devices: 5.31 us -> 3.41 us  [shards(): g7 = lax.all_to_all(pair7, 'z', 0, 0, tiled=True)]
    all_to_all x1, waiting for transfers between devices: 3.72 us -> 2.53 us  [shards(): g7 = lax.all_to_all(pair7, 'z', 0, 0, tiled=True)]
    ppermute x0 -> x1, starting transfers between devices: none -> 1.05 us  [shift(): lax.ppermute(array, AXES, [(i, i // span * span + (i + step(i)) % span) f...]
    pallas_call x1, Pallas kernels: 7.02 us -> 6.4 us  [shards(): pl.pallas_call(mid_kernel, out_shape=(of((rhs, points), F32), of((2, rhs,...]
  transfers between devices with their start and end apart: 12 -> 12, of which waited for: 3 -> 7; matrix products, arithmetic and copies ran while one was open for 0% -> 0% of each run, Pallas kernels for 20% -> 21%
where the time goes in v4:
time: 45.9 us; the launch traced here: 45.7 us
  starting transfers between devices  22.7 us (49%)
  Pallas kernels  14 us (31%)
  waiting for transfers between devices  8.76 us (19%)
    ppermute x9, starting transfers between devices, swap(): lax.ppermute(array, AXES, [(i, i ^ mask) for i in range(device_count())])  15.5 us
    pallas_call x1, Pallas kernels, shards(): pl.pallas_call(mid_kernel, out_shape=(of((rhs, points), F32), of((2, rhs,...  6.4 us
    ppermute x9, waiting for transfers between devices, swap(): lax.ppermute(array, AXES, [(i, i ^ mask) for i in range(device_count())])  6.23 us
    all_to_all x1, starting transfers between devices, shards(): g7 = lax.all_to_all(pair7, 'z', 0, 0, tiled=True)  3.41 us
    ppermute x1, starting transfers between devices, swap_across(): return lax.ppermute(array, AXES, pairs)  2.78 us
    all_to_all x1, waiting for transfers between devices, shards(): g7 = lax.all_to_all(pair7, 'z', 0, 0, tiled=True)  2.53 us
    pallas_call x1, Pallas kernels, shards(): pl.pallas_call(last_kernel, out_shape=of((rhs, points), BF16), in_specs=[...  2.23 us
    pallas_call x2, Pallas kernels, up4(): pl.pallas_call(lambda *refs: up4_kernel(copies, axis, refs), out_shape=(m...  1.74 us
  transfers between devices with their start and end apart: 12, of which 7 were waited for; matrix products, arithmetic and copies ran while one was open for 0% of the time, Pallas kernels for 21%

profile of v4, /device:TPU:1, one launch (start us, length us, event | category | flops | bytes accessed | tf_op | source)
XLA Modules:
  0.0 45.7 jit_solution(13405780724516900579)
XLA Ops:
  0.0 1.7 %leaf.1 = (bf16[64,2048]{1,0:T(8,128)(2,1)S(1)}, f32[3,64,64]{2,1,0:T(8,128)S(1)}, s32[3,4092]{1,0:T(4,128)S(1)}, bf16[4,64,64]{2,1,0:T(8,128)(2,1)S(1)}, f32[8,...) custom-call(bf16[64,2048]{1,0:T(8,128)(2,1)} %bitcast.7, bf16[8,64,256]{2,1,0:T(8,128)(2,1)} %bitcast.9, ...), custom_call_target="tpu_custom_call" | custom-call | tf_op jit(solution)/shard_map/leaf/pallas_call | solution.py:308
  1.7 2.8 %collective-permute-start.5 = (bf16[64,2048]{1,0:T(8,128)(2,1)S(1)}, bf16[64,2048]{1,0:T(8,128)(2,1)S(1)}, u32[]{:S(2)}, u32[]{:S(2)}) collective-permute-start(bf16[64,2048]{1,0:T(8,128)(2,1)S(1)} %get-tuple-element.27.refs_3_), channel_id=1, source_target_pairs={{0,252},{1,253},{2,254},{3,255},{4,8},{5,9},{6,10},{7,11},{8,4},{9... | collective-permute-start | bytes 786440 | tf_op jit(solution)/shard_map/ppermute | solution.py:67
  4.5 6.6 %collective-permute-start.4 = (bf16[64,2048]{1,0:T(8,128)(2,1)S(1)}, bf16[64,2048]{1,0:T(8,128)(2,1)S(1)}, u32[]{:S(2)}, u32[]{:S(2)}) collective-permute-start(bf16[64,2048]{1,0:T(8,128)(2,1)S(1)} %get-tuple-element.27.refs_3_), channel_id=1, source_target_pairs={{0,4},{1,5},{2,6},{3,7},{4,0},{5,1},{6,2},{7,3},{8,12},{9,13},{10,... | collective-permute-start | bytes 786440 | tf_op jit(solution)/shard_map/ppermute | solution.py:57
  11.1 2.5 %collective-permute-start.2 = (f32[64,128]{1,0:T(8,128)S(1)}, f32[64,128]{1,0:T(8,128)S(1)}, u32[]{:S(2)}, u32[]{:S(2)}) collective-permute-start(f32[64,128]{1,0:T(8,128)S(1)} %get-tuple-element.24.refs_0_), channel_id=1, source_target_pairs={{0,3},{1,2},{2,1},{3,0},{4,7},{5,6},{6,5},{7,4},{8,11},{9,10},{10,... | collective-permute-start | bytes 98312 | tf_op jit(solution)/shard_map/ppermute | solution.py:57
  13.5 0.5 %collective-permute-start.1 = (f32[64,128]{1,0:T(8,128)S(1)}, f32[64,128]{1,0:T(8,128)S(1)}, u32[]{:S(2)}, u32[]{:S(2)}) collective-permute-start(f32[64,128]{1,0:T(8,128)S(1)} %get-tuple-element.24.refs_0_), channel_id=1, source_target_pairs={{0,2},{1,3},{2,0},{3,1},{4,6},{5,7},{6,4},{7,5},{8,10},{9,11},{10,... | collective-permute-start | bytes 98312 | tf_op jit(solution)/shard_map/ppermute | solution.py:57
  14.0 0.3 collective-permute-start
  14.3 0.5 %low.1.refs_5_.loc_a = f32[4,64,64]{2,1,0:T(8,128)S(1)} custom-call(s32[3,4092]{1,0:T(4,128)S(1)} %get-tuple-element.21.far, f32[3,64,64]{2,1,0:T(8,128)S(1)} %get-tuple-element.22.coupling, f32[4,64,64]{2,1,0:T(8,128)S(1)} %get-tuple-element.25.m1), custom_call_target="tpu_custom_call" | custom-call | tf_op jit(solution)/shard_map/low/pallas_call | solution.py:335
  14.8 0.2 collective-permute-done.2.refs_3_
  15.0 2.8 %collective-permute-done.1.refs_2_ = f32[64,128]{1,0:T(8,128)S(1)} collective-permute-done((f32[64,128]{1,0:T(8,128)S(1)}, f32[64,128]{1,0:T(8,128)S(1)}, u32[]{:S(2)}, u32[]{:S(2)}) %collective-permute-start.1) | collective-permute-done | bytes 32800 | tf_op jit(solution)/shard_map/ppermute | solution.py:57
  17.8 0.0 collective-permute-done.refs_1_
  17.8 0.5 %up4.2 = (f32[12,64,64]{2,1,0:T(8,128)S(1)}, f32[64,128]{1,0:T(8,128)S(1)}) custom-call(f32[64,128]{1,0:T(8,128)S(1)} %get-tuple-element.24.refs_0_, f32[64,128]{1,0:T(8,128)S(1)} %collective-permute-done.refs_1_, f32[64,128]{1,0:T(8,128)S(1)} %collective-permute-done.1.refs_2_, f32[64,128]{1,0:T(8,128)S(1)} %collective-permute-done.2.refs_3_, ...), custom_call_target="tpu_custom_call" | custom-call | tf_op jit(solution)/shard_map/up4/pallas_call | solution.py:322
  18.3 1.7 %collective-permute-start.3 = (f32[64,128]{1,0:T(8,128)S(1)}, f32[64,128]{1,0:T(8,128)S(1)}, u32[]{:S(2)}, u32[]{:S(2)}) collective-permute-start(f32[64,128]{1,0:T(8,128)S(1)} %get-tuple-element.26.refs_0_), channel_id=1, source_target_pairs={{0,4},{1,5},{2,6},{3,7},{4,0},{5,1},{6,2},{7,3},{8,12},{9,13},{10,... | collective-permute-start | bytes 98312 | tf_op jit(solution)/shard_map/ppermute | solution.py:57
  20.0 0.9 %collective-permute-done.3.refs_1_ = f32[64,128]{1,0:T(8,128)S(1)} collective-permute-done((f32[64,128]{1,0:T(8,128)S(1)}, f32[64,128]{1,0:T(8,128)S(1)}, u32[]{:S(2)}, u32[]{:S(2)}) %collective-permute-start.3) | collective-permute-done | bytes 32800 | tf_op jit(solution)/shard_map/ppermute | solution.py:57
  20.9 0.0 collective-permute-done.5.refs_5_.cross4
  20.9 0.0 collective-permute-done.4.refs_4_.core
  20.9 0.3 up2.1
  21.2 1.1 %collective-permute-start.9 = (bf16[2,64,2048]{2,1,0:T(8,128)(2,1)S(1)}, bf16[2,64,2048]{2,1,0:T(8,128)(2,1)S(1)}, u32[]{:S(2)}, u32[]{:S(2)}) collective-permute-start(bf16[2,64,2048]{2,1,0:T(8,128)(2,1)S(1)} %get-tuple-element.34), channel_id=1, source_target_pairs={{0,1},{1,2},{2,3},{3,0},{4,7},{5,4},{6,5},{7,6},{8,9},{9,10},{10,1... | collective-permute-start | bytes 1572872 | tf_op jit(solution)/shard_map/ppermute | solution.py:73
  22.3 0.0 collective-permute-start.8
  22.3 0.0 collective-permute-start.7
  22.3 3.2 %collective-permute-start.6 = (f32[64,128]{1,0:T(8,128)S(1)}, f32[64,128]{1,0:T(8,128)S(1)}, u32[]{:S(2)}, u32[]{:S(2)}) collective-permute-start(f32[64,128]{1,0:T(8,128)S(1)} %get-tuple-element.28.behind.refs_0_), channel_id=1, source_target_pairs={{0,8},{1,9},{2,10},{3,11},{4,12},{5,13},{6,14},{7,15},{8,0},{9,1},... | collective-permute-start | bytes 98312 | tf_op jit(solution)/shard_map/ppermute | solution.py:57
  25.5 1.1 %low2.1.refs_5_.loc_b = f32[12,64,64]{2,1,0:T(8,128)S(1)} custom-call(s32[3,4092]{1,0:T(4,128)S(1)} %get-tuple-element.21.far, f32[3,64,64]{2,1,0:T(8,128)S(1)} %get-tuple-element.22.coupling, f32[8,64,64]{2,1,0:T(8,128)S(1)} %get-tuple-element.29.m0, f32[12,64,64]{2,1,0:T(8,128)S(1)} %get-tuple-element.30.m23, f32[4,64,64]{2,1,0:T(8,128)S(1)} %get-tuple-element.31.m4, ...), custom_call_target="tpu_custom_call" | custom-call | tf_op jit(solution)/shard_map/low2/pallas_call | solution.py:342
  26.7 0.8 %collective-permute-done.8.refs_3_ = f32[64,128]{1,0:T(8,128)S(1)} collective-permute-done((f32[64,128]{1,0:T(8,128)S(1)}, f32[64,128]{1,0:T(8,128)S(1)}, u32[]{:S(2)}, u32[]{:S(2)}) %collective-permute-start.8) | collective-permute-done | bytes 32800 | tf_op jit(solution)/shard_map/ppermute | solution.py:57
  27.5 0.0 collective-permute-done.7.refs_2_
  27.5 0.4 collective-permute-done.6.refs_1_
  27.9 1.3 %up4.3 = (f32[12,64,64]{2,1,0:T(8,128)S(1)}, f32[8,64,128]{2,1,0:T(8,128)}) custom-call(f32[64,128]{1,0:T(8,128)S(1)} %get-tuple-element.28.behind.refs_0_, f32[64,128]{1,0:T(8,128)S(1)} %collective-permute-done.6.refs_1_, f32[64,128]{1,0:T(8,128)S(1)} %collective-permute-done.7.refs_2_, f32[64,128]{1,0:T(8,128)S(1)} %collective-permute-done.8.refs_3_, ...), custom_call_target="tpu_custom_call" | custom-call | tf_op jit(solution)/shard_map/up4/pallas_call | solution.py:322
  29.2 3.4 %all-to-all-start = ((f32[8,64,128]{2,1,0:T(8,128)}), f32[8,64,128]{2,1,0:T(8,128)S(1)}, u32[]{:S(2)}, u32[]{:S(2)}) async-start(f32[8,64,128]{2,1,0:T(8,128)} %get-tuple-element.32), calls=%async_computation | async-start | bytes 524288 | tf_op jit(solution)/shard_map/all_to_all | solution.py:349
  32.6 0.0 collective-permute-done.9.shifted
  32.6 0.8 %collective-permute-start.10 = (bf16[64,2048]{1,0:T(8,128)(2,1)S(1)}, bf16[64,2048]{1,0:T(8,128)(2,1)S(1)}, u32[]{:S(2)}, u32[]{:S(2)}) collective-permute-start(bf16[64,2048]{1,0:T(8,128)(2,1)S(1)} %slice_bitcast_fusion), channel_id=1, source_target_pairs={{0,4},{1,5},{2,6},{3,7},{4,0},{5,1},{6,2},{7,3},{8,12},{9,13},{10,... | collective-permute-start | bytes 786440 | tf_op jit(solution)/shard_map/ppermute | solution.py:57
  33.4 1.2 %collective-permute-done.10.other = bf16[64,2048]{1,0:T(8,128)(2,1)S(1)} collective-permute-done((bf16[64,2048]{1,0:T(8,128)(2,1)S(1)}, bf16[64,2048]{1,0:T(8,128)(2,1)S(1)}, u32[]{:S(2)}, u32[]{:S(2)}) %collective-permute-start.10) | collective-permute-done | bytes 262176 | tf_op jit(solution)/shard_map/ppermute | solution.py:57
  34.5 6.4 %mid.1 = (f32[64,2048]{1,0:T(8,128)S(1)}, bf16[2,64,2048]{2,1,0:T(8,128)(2,1)S(1)}) custom-call(s32[3,4092]{1,0:T(4,128)S(1)} %get-tuple-element.21.far, f32[3,64,64]{2,1,0:T(8,128)S(1)} %get-tuple-element.22.coupling, bf16[4,64,64]{2,1,0:T(8,128)(2,1)S(1)} %get-tuple-element.23.refs_4_.refs_2_.tsplit, f32[4,64,64]{2,1,0:T(8,128)S(1)} %low.1.refs_5_.loc_a, ...), custom_call_target="tpu_custom_call" | custom-call | tf_op jit(solution)/shard_map/mid/pallas_call | solution.py:352
  40.9 2.5 %all-to-all-done.g7 = f32[8,64,128]{2,1,0:T(8,128)S(1)} async-done(((f32[8,64,128]{2,1,0:T(8,128)}), f32[8,64,128]{2,1,0:T(8,128)S(1)}, u32[]{:S(2)}, u32[]{:S(2)}) %all-to-all-start) | async-done | bytes 262176 | tf_op jit(solution)/shard_map/all_to_all | solution.py:349
  43.5 2.2 %last.1 = bf16[64,2048]{1,0:T(8,128)(2,1)} custom-call(s32[3,4092]{1,0:T(4,128)S(1)} %get-tuple-element.21.far, f32[3,64,64]{2,1,0:T(8,128)S(1)} %get-tuple-element.22.coupling, bf16[4,64,64]{2,1,0:T(8,128)(2,1)S(1)} %get-tuple-element.23.refs_4_.refs_2_.tsplit, f32[8,64,128]{2,1,0:T(8,128)S(1)} %all-to-all-done.g7, f32[64,2048]{1,0:T(8,128)S(1)} %get-tuple-element.35.part, ...), custom_call_target="tpu_custom_call" | custom-call | tf_op jit(solution)/shard_map/last/pallas_call | solution.py:369
  (1 shorter events, 0.0 us)
Async XLA Ops:
  1.7 19.2 %collective-permute-start.5 = (bf16[64,2048]{1,0:T(8,128)(2,1)S(1)}, bf16[64,2048]{1,0:T(8,128)(2,1)S(1)}, u32[]{:S(2)}, u32[]{:S(2)}) collective-permute-start(bf16[64,2048]{1,0:T(8,128)(2,1)S(1)} %get-tuple-element.27.refs_3_), channel_id=1, source_target_pairs={{0,252},{1,253},{2,254},{3,255},{4,8},{5,9},{6,10},{7,11},{8,4},{9... | collective-permute-start | bytes 786440 | tf_op jit(solution)/shard_map/ppermute | solution.py:67
  4.5 16.4 %collective-permute-start.4 = (bf16[64,2048]{1,0:T(8,128)(2,1)S(1)}, bf16[64,2048]{1,0:T(8,128)(2,1)S(1)}, u32[]{:S(2)}, u32[]{:S(2)}) collective-permute-start(bf16[64,2048]{1,0:T(8,128)(2,1)S(1)} %get-tuple-element.27.refs_3_), channel_id=1, source_target_pairs={{0,4},{1,5},{2,6},{3,7},{4,0},{5,1},{6,2},{7,3},{8,12},{9,13},{10,... | collective-permute-start | bytes 786440 | tf_op jit(solution)/shard_map/ppermute | solution.py:57
  11.1 4.0 %collective-permute-start.2 = (f32[64,128]{1,0:T(8,128)S(1)}, f32[64,128]{1,0:T(8,128)S(1)}, u32[]{:S(2)}, u32[]{:S(2)}) collective-permute-start(f32[64,128]{1,0:T(8,128)S(1)} %get-tuple-element.24.refs_0_), channel_id=1, source_target_pairs={{0,3},{1,2},{2,1},{3,0},{4,7},{5,6},{6,5},{7,4},{8,11},{9,10},{10,... | collective-permute-start | bytes 98312 | tf_op jit(solution)/shard_map/ppermute | solution.py:57
  13.5 4.3 %collective-permute-start.1 = (f32[64,128]{1,0:T(8,128)S(1)}, f32[64,128]{1,0:T(8,128)S(1)}, u32[]{:S(2)}, u32[]{:S(2)}) collective-permute-start(f32[64,128]{1,0:T(8,128)S(1)} %get-tuple-element.24.refs_0_), channel_id=1, source_target_pairs={{0,2},{1,3},{2,0},{3,1},{4,6},{5,7},{6,4},{7,5},{8,10},{9,11},{10,... | collective-permute-start | bytes 98312 | tf_op jit(solution)/shard_map/ppermute | solution.py:57
  14.0 3.8 %collective-permute-start = (f32[64,128]{1,0:T(8,128)S(1)}, f32[64,128]{1,0:T(8,128)S(1)}, u32[]{:S(2)}, u32[]{:S(2)}) collective-permute-start(f32[64,128]{1,0:T(8,128)S(1)} %get-tuple-element.24.refs_0_), channel_id=1, source_target_pairs={{0,1},{1,0},{2,3},{3,2},{4,5},{5,4},{6,7},{7,6},{8,9},{9,8},{10,11... | collective-permute-start | bytes 98312 | tf_op jit(solution)/shard_map/ppermute | solution.py:57
  18.3 2.5 %collective-permute-start.3 = (f32[64,128]{1,0:T(8,128)S(1)}, f32[64,128]{1,0:T(8,128)S(1)}, u32[]{:S(2)}, u32[]{:S(2)}) collective-permute-start(f32[64,128]{1,0:T(8,128)S(1)} %get-tuple-element.26.refs_0_), channel_id=1, source_target_pairs={{0,4},{1,5},{2,6},{3,7},{4,0},{5,1},{6,2},{7,3},{8,12},{9,13},{10,... | collective-permute-start | bytes 98312 | tf_op jit(solution)/shard_map/ppermute | solution.py:57
  21.2 11.4 %collective-permute-start.9 = (bf16[2,64,2048]{2,1,0:T(8,128)(2,1)S(1)}, bf16[2,64,2048]{2,1,0:T(8,128)(2,1)S(1)}, u32[]{:S(2)}, u32[]{:S(2)}) collective-permute-start(bf16[2,64,2048]{2,1,0:T(8,128)(2,1)S(1)} %get-tuple-element.34), channel_id=1, source_target_pairs={{0,1},{1,2},{2,3},{3,0},{4,7},{5,4},{6,5},{7,6},{8,9},{9,10},{10,1... | collective-permute-start | bytes 1572872 | tf_op jit(solution)/shard_map/ppermute | solution.py:73
  22.3 5.2 %collective-permute-start.8 = (f32[64,128]{1,0:T(8,128)S(1)}, f32[64,128]{1,0:T(8,128)S(1)}, u32[]{:S(2)}, u32[]{:S(2)}) collective-permute-start(f32[64,128]{1,0:T(8,128)S(1)} %get-tuple-element.28.behind.refs_0_), channel_id=1, source_target_pairs={{0,24},{1,25},{2,26},{3,27},{4,28},{5,29},{6,30},{7,31},{8,16},{9,... | collective-permute-start | bytes 98312 | tf_op jit(solution)/shard_map/ppermute | solution.py:57
  22.3 5.2 %collective-permute-start.7 = (f32[64,128]{1,0:T(8,128)S(1)}, f32[64,128]{1,0:T(8,128)S(1)}, u32[]{:S(2)}, u32[]{:S(2)}) collective-permute-start(f32[64,128]{1,0:T(8,128)S(1)} %get-tuple-element.28.behind.refs_0_), channel_id=1, source_target_pairs={{0,16},{1,17},{2,18},{3,19},{4,20},{5,21},{6,22},{7,23},{8,24},{9,... | collective-permute-start | bytes 98312 | tf_op jit(solution)/shard_map/ppermute | solution.py:57
  22.3 5.6 %collective-permute-start.6 = (f32[64,128]{1,0:T(8,128)S(1)}, f32[64,128]{1,0:T(8,128)S(1)}, u32[]{:S(2)}, u32[]{:S(2)}) collective-permute-start(f32[64,128]{1,0:T(8,128)S(1)} %get-tuple-element.28.behind.refs_0_), channel_id=1, source_target_pairs={{0,8},{1,9},{2,10},{3,11},{4,12},{5,13},{6,14},{7,15},{8,0},{9,1},... | collective-permute-start | bytes 98312 | tf_op jit(solution)/shard_map/ppermute | solution.py:57
  29.2 14.3 %all-to-all-start = ((f32[8,64,128]{2,1,0:T(8,128)}), f32[8,64,128]{2,1,0:T(8,128)S(1)}, u32[]{:S(2)}, u32[]{:S(2)}) async-start(f32[8,64,128]{2,1,0:T(8,128)} %get-tuple-element.32), calls=%async_computation | async-start | bytes 524288 | tf_op jit(solution)/shard_map/all_to_all | solution.py:349
  32.6 1.9 %collective-permute-start.10 = (bf16[64,2048]{1,0:T(8,128)(2,1)S(1)}, bf16[64,2048]{1,0:T(8,128)(2,1)S(1)}, u32[]{:S(2)}, u32[]{:S(2)}) collective-permute-start(bf16[64,2048]{1,0:T(8,128)(2,1)S(1)} %slice_bitcast_fusion), channel_id=1, source_target_pairs={{0,4},{1,5},{2,6},{3,7},{4,0},{5,1},{6,2},{7,3},{8,12},{9,13},{10,... | collective-permute-start | bytes 786440 | tf_op jit(solution)/shard_map/ppermute | solution.py:57

commit v5 on v4

v5 whole, which is shorter than its diff:
```python
import jax
import jax.numpy as jnp
from jax import lax
from jax.experimental import pallas as pl
from jax.experimental.pallas import tpu as pltpu
from jax.sharding import Mesh, PartitionSpec as P

AXES = ("z", "y", "c", "x")
F32 = jnp.float32
BF16 = jnp.bfloat16
NN = (((1,), (0,)), ((), ()))
NT = (((1,), (1,)), ((), ()))
VMEM = pl.BlockSpec(memory_space=pltpu.VMEM)
SMEM = pl.BlockSpec(memory_space=pltpu.SMEM)
HBM = pl.BlockSpec(memory_space=pltpu.HBM)
ORDER = (2, 1, 3)
PARAMS = pltpu.CompilerParams(vmem_limit_bytes=4 * 1024 * 1024)


def in_hbm(array):
    return pltpu.with_memory_space_constraint(array, pltpu.HBM)


def split(a):
    high = a.astype(BF16)
    return high, (a - high.astype(F32)).astype(BF16)


def dot(a, b, dims):
    return lax.dot_general(a, b, dims, preferred_element_type=F32)


def dot3(a, b, dims):
    return dot(a[0], b[0], dims) + (dot(a[0], b[1], dims) + dot(a[1], b[0], dims))


def lift(pairs, tsplit):
    return dot3(split(pairs), (tsplit[0], tsplit[1]), NN)


def child_transfer(tsplit, child):
    at = pl.ds(pl.multiple_of(child * 64, 64), 64)
    return tsplit[0, at], tsplit[1, at]


def paired(values):
    whole = [values[i * 64 : (i + 1) * 64] for i in range(values.shape[0] // 64)]
    return jnp.concatenate([pair_of(whole[i], whole[i + 1]) for i in range(0, len(whole), 2)], axis=0)


def pair_of(first, second):
    return jnp.concatenate([first, second], axis=1)


def device_index():
    z, y, c, x = (lax.axis_index(a) for a in AXES)
    return ((z * lax.axis_size("y") + y) * lax.axis_size("c") + c) * lax.axis_size("x") + x


def device_count():
    count = 1
    for a in AXES:
        count *= lax.axis_size(a)
    return count


def swap(array, mask):
    return lax.ppermute(array, AXES, [(i, i ^ mask) for i in range(device_count())])


def across(device, step, count):
    return (device + jnp.where(device & step, step, count - step)) % count


def swap_across(array, step):
    n = device_count()
    pairs = [(i, (i + (step if i & step else n - step)) % n) for i in range(n)]
    return lax.ppermute(array, AXES, pairs)


def shift(array):
    n, span = device_count(), lax.axis_size("x")
    step = lambda i: -1 if i // span % 2 else 1
    return lax.ppermute(array, AXES, [(i, i // span * span + (i + step(i)) % span) for i in range(n)])


def leaf_kernel(src_in, basis_in, transfer_in, coupling_in, far_in, src, coupling, far, tsplit, m0, m1, pair2, basis, raw, sems):
    copies = [
        pltpu.make_async_copy(a, b, sems.at[i])
        for i, (a, b) in enumerate(
            ((src_in, src), (basis_in, basis), (transfer_in, raw), (coupling_in, coupling), (far_in, far))
        )
    ]
    for copy in copies:
        copy.start()
    for copy in copies[:3]:
        copy.wait()
    for i in range(2):
        tsplit[0, i * 64 : (i + 1) * 64], tsplit[1, i * 64 : (i + 1) * 64] = split(raw[i])
    leaves, _, pts = basis.shape
    low = []
    for i in range(leaves):
        v = dot(src[:, i * pts : (i + 1) * pts], basis[i], NT)
        m0[i] = v
        low.append(v)
    mid = lift(paired(jnp.concatenate(low, axis=0)), tsplit)
    for i in range(leaves // 2):
        m1[i] = mid[i * 64 : (i + 1) * 64]
    pair2[...] = paired(lift(paired(mid), tsplit))
    for copy in copies[3:]:
        copy.wait()


def clusters(pairs, out):
    for i, p in enumerate(pairs):
        out[2 * i] = p[:, :64]
        out[2 * i + 1] = p[:, 64:]


def up4_kernel(copies, axis, refs):
    own, p1, p2, p3, tsplit = refs[:5]
    ab, pair, ordered = refs[-3:]
    here = lax.axis_index(axis)
    for i, ref in zip((0,) + ORDER, (own, p1, p2, p3)):
        ordered[here ^ i] = ref[...]
    clusters([ordered[i] for i in range(4)], ab)
    mid = lift(jnp.concatenate([ordered[i] for i in range(4)], axis=0), tsplit)
    for i in range(4):
        ab[8 + i] = mid[i * 64 : (i + 1) * 64]
    top = paired(lift(paired(mid), tsplit))
    if copies:
        for i in range(copies):
            pair[i] = top
    else:
        pair[...] = top


def up2_kernel(axis, refs):
    own, p1, tsplit, src, cross4, core = refs[:6]
    a, pair, both, ordered = refs[-4:]
    here = lax.axis_index(axis)
    for i, ref in enumerate((own, p1)):
        ordered[here ^ i] = ref[...]
    clusters([ordered[i] for i in range(2)], a)
    pair[...] = paired(lift(jnp.concatenate([ordered[i] for i in range(2)], axis=0), tsplit))
    c, x = lax.axis_index("c"), lax.axis_index("x")
    end = x == jnp.where(c == 0, lax.axis_size("x") - 1, 0)

    @pl.when(end)
    def _():
        both[0] = cross4[...]
        both[1] = src[...]

    @pl.when(jnp.logical_not(end))
    def _():
        both[0] = src[...]
        both[1] = core[...]


def start_of(level):
    return sum(2048 >> l for l in range(level))


def weights_of(far, level, cluster):
    row = start_of(level) + cluster
    total = far.shape[1]
    tail = total // 128 * 128
    if start_of(level) >= tail:
        chunk, base = far[:, tail:], tail
    else:
        base = row // 128 * 128
        chunk = far[:, pl.ds(pl.multiple_of(base, 128), 128)]
    lane = lax.broadcasted_iota(jnp.int32, chunk.shape, 1)
    w = jnp.sum(jnp.where(lane == row - base, chunk, 0), axis=1, keepdims=True).astype(F32)
    return [w[j : j + 1, :] for j in range(3)]


def couple(weights, sources, coupling):
    total = None
    for w, m, c in zip(weights, sources, coupling):
        term = dot3(split(m * w), c, NT)
        total = term if total is None else total + term
    return total


def local(far, c, level, cluster, values, width, first=0):
    at = cluster % width
    group = at // 4 * 4 + first
    return couple(weights_of(far, level, cluster), [values[group + (at + j) % 4] for j in (1, 2, 3)], c)


def low_kernel(far, coupling, tsplit, m1, loc_a, top, d7, d8, d9):
    c = [split(coupling[i]) for i in range(3)]
    d = device_index()
    for i in range(4):
        w = weights_of(far, 1, d * 4 + i)
        loc_a[i] = couple(w, [m1[(i + j) % 4] for j in (1, 2, 3)], c)

    at7, at8, at9 = d >> 4, d >> 5, d >> 6
    turned = jnp.concatenate([coupling[i].T for i in range(3)], axis=0)
    below8 = child_transfer(tsplit, at8 % 2)
    below7 = child_transfer(tsplit, at7 % 2)
    from8 = dot3(split(turned), below7, NT)
    from9 = dot3(split(dot3(split(turned), below8, NT)), below7, NT)
    for held, values, level, at in ((d7, turned, 7, at7), (d8, from8, 8, at8), (d9, from9, 9, at9)):
        w = weights_of(far, level, at)
        held[0] = jnp.zeros((64, 64), F32)
        for j in (1, 2, 3):
            held[j] = w[j - 1] * values[(j - 1) * 64 : j * 64]
    lifts = (tsplit[0], tsplit[1])
    whole = jnp.concatenate([d9[(p - at9) & 3] for p in range(4)], axis=1)
    for count, held, at in ((8, d8, at8), (16, d7, at7)):
        both = dot3(lifts, split(whole), NN)
        parts = []
        for p in range(count):
            own = held[(p - at) & 3] * jnp.where(p >> 2 == at >> 2, 1.0, 0.0)
            half, column = p % 2 * 64, p // 2 * 64
            parts.append(both[half : half + 64, column : column + 64] + own)
        whole = jnp.concatenate(parts, axis=1) if count == 8 else jnp.concatenate(parts, axis=0)
    top[0], top[1] = split(whole)


def low2_kernel(far, coupling, m0, m23, m4, behind, loc_b):
    c = [split(coupling[i]) for i in range(3)]
    d = device_index()
    for i in range(8):
        w = weights_of(far, 0, d * 8 + i)
        loc_b[4 + i] = couple(w, [m0[i // 4 * 4 + (i + j) % 4] for j in (1, 2, 3)], c)
    for i in range(2):
        loc_b[i] = local(far, c, 2, d * 2 + i, m23, 8)
    loc_b[2] = local(far, c, 3, d, m23, 4, 8)
    loc_b[3] = local(far, c, 4, d >> 1, m4, 4)


def mid_kernel(far, coupling, tsplit, loc_a, loc_b, m56, basis_in, blocks_in, part, g, blocks, basis, sems):
    basis_copy = pltpu.make_async_copy(basis_in, basis, sems.at[0])
    basis_copy.start()
    blocks_copy = pltpu.make_async_copy(blocks_in, blocks, sems.at[1])
    blocks_copy.start()
    c = [split(coupling[i]) for i in range(3)]
    d = device_index()
    rows = lax.broadcasted_iota(jnp.int32, (64, 64), 0)
    cols = lax.broadcasted_iota(jnp.int32, (64, 64), 1)
    chain = jnp.where(rows == cols, 1.0, 0.0).astype(F32)
    zero = jnp.zeros((64, 64), F32)
    state = jnp.concatenate([zero, chain], 0)
    for level, width, first in ((6, 4, 8), (5, 8, 0), (4, 0, 0), (3, 0, 0)):
        cluster = d >> (level - 3)
        here = local(far, c, level, cluster, m56, width, first) if width else loc_b[level - 1]
        state = dot3(split(state), child_transfer(tsplit, cluster % 2), NT) + jnp.concatenate([here, zero], 0)
    for locs, first, count in ((loc_b, 0, 2), (loc_a, 0, 4), (loc_b, 4, 8)):
        parts = split(state)
        sides = [dot3(parts, (tsplit[0, k * 64 : (k + 1) * 64], tsplit[1, k * 64 : (k + 1) * 64]), NT) for k in (0, 1)]
        below = []
        for i in range(count):
            at = i // 2 * 128
            below.append(sides[i % 2][at : at + 64] + locs[first + i])
            below.append(sides[i % 2][at + 64 : at + 128])
        state = jnp.concatenate(below, 0)
    basis_copy.wait()
    leaves, _, pts = basis.shape
    high, low = split(state)
    for i in range(leaves):
        rows_at = slice(i * 128, (i + 1) * 128)
        at = slice(i * pts, (i + 1) * pts)
        whole = dot(high[rows_at], basis[i], NN) + dot(low[rows_at], basis[i], NN)
        part[:, at] = whole[:64]
        g[0, :, at], g[1, :, at] = split(whole[64:])
    blocks_copy.wait()


def near_kernel(far_part, core, cross4, shifted, other, blocks, src_in, pattern_in, part, held, own, pattern, sems):
    leaves, slots, pts = blocks.shape[:3]
    own_copy = pltpu.make_async_copy(src_in, own, sems.at[0])
    own_copy.start()
    pattern_copy = pltpu.make_async_copy(pattern_in, pattern, sems.at[1])
    pattern_copy.start()
    for n, ref in enumerate((core, cross4, shifted.at[0], other)):
        for i in range(leaves):
            held[(n + 1) * leaves + i] = ref[:, i * pts : (i + 1) * pts]
    own_copy.wait()
    for i in range(leaves):
        held[i] = own[:, i * pts : (i + 1) * pts]
    pattern_copy.wait()
    d = device_index()
    others = [d, d ^ 4, across(d, 4, device_count()), d + jnp.where(lax.axis_index("c") == 0, -1, 1)]
    for i in range(leaves):
        at = slice(i * pts, (i + 1) * pts)
        total = far_part[:, at]
        for s in range(slots):
            j = pattern[s, i]
            device = j // leaves
            slot = jnp.int32(4)
            for k, other_device in enumerate(others):
                slot = jnp.where(device == other_device, k, slot)
            total = total + dot(held[slot * leaves + j % leaves], blocks[i, s], NT)
        part[:, at] = total


def last_kernel(top, g7, part, g, out):
    moments = jnp.concatenate([g7[i] for i in range(8)], axis=1)
    field = dot3(split(moments), (top[0], top[1]), NN)
    high, low = split(field)
    both = jnp.concatenate([high, low], 0)
    step = 256
    for at in range(0, out.shape[1], step):
        at = slice(at, at + step)
        first = dot(both, g[0, :, at], NN)
        far_part = first[:64] + (first[64:] + dot(high, g[1, :, at], NN))
        out[:, at] = (far_part + part[:, at]).astype(BF16)


def shards(sources, leaf_basis, transfer, coupling, near_blocks, near_pattern, far_pattern):
    leaves, pts, rank = leaf_basis.shape
    rhs = sources.shape[1]
    points = leaves * pts
    src_in = sources.T
    basis_in = jnp.swapaxes(leaf_basis, 1, 2)
    far_in = far_pattern.T
    of = jax.ShapeDtypeStruct
    mat = lambda n: of((n, rhs, rank), F32)
    pair = of((rhs, 2 * rank), F32)

    src, coup, far, tsplit, m0, m1, pair2 = pl.pallas_call(
        leaf_kernel,
        out_shape=(
            of(src_in.shape, BF16), of(coupling.shape, F32), of(far_in.shape, jnp.int32),
            of((2, 2 * rank, rank), BF16), mat(8), mat(4), pair,
        ),
        in_specs=[HBM] * 5, out_specs=(VMEM,) * 7,
        scratch_shapes=[pltpu.VMEM(basis_in.shape, BF16), pltpu.VMEM(transfer.shape, F32), pltpu.SemaphoreType.DMA((5,))],
        name="leaf", compiler_params=PARAMS,
    )(*[in_hbm(a) for a in (src_in, basis_in, transfer, coupling, far_in)])

    def up4(own, masks, axis, copies, *behind):
        got = [swap(own, masks[i - 1]) for i in ORDER]
        top = of((copies,) + pair.shape, F32) if copies else pair
        return pl.pallas_call(
            lambda *refs: up4_kernel(copies, axis, refs),
            out_shape=(mat(12), top), in_specs=[VMEM] * (5 + len(behind)), out_specs=(VMEM,) * 2,
            scratch_shapes=[pltpu.VMEM((4,) + pair.shape, F32)], name="up4", compiler_params=PARAMS,
        )(own, *got, tsplit, *behind)

    def up2(own, mask, axis, *sources):
        return pl.pallas_call(
            lambda *refs: up2_kernel(axis, refs),
            out_shape=(mat(4), pair, of((2,) + src_in.shape, BF16)), in_specs=[VMEM] * 6, out_specs=(VMEM,) * 3,
            scratch_shapes=[pltpu.VMEM((2,) + pair.shape, F32)], name="up2", compiler_params=PARAMS,
        )(own, swap(own, mask), tsplit, *sources)

    loc_a, top = pl.pallas_call(
        low_kernel, out_shape=(mat(4), of((2, 16 * rank, rank), BF16)), in_specs=[VMEM] * 4, out_specs=(VMEM,) * 2,
        scratch_shapes=[pltpu.VMEM((4, rank, rank), F32)] * 3,
        name="low", compiler_params=PARAMS,
    )(far, coup, tsplit, m1)
    core, cross4 = swap(src, 4), swap_across(src, 4)
    m23, pair4 = up4(pair2, (1, 2, 3), "x", 0, loc_a)
    m4, pair5, both = up2(pair4, 4, "c", src, cross4, core)
    loc_b = pl.pallas_call(
        low2_kernel, out_shape=mat(12), in_specs=[VMEM] * 6, out_specs=VMEM,
        name="low2", compiler_params=PARAMS,
    )(far, coup, m0, m23, m4, pair5)

    shifted = shift(both)
    m56, pair7 = up4(pair5, (8, 16, 24), "y", 8, loc_b)
    g7 = lax.all_to_all(pair7, "z", 0, 0, tiled=True)
    other = swap(shifted[1], 4)

    far_part, g, blocks = pl.pallas_call(
        mid_kernel,
        out_shape=(of((rhs, points), F32), of((2, rhs, points), BF16), of(near_blocks.shape, BF16)),
        in_specs=[VMEM] * 6 + [HBM] * 2, out_specs=(VMEM,) * 3,
        scratch_shapes=[pltpu.VMEM(basis_in.shape, BF16), pltpu.SemaphoreType.DMA((2,))],
        name="mid", compiler_params=PARAMS,
    )(far, coup, tsplit, loc_a, loc_b, m56, in_hbm(basis_in), in_hbm(near_blocks))
    part = pl.pallas_call(
        near_kernel,
        out_shape=of((rhs, points), F32),
        in_specs=[VMEM] * 6 + [HBM] * 2, out_specs=VMEM,
        scratch_shapes=[
            pltpu.VMEM((5 * leaves, rhs, pts), BF16),
            pltpu.VMEM(src_in.shape, BF16),
            pltpu.SMEM(near_pattern.shape[::-1], jnp.int32),
            pltpu.SemaphoreType.DMA((2,)),
        ],
        name="near", compiler_params=PARAMS,
    )(far_part, core, cross4, shifted, other, blocks, in_hbm(src_in), in_hbm(near_pattern.T))

    product = pl.pallas_call(
        last_kernel,
        out_shape=of((rhs, points), BF16),
        in_specs=[VMEM] * 4, out_specs=VMEM,
        name="last", compiler_params=PARAMS,
    )(top, g7, part, g)
    return product.T


def solution(mesh):
    leaf, sub = mesh.shape["leaf"], mesh.shape["sub"]
    cut = Mesh(mesh.devices.reshape(leaf // 8, 4, 2, sub), AXES)
    placed = (
        P(AXES, None),
        P(AXES, None, None),
        P(),
        P(),
        P(AXES, None, None, None),
        P(AXES, None),
        P(),
    )
    return jax.shard_map(shards, mesh=cut, in_specs=placed, out_specs=P(AXES, None), check_vma=False)
```

time: 45.9 us -> 45.2 us (0.985)
  the two profiles are of different devices: /device:TPU:1 before, /device:TPU:2 now
where the time goes in v5:
time: 45.2 us; the launch traced here: 45 us
  starting transfers between devices  21 us (46%)
  Pallas kernels  13.8 us (31%)
  waiting for transfers between devices  10.1 us (22%)
    ppermute x9, starting transfers between devices, swap(): lax.ppermute(array, AXES, [(i, i ^ mask) for i in range(device_count())])  8.37 us
    ppermute x1, starting transfers between devices, swap_across(): return lax.ppermute(array, AXES, pairs)  7.84 us
    all_to_all x1, waiting for transfers between devices, shards(): g7 = lax.all_to_all(pair7, 'z', 0, 0, tiled=True)  5.78 us
    ppermute x9, waiting for transfers between devices, swap(): lax.ppermute(array, AXES, [(i, i ^ mask) for i in range(device_count())])  4.32 us
    all_to_all x1, starting transfers between devices, shards(): g7 = lax.all_to_all(pair7, 'z', 0, 0, tiled=True)  4.19 us
    pallas_call x1, Pallas kernels, shards(): pl.pallas_call(mid_kernel, out_shape=(of((rhs, points), F32), of((2, rhs,...  3.65 us
    pallas_call x1, Pallas kernels, shards(): pl.pallas_call(near_kernel, out_shape=of((rhs, points), F32), in_specs=[V...  2.38 us
    pallas_call x1, Pallas kernels, shards(): pl.pallas_call(leaf_kernel, out_shape=(of(src_in.shape, BF16), of(couplin...  1.81 us
  transfers between devices with their start and end apart: 12, of which 7 were waited for; matrix products, arithmetic and copies ran while one was open for 0% of the time, Pallas kernels for 23%

profile of v5, /device:TPU:2, one launch (start us, length us, event | category | flops | bytes accessed | tf_op | source)
XLA Modules:
  0.0 45.0 jit_solution(4185354789079821596)
XLA Ops:
  0.0 1.8 %leaf.1 = (bf16[64,2048]{1,0:T(8,128)(2,1)S(1)}, f32[3,64,64]{2,1,0:T(8,128)S(1)}, s32[3,4092]{1,0:T(4,128)S(1)}, bf16[2,128,64]{2,1,0:T(8,128)(2,1)S(1)}, f32[8...) custom-call(bf16[64,2048]{1,0:T(8,128)(2,1)} %bitcast.9, bf16[8,64,256]{2,1,0:T(8,128)(2,1)} %bitcast.7, ...), custom_call_target="tpu_custom_call" | custom-call | tf_op jit(solution)/shard_map/leaf/pallas_call | solution.py:324
  1.8 7.8 %collective-permute-start.4 = (bf16[64,2048]{1,0:T(8,128)(2,1)S(1)}, bf16[64,2048]{1,0:T(8,128)(2,1)S(1)}, u32[]{:S(2)}, u32[]{:S(2)}) collective-permute-start(bf16[64,2048]{1,0:T(8,128)(2,1)S(1)} %get-tuple-element.32.refs_3_), channel_id=1, source_target_pairs={{0,252},{1,253},{2,254},{3,255},{4,8},{5,9},{6,10},{7,11},{8,4},{9... | collective-permute-start | bytes 786440 | tf_op jit(solution)/shard_map/ppermute | solution.py:78
  9.7 0.0 collective-permute-start.5
  9.7 2.1 %collective-permute-start = (f32[64,128]{1,0:T(8,128)S(1)}, f32[64,128]{1,0:T(8,128)S(1)}, u32[]{:S(2)}, u32[]{:S(2)}) collective-permute-start(f32[64,128]{1,0:T(8,128)S(1)} %get-tuple-element.29.refs_0_), channel_id=1, source_target_pairs={{0,2},{1,3},{2,0},{3,1},{4,6},{5,7},{6,4},{7,5},{8,10},{9,11},{10,... | collective-permute-start | bytes 98312 | tf_op jit(solution)/shard_map/ppermute | solution.py:68
  11.8 1.4 %collective-permute-start.1 = (f32[64,128]{1,0:T(8,128)S(1)}, f32[64,128]{1,0:T(8,128)S(1)}, u32[]{:S(2)}, u32[]{:S(2)}) collective-permute-start(f32[64,128]{1,0:T(8,128)S(1)} %get-tuple-element.29.refs_0_), channel_id=1, source_target_pairs={{0,1},{1,0},{2,3},{3,2},{4,5},{5,4},{6,7},{7,6},{8,9},{9,8},{10,11... | collective-permute-start | bytes 98312 | tf_op jit(solution)/shard_map/ppermute | solution.py:68
  13.2 0.5 %collective-permute-start.2 = (f32[64,128]{1,0:T(8,128)S(1)}, f32[64,128]{1,0:T(8,128)S(1)}, u32[]{:S(2)}, u32[]{:S(2)}) collective-permute-start(f32[64,128]{1,0:T(8,128)S(1)} %get-tuple-element.29.refs_0_), channel_id=1, source_target_pairs={{0,3},{1,2},{2,1},{3,0},{4,7},{5,6},{6,5},{7,4},{8,11},{9,10},{10,... | collective-permute-start | bytes 98312 | tf_op jit(solution)/shard_map/ppermute | solution.py:68
  13.8 1.5 %low.1 = (f32[4,64,64]{2,1,0:T(8,128)S(1)}, bf16[2,1024,64]{2,1,0:T(8,128)(2,1)S(1)}) custom-call(s32[3,4092]{1,0:T(4,128)S(1)} %get-tuple-element.24.far, f32[3,64,64]{2,1,0:T(8,128)S(1)} %get-tuple-element.25.coupling, bf16[2,128,64]{2,1,0:T(8,128)(2,1)S(1)} %get-tuple-element.26.tsplit.refs_4_.refs_2_, f32[4,64,64]{2,1,0:T(8,128)S(1)} %get-tuple-element.27.m1), custom_call_target="tpu_custom_call" | custom-call | tf_op jit(solution)/shard_map/low/pallas_call | solution.py:351
  15.2 0.1 collective-permute-done.refs_1_
  15.3 0.4 collective-permute-done.1.refs_2_
  15.7 1.4 %collective-permute-done.2.refs_3_ = f32[64,128]{1,0:T(8,128)S(1)} collective-permute-done((f32[64,128]{1,0:T(8,128)S(1)}, f32[64,128]{1,0:T(8,128)S(1)}, u32[]{:S(2)}, u32[]{:S(2)}) %collective-permute-start.2) | collective-permute-done | bytes 32800 | tf_op jit(solution)/shard_map/ppermute | solution.py:68
  17.1 0.5 %up4.2 = (f32[12,64,64]{2,1,0:T(8,128)S(1)}, f32[64,128]{1,0:T(8,128)S(1)}) custom-call(f32[64,128]{1,0:T(8,128)S(1)} %get-tuple-element.29.refs_0_, f32[64,128]{1,0:T(8,128)S(1)} %collective-permute-done.refs_1_, f32[64,128]{1,0:T(8,128)S(1)} %collective-permute-done.1.refs_2_, f32[64,128]{1,0:T(8,128)S(1)} %collective-permute-done.2.refs_3_, ...), custom_call_target="tpu_custom_call" | custom-call | tf_op jit(solution)/shard_map/up4/pallas_call | solution.py:338
  17.6 0.1 collective-permute-start.3
  17.7 1.2 %collective-permute-done.3.refs_1_ = f32[64,128]{1,0:T(8,128)S(1)} collective-permute-done((f32[64,128]{1,0:T(8,128)S(1)}, f32[64,128]{1,0:T(8,128)S(1)}, u32[]{:S(2)}, u32[]{:S(2)}) %collective-permute-start.3) | collective-permute-done | bytes 32800 | tf_op jit(solution)/shard_map/ppermute | solution.py:68
  18.9 0.0 collective-permute-done.4.refs_4_.cross4
  18.9 0.0 collective-permute-done.5.refs_5_.core
  18.9 0.3 up2.1
  19.2 0.6 %collective-permute-start.9 = (bf16[2,64,2048]{2,1,0:T(8,128)(2,1)S(1)}, bf16[2,64,2048]{2,1,0:T(8,128)(2,1)S(1)}, u32[]{:S(2)}, u32[]{:S(2)}) collective-permute-start(bf16[2,64,2048]{2,1,0:T(8,128)(2,1)S(1)} %get-tuple-element.40), channel_id=1, source_target_pairs={{0,1},{1,2},{2,3},{3,0},{4,7},{5,4},{6,5},{7,6},{8,9},{9,10},{10,1... | collective-permute-start | bytes 1572872 | tf_op jit(solution)/shard_map/ppermute | solution.py:84
  19.8 0.0 collective-permute-start.6
  19.9 0.0 collective-permute-start.7
  19.9 4.1 %collective-permute-start.8 = (f32[64,128]{1,0:T(8,128)S(1)}, f32[64,128]{1,0:T(8,128)S(1)}, u32[]{:S(2)}, u32[]{:S(2)}) collective-permute-start(f32[64,128]{1,0:T(8,128)S(1)} %get-tuple-element.33.behind.refs_0_), channel_id=1, source_target_pairs={{0,24},{1,25},{2,26},{3,27},{4,28},{5,29},{6,30},{7,31},{8,16},{9,... | collective-permute-start | bytes 98312 | tf_op jit(solution)/shard_map/ppermute | solution.py:68
  23.9 1.1 %low2.1.refs_5_.loc_b = f32[12,64,64]{2,1,0:T(8,128)S(1)} custom-call(s32[3,4092]{1,0:T(4,128)S(1)} %get-tuple-element.24.far, f32[3,64,64]{2,1,0:T(8,128)S(1)} %get-tuple-element.25.coupling, f32[8,64,64]{2,1,0:T(8,128)S(1)} %get-tuple-element.34.m0, f32[12,64,64]{2,1,0:T(8,128)S(1)} %get-tuple-element.35.m23, f32[4,64,64]{2,1,0:T(8,128)S(1)} %get-tuple-element.36.m4, ...), custom_call_target="tpu_custom_call" | custom-call | tf_op jit(solution)/shard_map/low2/pallas_call | solution.py:359
  25.1 0.4 collective-permute-done.6.refs_1_
  25.5 0.0 collective-permute-done.7.refs_2_
  25.5 0.9 %collective-permute-done.8.refs_3_ = f32[64,128]{1,0:T(8,128)S(1)} collective-permute-done((f32[64,128]{1,0:T(8,128)S(1)}, f32[64,128]{1,0:T(8,128)S(1)}, u32[]{:S(2)}, u32[]{:S(2)}) %collective-permute-start.8) | collective-permute-done | bytes 32800 | tf_op jit(solution)/shard_map/ppermute | solution.py:68
  26.3 1.2 %up4.3 = (f32[12,64,64]{2,1,0:T(8,128)S(1)}, f32[8,64,128]{2,1,0:T(8,128)}) custom-call(f32[64,128]{1,0:T(8,128)S(1)} %get-tuple-element.33.behind.refs_0_, f32[64,128]{1,0:T(8,128)S(1)} %collective-permute-done.6.refs_1_, f32[64,128]{1,0:T(8,128)S(1)} %collective-permute-done.7.refs_2_, f32[64,128]{1,0:T(8,128)S(1)} %collective-permute-done.8.refs_3_, ...), custom_call_target="tpu_custom_call" | custom-call | tf_op jit(solution)/shard_map/up4/pallas_call | solution.py:338
  27.6 4.2 %all-to-all-start = ((f32[8,64,128]{2,1,0:T(8,128)}), f32[8,64,128]{2,1,0:T(8,128)S(1)}, u32[]{:S(2)}, u32[]{:S(2)}) async-start(f32[8,64,128]{2,1,0:T(8,128)} %get-tuple-element.37), calls=%async_computation | async-start | bytes 524288 | tf_op jit(solution)/shard_map/all_to_all | solution.py:366
  31.7 0.0 collective-permute-done.9.shifted
  31.8 0.1 collective-permute-start.10
  31.9 3.6 %mid.1 = (f32[64,2048]{1,0:T(8,128)S(1)}, bf16[2,64,2048]{2,1,0:T(8,128)(2,1)S(1)}, bf16[8,4,256,256]{3,2,1,0:T(8,128)(2,1)S(1)}) custom-call(s32[3,4092]{1,0:T(4,128)S(1)} %get-tuple-element.24.far, f32[3,64,64]{2,1,0:T(8,128)S(1)} %get-tuple-element.25.coupling, bf16[2,128,64]{2,1,0:T(8,128)(2,1)S(1)} %get-tuple-element.26.tsplit.refs_4_.refs_2_, ...), custom_call_target="tpu_custom_call" | custom-call | tf_op jit(solution)/shard_map/mid/pallas_call | solution.py:369
  35.5 0.0 collective-permute-done.10.other
  35.5 2.4 %near.1.part = f32[64,2048]{1,0:T(8,128)S(1)} custom-call(f32[64,2048]{1,0:T(8,128)S(1)} %get-tuple-element.39.far_part, bf16[64,2048]{1,0:T(8,128)(2,1)S(1)} %collective-permute-done.5.refs_5_.core, bf16[64,2048]{1,0:T(8,128)(2,1)S(1)} %collective-permute-done.4.refs_4_.cross4, bf16[2,64,2048]{2,1,0:T(8,128)(2,1)S(1)} %collective-permute-done.9.shifted, ...), custom_call_target="tpu_custom_call" | custom-call | tf_op jit(solution)/shard_map/near/pallas_call | solution.py:376
  37.9 5.8 %all-to-all-done.g7 = f32[8,64,128]{2,1,0:T(8,128)S(1)} async-done(((f32[8,64,128]{2,1,0:T(8,128)}), f32[8,64,128]{2,1,0:T(8,128)S(1)}, u32[]{:S(2)}, u32[]{:S(2)}) %all-to-all-start) | async-done | bytes 262176 | tf_op jit(solution)/shard_map/all_to_all | solution.py:366
  43.7 1.3 %last.1 = bf16[64,2048]{1,0:T(8,128)(2,1)} custom-call(bf16[2,1024,64]{2,1,0:T(8,128)(2,1)S(1)} %get-tuple-element.28.top, f32[8,64,128]{2,1,0:T(8,128)S(1)} %all-to-all-done.g7, f32[64,2048]{1,0:T(8,128)S(1)} %near.1.part, bf16[2,64,2048]{2,1,0:T(8,128)(2,1)S(1)} %get-tuple-element.42.g), custom_call_target="tpu_custom_call" | custom-call | tf_op jit(solution)/shard_map/last/pallas_call | solution.py:389
  (1 shorter events, 0.0 us)
Async XLA Ops:
  1.8 17.1 %collective-permute-start.4 = (bf16[64,2048]{1,0:T(8,128)(2,1)S(1)}, bf16[64,2048]{1,0:T(8,128)(2,1)S(1)}, u32[]{:S(2)}, u32[]{:S(2)}) collective-permute-start(bf16[64,2048]{1,0:T(8,128)(2,1)S(1)} %get-tuple-element.32.refs_3_), channel_id=1, source_target_pairs={{0,252},{1,253},{2,254},{3,255},{4,8},{5,9},{6,10},{7,11},{8,4},{9... | collective-permute-start | bytes 786440 | tf_op jit(solution)/shard_map/ppermute | solution.py:78
  9.7 9.3 %collective-permute-start.5 = (bf16[64,2048]{1,0:T(8,128)(2,1)S(1)}, bf16[64,2048]{1,0:T(8,128)(2,1)S(1)}, u32[]{:S(2)}, u32[]{:S(2)}) collective-permute-start(bf16[64,2048]{1,0:T(8,128)(2,1)S(1)} %get-tuple-element.32.refs_3_), channel_id=1, source_target_pairs={{0,4},{1,5},{2,6},{3,7},{4,0},{5,1},{6,2},{7,3},{8,12},{9,13},{10,... | collective-permute-start | bytes 786440 | tf_op jit(solution)/shard_map/ppermute | solution.py:68
  9.7 5.7 %collective-permute-start = (f32[64,128]{1,0:T(8,128)S(1)}, f32[64,128]{1,0:T(8,128)S(1)}, u32[]{:S(2)}, u32[]{:S(2)}) collective-permute-start(f32[64,128]{1,0:T(8,128)S(1)} %get-tuple-element.29.refs_0_), channel_id=1, source_target_pairs={{0,2},{1,3},{2,0},{3,1},{4,6},{5,7},{6,4},{7,5},{8,10},{9,11},{10,... | collective-permute-start | bytes 98312 | tf_op jit(solution)/shard_map/ppermute | solution.py:68
  11.8 3.9 %collective-permute-start.1 = (f32[64,128]{1,0:T(8,128)S(1)}, f32[64,128]{1,0:T(8,128)S(1)}, u32[]{:S(2)}, u32[]{:S(2)}) collective-permute-start(f32[64,128]{1,0:T(8,128)S(1)} %get-tuple-element.29.refs_0_), channel_id=1, source_target_pairs={{0,1},{1,0},{2,3},{3,2},{4,5},{5,4},{6,7},{7,6},{8,9},{9,8},{10,11... | collective-permute-start | bytes 98312 | tf_op jit(solution)/shard_map/ppermute | solution.py:68
  13.2 3.9 %collective-permute-start.2 = (f32[64,128]{1,0:T(8,128)S(1)}, f32[64,128]{1,0:T(8,128)S(1)}, u32[]{:S(2)}, u32[]{:S(2)}) collective-permute-start(f32[64,128]{1,0:T(8,128)S(1)} %get-tuple-element.29.refs_0_), channel_id=1, source_target_pairs={{0,3},{1,2},{2,1},{3,0},{4,7},{5,6},{6,5},{7,4},{8,11},{9,10},{10,... | collective-permute-start | bytes 98312 | tf_op jit(solution)/shard_map/ppermute | solution.py:68
  17.6 1.3 %collective-permute-start.3 = (f32[64,128]{1,0:T(8,128)S(1)}, f32[64,128]{1,0:T(8,128)S(1)}, u32[]{:S(2)}, u32[]{:S(2)}) collective-permute-start(f32[64,128]{1,0:T(8,128)S(1)} %get-tuple-element.31.refs_0_), channel_id=1, source_target_pairs={{0,4},{1,5},{2,6},{3,7},{4,0},{5,1},{6,2},{7,3},{8,12},{9,13},{10,... | collective-permute-start | bytes 98312 | tf_op jit(solution)/shard_map/ppermute | solution.py:68
  19.2 12.5 %collective-permute-start.9 = (bf16[2,64,2048]{2,1,0:T(8,128)(2,1)S(1)}, bf16[2,64,2048]{2,1,0:T(8,128)(2,1)S(1)}, u32[]{:S(2)}, u32[]{:S(2)}) collective-permute-start(bf16[2,64,2048]{2,1,0:T(8,128)(2,1)S(1)} %get-tuple-element.40), channel_id=1, source_target_pairs={{0,1},{1,2},{2,3},{3,0},{4,7},{5,4},{6,5},{7,6},{8,9},{9,10},{10,1... | collective-permute-start | bytes 1572872 | tf_op jit(solution)/shard_map/ppermute | solution.py:84
  19.8 5.6 %collective-permute-start.6 = (f32[64,128]{1,0:T(8,128)S(1)}, f32[64,128]{1,0:T(8,128)S(1)}, u32[]{:S(2)}, u32[]{:S(2)}) collective-permute-start(f32[64,128]{1,0:T(8,128)S(1)} %get-tuple-element.33.behind.refs_0_), channel_id=1, source_target_pairs={{0,16},{1,17},{2,18},{3,19},{4,20},{5,21},{6,22},{7,23},{8,24},{9,... | collective-permute-start | bytes 98312 | tf_op jit(solution)/shard_map/ppermute | solution.py:68
  19.9 5.6 %collective-permute-start.7 = (f32[64,128]{1,0:T(8,128)S(1)}, f32[64,128]{1,0:T(8,128)S(1)}, u32[]{:S(2)}, u32[]{:S(2)}) collective-permute-start(f32[64,128]{1,0:T(8,128)S(1)} %get-tuple-element.33.behind.refs_0_), channel_id=1, source_target_pairs={{0,8},{1,9},{2,10},{3,11},{4,12},{5,13},{6,14},{7,15},{8,0},{9,1},... | collective-permute-start | bytes 98312 | tf_op jit(solution)/shard_map/ppermute | solution.py:68
  19.9 6.5 %collective-permute-start.8 = (f32[64,128]{1,0:T(8,128)S(1)}, f32[64,128]{1,0:T(8,128)S(1)}, u32[]{:S(2)}, u32[]{:S(2)}) collective-permute-start(f32[64,128]{1,0:T(8,128)S(1)} %get-tuple-element.33.behind.refs_0_), channel_id=1, source_target_pairs={{0,24},{1,25},{2,26},{3,27},{4,28},{5,29},{6,30},{7,31},{8,16},{9,... | collective-permute-start | bytes 98312 | tf_op jit(solution)/shard_map/ppermute | solution.py:68
  27.6 16.2 %all-to-all-start = ((f32[8,64,128]{2,1,0:T(8,128)}), f32[8,64,128]{2,1,0:T(8,128)S(1)}, u32[]{:S(2)}, u32[]{:S(2)}) async-start(f32[8,64,128]{2,1,0:T(8,128)} %get-tuple-element.37), calls=%async_computation | async-start | bytes 524288 | tf_op jit(solution)/shard_map/all_to_all | solution.py:366
  31.8 3.8 %collective-permute-start.10 = (bf16[64,2048]{1,0:T(8,128)(2,1)S(1)}, bf16[64,2048]{1,0:T(8,128)(2,1)S(1)}, u32[]{:S(2)}, u32[]{:S(2)}) collective-permute-start(bf16[64,2048]{1,0:T(8,128)(2,1)S(1)} %slice_bitcast_fusion), channel_id=1, source_target_pairs={{0,4},{1,5},{2,6},{3,7},{4,0},{5,1},{6,2},{7,3},{8,12},{9,13},{10,... | collective-permute-start | bytes 786440 | tf_op jit(solution)/shard_map/ppermute | solution.py:68

commit v6 on v5

--- a/solution.py
+++ b/solution.py
@@ -74,8 +74,8 @@
 
 def swap_across(array, step):
     n = device_count()
-    pairs = [(i, (i + (step if i & step else n - step)) % n) for i in range(n)]
-    return lax.ppermute(array, AXES, pairs)
+    others = [i + step if i & step else i - step for i in range(n)]
+    return lax.ppermute(array, AXES, [(i, o if 0 <= o < n else i ^ 1) for i, o in enumerate(others)])
 
 
 def shift(array):
@@ -129,8 +129,11 @@
         ab[8 + i] = mid[i * 64 : (i + 1) * 64]
     top = paired(lift(paired(mid), tsplit))
     if copies:
+        onward = refs[5]
+        sent = dot3(split(top), (onward[0], onward[1]), NN)
         for i in range(copies):
-            pair[i] = top
+            one = sent[:, i * 64 : (i + 1) * 64]
+            pair[i] = pair_of(one[:32], one[32:])
     else:
         pair[...] = top
 
@@ -175,6 +178,21 @@
     return [w[j : j + 1, :] for j in range(3)]
 
 
+def weight_at(far, level, cluster, offset):
+    row = start_of(level) + cluster
+    total = far.shape[1]
+    tail = total // 128 * 128
+    if start_of(level) >= tail:
+        chunk, base = far[:, tail:], tail
+    else:
+        base = row // 128 * 128
+        chunk = far[:, pl.ds(pl.multiple_of(base, 128), 128)]
+    lane = lax.broadcasted_iota(jnp.int32, chunk.shape, 1)
+    which = lax.broadcasted_iota(jnp.int32, chunk.shape, 0)
+    found = jnp.where((lane == row - base) & (which == offset - 1), chunk, 0)
+    return jnp.sum(jnp.sum(found, axis=1, keepdims=True), axis=0, keepdims=True).astype(F32)
+
+
 def couple(weights, sources, coupling):
     total = None
     for w, m, c in zip(weights, sources, coupling):
@@ -196,28 +214,30 @@
         w = weights_of(far, 1, d * 4 + i)
         loc_a[i] = couple(w, [m1[(i + j) % 4] for j in (1, 2, 3)], c)
 
-    at7, at8, at9 = d >> 4, d >> 5, d >> 6
+    z, half, planes = lax.axis_index("z"), lax.axis_index("y") >> 1, lax.axis_size("z")
     turned = jnp.concatenate([coupling[i].T for i in range(3)], axis=0)
-    below8 = child_transfer(tsplit, at8 % 2)
-    below7 = child_transfer(tsplit, at7 % 2)
-    from8 = dot3(split(turned), below7, NT)
-    from9 = dot3(split(dot3(split(turned), below8, NT)), below7, NT)
-    for held, values, level, at in ((d7, turned, 7, at7), (d8, from8, 8, at8), (d9, from9, 9, at9)):
-        w = weights_of(far, level, at)
-        held[0] = jnp.zeros((64, 64), F32)
-        for j in (1, 2, 3):
-            held[j] = w[j - 1] * values[(j - 1) * 64 : j * 64]
-    lifts = (tsplit[0], tsplit[1])
-    whole = jnp.concatenate([d9[(p - at9) & 3] for p in range(4)], axis=1)
-    for count, held, at in ((8, d8, at8), (16, d7, at7)):
-        both = dot3(lifts, split(whole), NN)
-        parts = []
-        for p in range(count):
-            own = held[(p - at) & 3] * jnp.where(p >> 2 == at >> 2, 1.0, 0.0)
-            half, column = p % 2 * 64, p // 2 * 64
-            parts.append(both[half : half + 64, column : column + 64] + own)
-        whole = jnp.concatenate(parts, axis=1) if count == 8 else jnp.concatenate(parts, axis=0)
-    top[0], top[1] = split(whole)
+    below = child_transfer(tsplit, half)
+    parts = split(turned)
+    above = [dot3(parts, child_transfer(tsplit, k), NT) for k in (0, 1)]
+    from8 = dot3(parts, below, NT)
+    from9 = dot3(split(jnp.concatenate(above, axis=0)), below, NT)
+    for held, values in ((d7, turned), (d8, from8), (d9, from9)):
+        for j in range(values.shape[0] // 64):
+            held[j] = values[j * 64 : (j + 1) * 64]
+
+    def term(held, first, level, target, source):
+        offset = (source - target) & 3
+        w = weight_at(far, level, target, offset) * jnp.where(source >> 2 == target >> 2, 1.0, 0.0)
+        return w * held[first + jnp.maximum(offset - 1, 0)]
+
+    whole = jnp.concatenate([term(d9, p % 2 * 3, 9, p >> 1, z >> 1) for p in range(planes)], axis=1)
+    whole = dot3(child_transfer(tsplit, z & 1), split(whole), NN)
+    whole = whole + jnp.concatenate([term(d8, 0, 8, p, z) for p in range(planes)], axis=1)
+    whole = dot3((tsplit[0], tsplit[1]), split(whole), NN)
+    own = [
+        jnp.concatenate([term(d7, 0, 7, 2 * p + half, 2 * z + k) for p in range(planes)], axis=1) for k in (0, 1)
+    ]
+    top[0], top[1] = split(whole + jnp.concatenate(own, axis=0))
 
 
 def low2_kernel(far, coupling, m0, m23, m4, behind, loc_b):
@@ -297,9 +317,11 @@
         part[:, at] = total
 
 
-def last_kernel(top, g7, part, g, out):
-    moments = jnp.concatenate([g7[i] for i in range(8)], axis=1)
-    field = dot3(split(moments), (top[0], top[1]), NN)
+def last_kernel(g7, part, g, out):
+    total = g7[0]
+    for i in range(1, g7.shape[0]):
+        total = total + g7[i]
+    field = jnp.concatenate([total[:, :64], total[:, 64:]], axis=0)
     high, low = split(field)
     both = jnp.concatenate([high, low], 0)
     step = 256
@@ -334,7 +356,7 @@
 
     def up4(own, masks, axis, copies, *behind):
         got = [swap(own, masks[i - 1]) for i in ORDER]
-        top = of((copies,) + pair.shape, F32) if copies else pair
+        top = of((copies, rhs // 2, 2 * rank), F32) if copies else pair
         return pl.pallas_call(
             lambda *refs: up4_kernel(copies, axis, refs),
             out_shape=(mat(12), top), in_specs=[VMEM] * (5 + len(behind)), out_specs=(VMEM,) * 2,
@@ -349,8 +371,8 @@
         )(own, swap(own, mask), tsplit, *sources)
 
     loc_a, top = pl.pallas_call(
-        low_kernel, out_shape=(mat(4), of((2, 16 * rank, rank), BF16)), in_specs=[VMEM] * 4, out_specs=(VMEM,) * 2,
-        scratch_shapes=[pltpu.VMEM((4, rank, rank), F32)] * 3,
+        low_kernel, out_shape=(mat(4), of((2, 2 * rank, lax.axis_size("z") * rank), BF16)), in_specs=[VMEM] * 4, out_specs=(VMEM,) * 2,
+        scratch_shapes=[pltpu.VMEM((n, rank, rank), F32) for n in (3, 3, 6)],
         name="low", compiler_params=PARAMS,
     )(far, coup, tsplit, m1)
     core, cross4 = swap(src, 4), swap_across(src, 4)
@@ -362,9 +384,10 @@
     )(far, coup, m0, m23, m4, pair5)
 
     shifted = shift(both)
-    m56, pair7 = up4(pair5, (8, 16, 24), "y", 8, loc_b)
+    m56, pair7 = up4(pair5, (8, 16, 24), "y", lax.axis_size("z"), top, loc_b)
     g7 = lax.all_to_all(pair7, "z", 0, 0, tiled=True)
-    other = swap(shifted[1], 4)
+    late = lax.optimization_barrier((shifted, m56))[0]
+    other = swap(late[1], 4)
 
     far_part, g, blocks = pl.pallas_call(
         mid_kernel,
@@ -389,9 +412,9 @@
     product = pl.pallas_call(
         last_kernel,
         out_shape=of((rhs, points), BF16),
-        in_specs=[VMEM] * 4, out_specs=VMEM,
+        in_specs=[VMEM] * 3, out_specs=VMEM,
         name="last", compiler_params=PARAMS,
-    )(top, g7, part, g)
+    )(g7, part, g)
     return product.T
 
 

time: 45.2 us -> 45.3 us (level)
  the two profiles are of different devices: /device:TPU:2 before, /device:TPU:1 now
where the time goes in v6:
time: 45.3 us; the launch traced here: 45.1 us
  starting transfers between devices  24.8 us (55%)
  Pallas kernels  13.7 us (30%)
  waiting for transfers between devices  6.46 us (14%)
    ppermute x9, starting transfers between devices, swap(): lax.ppermute(array, AXES, [(i, i ^ mask) for i in range(device_count())])  12.1 us
    all_to_all x1, starting transfers between devices, shards(): g7 = lax.all_to_all(pair7, 'z', 0, 0, tiled=True)  8.65 us
    ppermute x9, waiting for transfers between devices, swap(): lax.ppermute(array, AXES, [(i, i ^ mask) for i in range(device_count())])  4.01 us
    pallas_call x1, Pallas kernels, shards(): pl.pallas_call(mid_kernel, out_shape=(of((rhs, points), F32), of((2, rhs,...  3.64 us
    ppermute x1, starting transfers between devices, swap_across(): lax.ppermute(array, AXES, [(i, o if 0 <= o < n else i ^ 1) for i, o in en...  2.77 us
    all_to_all x1, waiting for transfers between devices, shards(): g7 = lax.all_to_all(pair7, 'z', 0, 0, tiled=True)  2.45 us
    pallas_call x1, Pallas kernels, shards(): pl.pallas_call(near_kernel, out_shape=of((rhs, points), F32), in_specs=[V...  2.38 us
    pallas_call x2, Pallas kernels, up4(): pl.pallas_call(lambda *refs: up4_kernel(copies, axis, refs), out_shape=(m...  1.97 us
  transfers between devices with their start and end apart: 12, of which 7 were waited for; matrix products, arithmetic and copies ran while one was open for 0% of the time, Pallas kernels for 23%

profile of v6, /device:TPU:1, one launch (start us, length us, event | category | flops | bytes accessed | tf_op | source)
XLA Modules:
  0.0 45.1 jit_solution(7224900428079605998)
XLA Ops:
  0.0 1.8 %leaf.1 = (bf16[64,2048]{1,0:T(8,128)(2,1)S(1)}, f32[3,64,64]{2,1,0:T(8,128)S(1)}, s32[3,4092]{1,0:T(4,128)S(1)}, bf16[2,128,64]{2,1,0:T(8,128)(2,1)S(1)}, f32[8...) custom-call(bf16[64,2048]{1,0:T(8,128)(2,1)} %bitcast.9, bf16[8,64,256]{2,1,0:T(8,128)(2,1)} %bitcast.7, ...), custom_call_target="tpu_custom_call" | custom-call | tf_op jit(solution)/shard_map/leaf/pallas_call | solution.py:346
  1.8 2.8 %collective-permute-start.4 = (bf16[64,2048]{1,0:T(8,128)(2,1)S(1)}, bf16[64,2048]{1,0:T(8,128)(2,1)S(1)}, u32[]{:S(2)}, u32[]{:S(2)}) collective-permute-start(bf16[64,2048]{1,0:T(8,128)(2,1)S(1)} %get-tuple-element.32.refs_3_), channel_id=1, source_target_pairs={{0,1},{1,0},{2,3},{3,2},{4,8},{5,9},{6,10},{7,11},{8,4},{9,5},{10,... | collective-permute-start | bytes 786440 | tf_op jit(solution)/shard_map/ppermute | solution.py:78
  4.6 0.7 %collective-permute-start.5 = (bf16[64,2048]{1,0:T(8,128)(2,1)S(1)}, bf16[64,2048]{1,0:T(8,128)(2,1)S(1)}, u32[]{:S(2)}, u32[]{:S(2)}) collective-permute-start(bf16[64,2048]{1,0:T(8,128)(2,1)S(1)} %get-tuple-element.32.refs_3_), channel_id=1, source_target_pairs={{0,4},{1,5},{2,6},{3,7},{4,0},{5,1},{6,2},{7,3},{8,12},{9,13},{10,... | collective-permute-start | bytes 786440 | tf_op jit(solution)/shard_map/ppermute | solution.py:68
  5.2 2.1 %collective-permute-start = (f32[64,128]{1,0:T(8,128)S(1)}, f32[64,128]{1,0:T(8,128)S(1)}, u32[]{:S(2)}, u32[]{:S(2)}) collective-permute-start(f32[64,128]{1,0:T(8,128)S(1)} %get-tuple-element.25.refs_0_), channel_id=1, source_target_pairs={{0,2},{1,3},{2,0},{3,1},{4,6},{5,7},{6,4},{7,5},{8,10},{9,11},{10,... | collective-permute-start | bytes 98312 | tf_op jit(solution)/shard_map/ppermute | solution.py:68
  7.4 0.3 collective-permute-start.1
  7.7 1.6 %collective-permute-start.2 = (f32[64,128]{1,0:T(8,128)S(1)}, f32[64,128]{1,0:T(8,128)S(1)}, u32[]{:S(2)}, u32[]{:S(2)}) collective-permute-start(f32[64,128]{1,0:T(8,128)S(1)} %get-tuple-element.25.refs_0_), channel_id=1, source_target_pairs={{0,3},{1,2},{2,1},{3,0},{4,7},{5,6},{6,5},{7,4},{8,11},{9,10},{10,... | collective-permute-start | bytes 98312 | tf_op jit(solution)/shard_map/ppermute | solution.py:68
  9.3 1.4 %low.1 = (f32[4,64,64]{2,1,0:T(8,128)S(1)}, bf16[2,128,512]{2,1,0:T(8,128)(2,1)S(1)}) custom-call(s32[3,4092]{1,0:T(4,128)S(1)} %get-tuple-element.27.far, f32[3,64,64]{2,1,0:T(8,128)S(1)} %get-tuple-element.28.coupling, bf16[2,128,64]{2,1,0:T(8,128)(2,1)S(1)} %get-tuple-element.26.tsplit.refs_4_.refs_2_, f32[4,64,64]{2,1,0:T(8,128)S(1)} %get-tuple-element.29.m1), custom_call_target="tpu_custom_call" | custom-call | tf_op jit(solution)/shard_map/low/pallas_call | solution.py:373
  10.7 0.0 collective-permute-done.refs_1_
  10.7 0.1 collective-permute-done.1.refs_2_
  10.8 0.8 %collective-permute-done.2.refs_3_ = f32[64,128]{1,0:T(8,128)S(1)} collective-permute-done((f32[64,128]{1,0:T(8,128)S(1)}, f32[64,128]{1,0:T(8,128)S(1)}, u32[]{:S(2)}, u32[]{:S(2)}) %collective-permute-start.2) | collective-permute-done | bytes 32800 | tf_op jit(solution)/shard_map/ppermute | solution.py:68
  11.6 0.5 %up4.2 = (f32[12,64,64]{2,1,0:T(8,128)S(1)}, f32[64,128]{1,0:T(8,128)S(1)}) custom-call(f32[64,128]{1,0:T(8,128)S(1)} %get-tuple-element.25.refs_0_, f32[64,128]{1,0:T(8,128)S(1)} %collective-permute-done.refs_1_, f32[64,128]{1,0:T(8,128)S(1)} %collective-permute-done.1.refs_2_, f32[64,128]{1,0:T(8,128)S(1)} %collective-permute-done.2.refs_3_, ...), custom_call_target="tpu_custom_call" | custom-call | tf_op jit(solution)/shard_map/up4/pallas_call | solution.py:360
  12.1 2.3 %collective-permute-start.3 = (f32[64,128]{1,0:T(8,128)S(1)}, f32[64,128]{1,0:T(8,128)S(1)}, u32[]{:S(2)}, u32[]{:S(2)}) collective-permute-start(f32[64,128]{1,0:T(8,128)S(1)} %get-tuple-element.31.refs_0_), channel_id=1, source_target_pairs={{0,4},{1,5},{2,6},{3,7},{4,0},{5,1},{6,2},{7,3},{8,12},{9,13},{10,... | collective-permute-start | bytes 98312 | tf_op jit(solution)/shard_map/ppermute | solution.py:68
  14.5 0.9 %collective-permute-done.3.refs_1_ = f32[64,128]{1,0:T(8,128)S(1)} collective-permute-done((f32[64,128]{1,0:T(8,128)S(1)}, f32[64,128]{1,0:T(8,128)S(1)}, u32[]{:S(2)}, u32[]{:S(2)}) %collective-permute-start.3) | collective-permute-done | bytes 32800 | tf_op jit(solution)/shard_map/ppermute | solution.py:68
  15.3 0.0 collective-permute-done.4.refs_4_.cross4
  15.3 0.0 collective-permute-done.5.refs_5_.core
  15.3 0.3 up2.1
  15.6 1.3 %collective-permute-start.9 = (bf16[2,64,2048]{2,1,0:T(8,128)(2,1)S(1)}, bf16[2,64,2048]{2,1,0:T(8,128)(2,1)S(1)}, u32[]{:S(2)}, u32[]{:S(2)}) collective-permute-start(bf16[2,64,2048]{2,1,0:T(8,128)(2,1)S(1)} %get-tuple-element.41), channel_id=1, source_target_pairs={{0,1},{1,2},{2,3},{3,0},{4,7},{5,4},{6,5},{7,6},{8,9},{9,10},{10,1... | collective-permute-start | bytes 1572872 | tf_op jit(solution)/shard_map/ppermute | solution.py:84
  16.9 1.7 %collective-permute-start.6 = (f32[64,128]{1,0:T(8,128)S(1)}, f32[64,128]{1,0:T(8,128)S(1)}, u32[]{:S(2)}, u32[]{:S(2)}) collective-permute-start(f32[64,128]{1,0:T(8,128)S(1)} %get-tuple-element.33.behind.refs_0_), channel_id=1, source_target_pairs={{0,16},{1,17},{2,18},{3,19},{4,20},{5,21},{6,22},{7,23},{8,24},{9,... | collective-permute-start | bytes 98312 | tf_op jit(solution)/shard_map/ppermute | solution.py:68
  18.6 0.7 %collective-permute-start.7 = (f32[64,128]{1,0:T(8,128)S(1)}, f32[64,128]{1,0:T(8,128)S(1)}, u32[]{:S(2)}, u32[]{:S(2)}) collective-permute-start(f32[64,128]{1,0:T(8,128)S(1)} %get-tuple-element.33.behind.refs_0_), channel_id=1, source_target_pairs={{0,8},{1,9},{2,10},{3,11},{4,12},{5,13},{6,14},{7,15},{8,0},{9,1},... | collective-permute-start | bytes 98312 | tf_op jit(solution)/shard_map/ppermute | solution.py:68
  19.3 0.9 %collective-permute-start.8 = (f32[64,128]{1,0:T(8,128)S(1)}, f32[64,128]{1,0:T(8,128)S(1)}, u32[]{:S(2)}, u32[]{:S(2)}) collective-permute-start(f32[64,128]{1,0:T(8,128)S(1)} %get-tuple-element.33.behind.refs_0_), channel_id=1, source_target_pairs={{0,24},{1,25},{2,26},{3,27},{4,28},{5,29},{6,30},{7,31},{8,16},{9,... | collective-permute-start | bytes 98312 | tf_op jit(solution)/shard_map/ppermute | solution.py:68
  20.2 1.1 %low2.1.refs_6_.loc_b = f32[12,64,64]{2,1,0:T(8,128)S(1)} custom-call(s32[3,4092]{1,0:T(4,128)S(1)} %get-tuple-element.27.far, f32[3,64,64]{2,1,0:T(8,128)S(1)} %get-tuple-element.28.coupling, f32[8,64,64]{2,1,0:T(8,128)S(1)} %get-tuple-element.35.m0, f32[12,64,64]{2,1,0:T(8,128)S(1)} %get-tuple-element.36.m23, f32[4,64,64]{2,1,0:T(8,128)S(1)} %get-tuple-element.37.m4, ...), custom_call_target="tpu_custom_call" | custom-call | tf_op jit(solution)/shard_map/low2/pallas_call | solution.py:381
  21.3 0.2 collective-permute-done.6.refs_1_
  21.4 0.5 %collective-permute-done.7.refs_2_ = f32[64,128]{1,0:T(8,128)S(1)} collective-permute-done((f32[64,128]{1,0:T(8,128)S(1)}, f32[64,128]{1,0:T(8,128)S(1)}, u32[]{:S(2)}, u32[]{:S(2)}) %collective-permute-start.7) | collective-permute-done | bytes 32800 | tf_op jit(solution)/shard_map/ppermute | solution.py:68
  22.0 1.6 %collective-permute-done.8.refs_3_ = f32[64,128]{1,0:T(8,128)S(1)} collective-permute-done((f32[64,128]{1,0:T(8,128)S(1)}, f32[64,128]{1,0:T(8,128)S(1)}, u32[]{:S(2)}, u32[]{:S(2)}) %collective-permute-start.8) | collective-permute-done | bytes 32800 | tf_op jit(solution)/shard_map/ppermute | solution.py:68
  23.5 1.5 %up4.3 = (f32[12,64,64]{2,1,0:T(8,128)S(1)}, f32[8,32,128]{2,1,0:T(8,128)}) custom-call(f32[64,128]{1,0:T(8,128)S(1)} %get-tuple-element.33.behind.refs_0_, f32[64,128]{1,0:T(8,128)S(1)} %collective-permute-done.6.refs_1_, f32[64,128]{1,0:T(8,128)S(1)} %collective-permute-done.7.refs_2_, f32[64,128]{1,0:T(8,128)S(1)} %collective-permute-done.8.refs_3_, ...), custom_call_target="tpu_custom_call" | custom-call | tf_op jit(solution)/shard_map/up4/pallas_call | solution.py:360
  25.0 0.0 collective-permute-done.9.shifted
  25.0 1.8 %collective-permute-start.10 = (bf16[64,2048]{1,0:T(8,128)(2,1)S(1)}, bf16[64,2048]{1,0:T(8,128)(2,1)S(1)}, u32[]{:S(2)}, u32[]{:S(2)}) collective-permute-start(bf16[64,2048]{1,0:T(8,128)(2,1)S(1)} %slice_bitcast_fusion), channel_id=1, source_target_pairs={{0,4},{1,5},{2,6},{3,7},{4,0},{5,1},{6,2},{7,3},{8,12},{9,13},{10,... | collective-permute-start | bytes 786440 | tf_op jit(solution)/shard_map/ppermute | solution.py:68
  26.8 8.7 %all-to-all-start = ((f32[8,32,128]{2,1,0:T(8,128)}), f32[8,32,128]{2,1,0:T(8,128)S(1)}, u32[]{:S(2)}, u32[]{:S(2)}) async-start(f32[8,32,128]{2,1,0:T(8,128)} %get-tuple-element.38), calls=%async_computation | async-start | bytes 262144 | tf_op jit(solution)/shard_map/all_to_all | solution.py:388
  35.5 3.6 %mid.1 = (f32[64,2048]{1,0:T(8,128)S(1)}, bf16[2,64,2048]{2,1,0:T(8,128)(2,1)S(1)}, bf16[8,4,256,256]{3,2,1,0:T(8,128)(2,1)S(1)}) custom-call(s32[3,4092]{1,0:T(4,128)S(1)} %get-tuple-element.27.far, f32[3,64,64]{2,1,0:T(8,128)S(1)} %get-tuple-element.28.coupling, bf16[2,128,64]{2,1,0:T(8,128)(2,1)S(1)} %get-tuple-element.26.tsplit.refs_4_.refs_2_, ...), custom_call_target="tpu_custom_call" | custom-call | tf_op jit(solution)/shard_map/mid/pallas_call | solution.py:392
  39.1 0.0 collective-permute-done.10.other
  39.1 2.4 %near.1.part = f32[64,2048]{1,0:T(8,128)S(1)} custom-call(f32[64,2048]{1,0:T(8,128)S(1)} %get-tuple-element.40.far_part, bf16[64,2048]{1,0:T(8,128)(2,1)S(1)} %collective-permute-done.5.refs_5_.core, bf16[64,2048]{1,0:T(8,128)(2,1)S(1)} %collective-permute-done.4.refs_4_.cross4, bf16[2,64,2048]{2,1,0:T(8,128)(2,1)S(1)} %collective-permute-done.9.shifted, ...), custom_call_target="tpu_custom_call" | custom-call | tf_op jit(solution)/shard_map/near/pallas_call | solution.py:399
  41.5 2.4 %all-to-all-done.g7 = f32[8,32,128]{2,1,0:T(8,128)S(1)} async-done(((f32[8,32,128]{2,1,0:T(8,128)}), f32[8,32,128]{2,1,0:T(8,128)S(1)}, u32[]{:S(2)}, u32[]{:S(2)}) %all-to-all-start) | async-done | bytes 131104 | tf_op jit(solution)/shard_map/all_to_all | solution.py:388
  44.0 1.1 %last.1 = bf16[64,2048]{1,0:T(8,128)(2,1)} custom-call(f32[8,32,128]{2,1,0:T(8,128)S(1)} %all-to-all-done.g7, f32[64,2048]{1,0:T(8,128)S(1)} %near.1.part, bf16[2,64,2048]{2,1,0:T(8,128)(2,1)S(1)} %get-tuple-element.44.g), custom_call_target="tpu_custom_call" | custom-call | tf_op jit(solution)/shard_map/last/pallas_call | solution.py:412
  (1 shorter events, 0.0 us)
Async XLA Ops:
  1.8 13.5 %collective-permute-start.4 = (bf16[64,2048]{1,0:T(8,128)(2,1)S(1)}, bf16[64,2048]{1,0:T(8,128)(2,1)S(1)}, u32[]{:S(2)}, u32[]{:S(2)}) collective-permute-start(bf16[64,2048]{1,0:T(8,128)(2,1)S(1)} %get-tuple-element.32.refs_3_), channel_id=1, source_target_pairs={{0,1},{1,0},{2,3},{3,2},{4,8},{5,9},{6,10},{7,11},{8,4},{9,5},{10,... | collective-permute-start | bytes 786440 | tf_op jit(solution)/shard_map/ppermute | solution.py:78
  4.6 10.7 %collective-permute-start.5 = (bf16[64,2048]{1,0:T(8,128)(2,1)S(1)}, bf16[64,2048]{1,0:T(8,128)(2,1)S(1)}, u32[]{:S(2)}, u32[]{:S(2)}) collective-permute-start(bf16[64,2048]{1,0:T(8,128)(2,1)S(1)} %get-tuple-element.32.refs_3_), channel_id=1, source_target_pairs={{0,4},{1,5},{2,6},{3,7},{4,0},{5,1},{6,2},{7,3},{8,12},{9,13},{10,... | collective-permute-start | bytes 786440 | tf_op jit(solution)/shard_map/ppermute | solution.py:68
  5.2 5.5 %collective-permute-start = (f32[64,128]{1,0:T(8,128)S(1)}, f32[64,128]{1,0:T(8,128)S(1)}, u32[]{:S(2)}, u32[]{:S(2)}) collective-permute-start(f32[64,128]{1,0:T(8,128)S(1)} %get-tuple-element.25.refs_0_), channel_id=1, source_target_pairs={{0,2},{1,3},{2,0},{3,1},{4,6},{5,7},{6,4},{7,5},{8,10},{9,11},{10,... | collective-permute-start | bytes 98312 | tf_op jit(solution)/shard_map/ppermute | solution.py:68
  7.4 3.5 %collective-permute-start.1 = (f32[64,128]{1,0:T(8,128)S(1)}, f32[64,128]{1,0:T(8,128)S(1)}, u32[]{:S(2)}, u32[]{:S(2)}) collective-permute-start(f32[64,128]{1,0:T(8,128)S(1)} %get-tuple-element.25.refs_0_), channel_id=1, source_target_pairs={{0,1},{1,0},{2,3},{3,2},{4,5},{5,4},{6,7},{7,6},{8,9},{9,8},{10,11... | collective-permute-start | bytes 98312 | tf_op jit(solution)/shard_map/ppermute | solution.py:68
  7.7 4.0 %collective-permute-start.2 = (f32[64,128]{1,0:T(8,128)S(1)}, f32[64,128]{1,0:T(8,128)S(1)}, u32[]{:S(2)}, u32[]{:S(2)}) collective-permute-start(f32[64,128]{1,0:T(8,128)S(1)} %get-tuple-element.25.refs_0_), channel_id=1, source_target_pairs={{0,3},{1,2},{2,1},{3,0},{4,7},{5,6},{6,5},{7,4},{8,11},{9,10},{10,... | collective-permute-start | bytes 98312 | tf_op jit(solution)/shard_map/ppermute | solution.py:68
  12.1 3.2 %collective-permute-start.3 = (f32[64,128]{1,0:T(8,128)S(1)}, f32[64,128]{1,0:T(8,128)S(1)}, u32[]{:S(2)}, u32[]{:S(2)}) collective-permute-start(f32[64,128]{1,0:T(8,128)S(1)} %get-tuple-element.31.refs_0_), channel_id=1, source_target_pairs={{0,4},{1,5},{2,6},{3,7},{4,0},{5,1},{6,2},{7,3},{8,12},{9,13},{10,... | collective-permute-start | bytes 98312 | tf_op jit(solution)/shard_map/ppermute | solution.py:68
  15.6 9.4 %collective-permute-start.9 = (bf16[2,64,2048]{2,1,0:T(8,128)(2,1)S(1)}, bf16[2,64,2048]{2,1,0:T(8,128)(2,1)S(1)}, u32[]{:S(2)}, u32[]{:S(2)}) collective-permute-start(bf16[2,64,2048]{2,1,0:T(8,128)(2,1)S(1)} %get-tuple-element.41), channel_id=1, source_target_pairs={{0,1},{1,2},{2,3},{3,0},{4,7},{5,4},{6,5},{7,6},{8,9},{9,10},{10,1... | collective-permute-start | bytes 1572872 | tf_op jit(solution)/shard_map/ppermute | solution.py:84
  16.9 4.6 %collective-permute-start.6 = (f32[64,128]{1,0:T(8,128)S(1)}, f32[64,128]{1,0:T(8,128)S(1)}, u32[]{:S(2)}, u32[]{:S(2)}) collective-permute-start(f32[64,128]{1,0:T(8,128)S(1)} %get-tuple-element.33.behind.refs_0_), channel_id=1, source_target_pairs={{0,16},{1,17},{2,18},{3,19},{4,20},{5,21},{6,22},{7,23},{8,24},{9,... | collective-permute-start | bytes 98312 | tf_op jit(solution)/shard_map/ppermute | solution.py:68
  18.6 3.4 %collective-permute-start.7 = (f32[64,128]{1,0:T(8,128)S(1)}, f32[64,128]{1,0:T(8,128)S(1)}, u32[]{:S(2)}, u32[]{:S(2)}) collective-permute-start(f32[64,128]{1,0:T(8,128)S(1)} %get-tuple-element.33.behind.refs_0_), channel_id=1, source_target_pairs={{0,8},{1,9},{2,10},{3,11},{4,12},{5,13},{6,14},{7,15},{8,0},{9,1},... | collective-permute-start | bytes 98312 | tf_op jit(solution)/shard_map/ppermute | solution.py:68
  19.3 4.3 %collective-permute-start.8 = (f32[64,128]{1,0:T(8,128)S(1)}, f32[64,128]{1,0:T(8,128)S(1)}, u32[]{:S(2)}, u32[]{:S(2)}) collective-permute-start(f32[64,128]{1,0:T(8,128)S(1)} %get-tuple-element.33.behind.refs_0_), channel_id=1, source_target_pairs={{0,24},{1,25},{2,26},{3,27},{4,28},{5,29},{6,30},{7,31},{8,16},{9,... | collective-permute-start | bytes 98312 | tf_op jit(solution)/shard_map/ppermute | solution.py:68
  25.0 14.1 %collective-permute-start.10 = (bf16[64,2048]{1,0:T(8,128)(2,1)S(1)}, bf16[64,2048]{1,0:T(8,128)(2,1)S(1)}, u32[]{:S(2)}, u32[]{:S(2)}) collective-permute-start(bf16[64,2048]{1,0:T(8,128)(2,1)S(1)} %slice_bitcast_fusion), channel_id=1, source_target_pairs={{0,4},{1,5},{2,6},{3,7},{4,0},{5,1},{6,2},{7,3},{8,12},{9,13},{10,... | collective-permute-start | bytes 786440 | tf_op jit(solution)/shard_map/ppermute | solution.py:68
  26.8 17.1 %all-to-all-start = ((f32[8,32,128]{2,1,0:T(8,128)}), f32[8,32,128]{2,1,0:T(8,128)S(1)}, u32[]{:S(2)}, u32[]{:S(2)}) async-start(f32[8,32,128]{2,1,0:T(8,128)} %get-tuple-element.38), calls=%async_computation | async-start | bytes 262144 | tf_op jit(solution)/shard_map/all_to_all | solution.py:388

commit v7 on v5

--- a/solution.py
+++ b/solution.py
@@ -74,8 +74,8 @@
 
 def swap_across(array, step):
     n = device_count()
-    pairs = [(i, (i + (step if i & step else n - step)) % n) for i in range(n)]
-    return lax.ppermute(array, AXES, pairs)
+    others = [i + step if i & step else i - step for i in range(n)]
+    return lax.ppermute(array, AXES, [(i, o if 0 <= o < n else i ^ 1) for i, o in enumerate(others)])
 
 
 def shift(array):

time: 45.2 us -> 45.2 us (level)
  waiting for transfers between devices: 10.1 us -> 11.5 us
  starting transfers between devices: 21 us -> 19.6 us
    ppermute x1, starting transfers between devices: 7.84 us -> 2.36 us  [swap_across(): lax.ppermute(array, AXES, [(i, o if 0 <= o < n else i ^ 1) for i, o in en...]
    all_to_all x1, starting transfers between devices: 4.19 us -> 7.72 us  [shards(): g7 = lax.all_to_all(pair7, 'z', 0, 0, tiled=True)]
    ppermute x9, waiting for transfers between devices: 4.32 us -> 5.69 us  [swap(): lax.ppermute(array, AXES, [(i, i ^ mask) for i in range(device_count())])]
    ppermute x1, starting transfers between devices: 0.61 us -> 1.19 us  [shift(): lax.ppermute(array, AXES, [(i, i // span * span + (i + step(i)) % span) f...]
where the time goes in v7:
time: 45.2 us; the launch traced here: 45 us
  starting transfers between devices  19.6 us (43%)
  Pallas kernels  13.8 us (31%)
  waiting for transfers between devices  11.5 us (25%)
    ppermute x9, starting transfers between devices, swap(): lax.ppermute(array, AXES, [(i, i ^ mask) for i in range(device_count())])  8.37 us
    all_to_all x1, starting transfers between devices, shards(): g7 = lax.all_to_all(pair7, 'z', 0, 0, tiled=True)  7.72 us
    all_to_all x1, waiting for transfers between devices, shards(): g7 = lax.all_to_all(pair7, 'z', 0, 0, tiled=True)  5.78 us
    ppermute x9, waiting for transfers between devices, swap(): lax.ppermute(array, AXES, [(i, i ^ mask) for i in range(device_count())])  5.69 us
    pallas_call x1, Pallas kernels, shards(): pl.pallas_call(mid_kernel, out_shape=(of((rhs, points), F32), of((2, rhs,...  3.65 us
    pallas_call x1, Pallas kernels, shards(): pl.pallas_call(near_kernel, out_shape=of((rhs, points), F32), in_specs=[V...  2.38 us
    ppermute x1, starting transfers between devices, swap_across(): lax.ppermute(array, AXES, [(i, o if 0 <= o < n else i ^ 1) for i, o in en...  2.36 us
    pallas_call x1, Pallas kernels, shards(): pl.pallas_call(leaf_kernel, out_shape=(of(src_in.shape, BF16), of(couplin...  1.81 us
  transfers between devices with their start and end apart: 12, of which 7 were waited for; matrix products, arithmetic and copies ran while one was open for 0% of the time, Pallas kernels for 23%

profile of v7, /device:TPU:2, one launch (start us, length us, event | category | flops | bytes accessed | tf_op | source)
XLA Modules:
  0.0 45.0 jit_solution(9424660365863549039)
XLA Ops:
  0.0 1.8 %leaf.1 = (bf16[64,2048]{1,0:T(8,128)(2,1)S(1)}, f32[3,64,64]{2,1,0:T(8,128)S(1)}, s32[3,4092]{1,0:T(4,128)S(1)}, bf16[2,128,64]{2,1,0:T(8,128)(2,1)S(1)}, f32[8...) custom-call(bf16[64,2048]{1,0:T(8,128)(2,1)} %bitcast.9, bf16[8,64,256]{2,1,0:T(8,128)(2,1)} %bitcast.7, ...), custom_call_target="tpu_custom_call" | custom-call | tf_op jit(solution)/shard_map/leaf/pallas_call | solution.py:324
  1.8 2.4 %collective-permute-start.4 = (bf16[64,2048]{1,0:T(8,128)(2,1)S(1)}, bf16[64,2048]{1,0:T(8,128)(2,1)S(1)}, u32[]{:S(2)}, u32[]{:S(2)}) collective-permute-start(bf16[64,2048]{1,0:T(8,128)(2,1)S(1)} %get-tuple-element.32.refs_3_), channel_id=1, source_target_pairs={{0,1},{1,0},{2,3},{3,2},{4,8},{5,9},{6,10},{7,11},{8,4},{9,5},{10,... | collective-permute-start | bytes 786440 | tf_op jit(solution)/shard_map/ppermute | solution.py:78
  4.2 0.0 collective-permute-start.5
  4.2 1.5 %collective-permute-start = (f32[64,128]{1,0:T(8,128)S(1)}, f32[64,128]{1,0:T(8,128)S(1)}, u32[]{:S(2)}, u32[]{:S(2)}) collective-permute-start(f32[64,128]{1,0:T(8,128)S(1)} %get-tuple-element.29.refs_0_), channel_id=1, source_target_pairs={{0,2},{1,3},{2,0},{3,1},{4,6},{5,7},{6,4},{7,5},{8,10},{9,11},{10,... | collective-permute-start | bytes 98312 | tf_op jit(solution)/shard_map/ppermute | solution.py:68
  5.7 1.4 %collective-permute-start.1 = (f32[64,128]{1,0:T(8,128)S(1)}, f32[64,128]{1,0:T(8,128)S(1)}, u32[]{:S(2)}, u32[]{:S(2)}) collective-permute-start(f32[64,128]{1,0:T(8,128)S(1)} %get-tuple-element.29.refs_0_), channel_id=1, source_target_pairs={{0,1},{1,0},{2,3},{3,2},{4,5},{5,4},{6,7},{7,6},{8,9},{9,8},{10,11... | collective-permute-start | bytes 98312 | tf_op jit(solution)/shard_map/ppermute | solution.py:68
  7.2 1.1 %collective-permute-start.2 = (f32[64,128]{1,0:T(8,128)S(1)}, f32[64,128]{1,0:T(8,128)S(1)}, u32[]{:S(2)}, u32[]{:S(2)}) collective-permute-start(f32[64,128]{1,0:T(8,128)S(1)} %get-tuple-element.29.refs_0_), channel_id=1, source_target_pairs={{0,3},{1,2},{2,1},{3,0},{4,7},{5,6},{6,5},{7,4},{8,11},{9,10},{10,... | collective-permute-start | bytes 98312 | tf_op jit(solution)/shard_map/ppermute | solution.py:68
  8.3 1.5 %low.1 = (f32[4,64,64]{2,1,0:T(8,128)S(1)}, bf16[2,1024,64]{2,1,0:T(8,128)(2,1)S(1)}) custom-call(s32[3,4092]{1,0:T(4,128)S(1)} %get-tuple-element.24.far, f32[3,64,64]{2,1,0:T(8,128)S(1)} %get-tuple-element.25.coupling, bf16[2,128,64]{2,1,0:T(8,128)(2,1)S(1)} %get-tuple-element.26.tsplit.refs_4_.refs_2_, f32[4,64,64]{2,1,0:T(8,128)S(1)} %get-tuple-element.27.m1), custom_call_target="tpu_custom_call" | custom-call | tf_op jit(solution)/shard_map/low/pallas_call | solution.py:351
  9.8 0.5 %collective-permute-done.refs_1_ = f32[64,128]{1,0:T(8,128)S(1)} collective-permute-done((f32[64,128]{1,0:T(8,128)S(1)}, f32[64,128]{1,0:T(8,128)S(1)}, u32[]{:S(2)}, u32[]{:S(2)}) %collective-permute-start) | collective-permute-done | bytes 32800 | tf_op jit(solution)/shard_map/ppermute | solution.py:68
  10.3 0.0 collective-permute-done.1.refs_2_
  10.3 0.8 %collective-permute-done.2.refs_3_ = f32[64,128]{1,0:T(8,128)S(1)} collective-permute-done((f32[64,128]{1,0:T(8,128)S(1)}, f32[64,128]{1,0:T(8,128)S(1)}, u32[]{:S(2)}, u32[]{:S(2)}) %collective-permute-start.2) | collective-permute-done | bytes 32800 | tf_op jit(solution)/shard_map/ppermute | solution.py:68
  11.1 0.5 %up4.2 = (f32[12,64,64]{2,1,0:T(8,128)S(1)}, f32[64,128]{1,0:T(8,128)S(1)}) custom-call(f32[64,128]{1,0:T(8,128)S(1)} %get-tuple-element.29.refs_0_, f32[64,128]{1,0:T(8,128)S(1)} %collective-permute-done.refs_1_, f32[64,128]{1,0:T(8,128)S(1)} %collective-permute-done.1.refs_2_, f32[64,128]{1,0:T(8,128)S(1)} %collective-permute-done.2.refs_3_, ...), custom_call_target="tpu_custom_call" | custom-call | tf_op jit(solution)/shard_map/up4/pallas_call | solution.py:338
  11.6 0.1 collective-permute-start.3
  11.7 1.2 %collective-permute-done.3.refs_1_ = f32[64,128]{1,0:T(8,128)S(1)} collective-permute-done((f32[64,128]{1,0:T(8,128)S(1)}, f32[64,128]{1,0:T(8,128)S(1)}, u32[]{:S(2)}, u32[]{:S(2)}) %collective-permute-start.3) | collective-permute-done | bytes 32800 | tf_op jit(solution)/shard_map/ppermute | solution.py:68
  12.9 0.0 collective-permute-done.4.refs_4_.cross4
  12.9 0.0 collective-permute-done.5.refs_5_.core
  12.9 0.3 up2.1
  13.2 1.2 %collective-permute-start.9 = (bf16[2,64,2048]{2,1,0:T(8,128)(2,1)S(1)}, bf16[2,64,2048]{2,1,0:T(8,128)(2,1)S(1)}, u32[]{:S(2)}, u32[]{:S(2)}) collective-permute-start(bf16[2,64,2048]{2,1,0:T(8,128)(2,1)S(1)} %get-tuple-element.40), channel_id=1, source_target_pairs={{0,1},{1,2},{2,3},{3,0},{4,7},{5,4},{6,5},{7,6},{8,9},{9,10},{10,1... | collective-permute-start | bytes 1572872 | tf_op jit(solution)/shard_map/ppermute | solution.py:84
  14.4 2.3 %collective-permute-start.6 = (f32[64,128]{1,0:T(8,128)S(1)}, f32[64,128]{1,0:T(8,128)S(1)}, u32[]{:S(2)}, u32[]{:S(2)}) collective-permute-start(f32[64,128]{1,0:T(8,128)S(1)} %get-tuple-element.33.behind.refs_0_), channel_id=1, source_target_pairs={{0,16},{1,17},{2,18},{3,19},{4,20},{5,21},{6,22},{7,23},{8,24},{9,... | collective-permute-start | bytes 98312 | tf_op jit(solution)/shard_map/ppermute | solution.py:68
  16.7 1.0 %collective-permute-start.7 = (f32[64,128]{1,0:T(8,128)S(1)}, f32[64,128]{1,0:T(8,128)S(1)}, u32[]{:S(2)}, u32[]{:S(2)}) collective-permute-start(f32[64,128]{1,0:T(8,128)S(1)} %get-tuple-element.33.behind.refs_0_), channel_id=1, source_target_pairs={{0,8},{1,9},{2,10},{3,11},{4,12},{5,13},{6,14},{7,15},{8,0},{9,1},... | collective-permute-start | bytes 98312 | tf_op jit(solution)/shard_map/ppermute | solution.py:68
  17.7 0.8 %collective-permute-start.8 = (f32[64,128]{1,0:T(8,128)S(1)}, f32[64,128]{1,0:T(8,128)S(1)}, u32[]{:S(2)}, u32[]{:S(2)}) collective-permute-start(f32[64,128]{1,0:T(8,128)S(1)} %get-tuple-element.33.behind.refs_0_), channel_id=1, source_target_pairs={{0,24},{1,25},{2,26},{3,27},{4,28},{5,29},{6,30},{7,31},{8,16},{9,... | collective-permute-start | bytes 98312 | tf_op jit(solution)/shard_map/ppermute | solution.py:68
  18.5 1.1 %low2.1.refs_5_.loc_b = f32[12,64,64]{2,1,0:T(8,128)S(1)} custom-call(s32[3,4092]{1,0:T(4,128)S(1)} %get-tuple-element.24.far, f32[3,64,64]{2,1,0:T(8,128)S(1)} %get-tuple-element.25.coupling, f32[8,64,64]{2,1,0:T(8,128)S(1)} %get-tuple-element.34.m0, f32[12,64,64]{2,1,0:T(8,128)S(1)} %get-tuple-element.35.m23, f32[4,64,64]{2,1,0:T(8,128)S(1)} %get-tuple-element.36.m4, ...), custom_call_target="tpu_custom_call" | custom-call | tf_op jit(solution)/shard_map/low2/pallas_call | solution.py:359
  19.6 0.2 collective-permute-done.6.refs_1_
  19.8 1.0 %collective-permute-done.7.refs_2_ = f32[64,128]{1,0:T(8,128)S(1)} collective-permute-done((f32[64,128]{1,0:T(8,128)S(1)}, f32[64,128]{1,0:T(8,128)S(1)}, u32[]{:S(2)}, u32[]{:S(2)}) %collective-permute-start.7) | collective-permute-done | bytes 32800 | tf_op jit(solution)/shard_map/ppermute | solution.py:68
  20.8 2.0 %collective-permute-done.8.refs_3_ = f32[64,128]{1,0:T(8,128)S(1)} collective-permute-done((f32[64,128]{1,0:T(8,128)S(1)}, f32[64,128]{1,0:T(8,128)S(1)}, u32[]{:S(2)}, u32[]{:S(2)}) %collective-permute-start.8) | collective-permute-done | bytes 32800 | tf_op jit(solution)/shard_map/ppermute | solution.py:68
  22.8 1.2 %up4.3 = (f32[12,64,64]{2,1,0:T(8,128)S(1)}, f32[8,64,128]{2,1,0:T(8,128)}) custom-call(f32[64,128]{1,0:T(8,128)S(1)} %get-tuple-element.33.behind.refs_0_, f32[64,128]{1,0:T(8,128)S(1)} %collective-permute-done.6.refs_1_, f32[64,128]{1,0:T(8,128)S(1)} %collective-permute-done.7.refs_2_, f32[64,128]{1,0:T(8,128)S(1)} %collective-permute-done.8.refs_3_, ...), custom_call_target="tpu_custom_call" | custom-call | tf_op jit(solution)/shard_map/up4/pallas_call | solution.py:338
  24.0 7.7 %all-to-all-start = ((f32[8,64,128]{2,1,0:T(8,128)}), f32[8,64,128]{2,1,0:T(8,128)S(1)}, u32[]{:S(2)}, u32[]{:S(2)}) async-start(f32[8,64,128]{2,1,0:T(8,128)} %get-tuple-element.37), calls=%async_computation | async-start | bytes 524288 | tf_op jit(solution)/shard_map/all_to_all | solution.py:366
  31.7 0.0 collective-permute-done.9.shifted
  31.8 0.1 collective-permute-start.10
  31.9 3.6 %mid.1 = (f32[64,2048]{1,0:T(8,128)S(1)}, bf16[2,64,2048]{2,1,0:T(8,128)(2,1)S(1)}, bf16[8,4,256,256]{3,2,1,0:T(8,128)(2,1)S(1)}) custom-call(s32[3,4092]{1,0:T(4,128)S(1)} %get-tuple-element.24.far, f32[3,64,64]{2,1,0:T(8,128)S(1)} %get-tuple-element.25.coupling, bf16[2,128,64]{2,1,0:T(8,128)(2,1)S(1)} %get-tuple-element.26.tsplit.refs_4_.refs_2_, ...), custom_call_target="tpu_custom_call" | custom-call | tf_op jit(solution)/shard_map/mid/pallas_call | solution.py:369
  35.5 0.0 collective-permute-done.10.other
  35.5 2.4 %near.1.part = f32[64,2048]{1,0:T(8,128)S(1)} custom-call(f32[64,2048]{1,0:T(8,128)S(1)} %get-tuple-element.39.far_part, bf16[64,2048]{1,0:T(8,128)(2,1)S(1)} %collective-permute-done.5.refs_5_.core, bf16[64,2048]{1,0:T(8,128)(2,1)S(1)} %collective-permute-done.4.refs_4_.cross4, bf16[2,64,2048]{2,1,0:T(8,128)(2,1)S(1)} %collective-permute-done.9.shifted, ...), custom_call_target="tpu_custom_call" | custom-call | tf_op jit(solution)/shard_map/near/pallas_call | solution.py:376
  37.9 5.8 %all-to-all-done.g7 = f32[8,64,128]{2,1,0:T(8,128)S(1)} async-done(((f32[8,64,128]{2,1,0:T(8,128)}), f32[8,64,128]{2,1,0:T(8,128)S(1)}, u32[]{:S(2)}, u32[]{:S(2)}) %all-to-all-start) | async-done | bytes 262176 | tf_op jit(solution)/shard_map/all_to_all | solution.py:366
  43.7 1.3 %last.1 = bf16[64,2048]{1,0:T(8,128)(2,1)} custom-call(bf16[2,1024,64]{2,1,0:T(8,128)(2,1)S(1)} %get-tuple-element.28.top, f32[8,64,128]{2,1,0:T(8,128)S(1)} %all-to-all-done.g7, f32[64,2048]{1,0:T(8,128)S(1)} %near.1.part, bf16[2,64,2048]{2,1,0:T(8,128)(2,1)S(1)} %get-tuple-element.42.g), custom_call_target="tpu_custom_call" | custom-call | tf_op jit(solution)/shard_map/last/pallas_call | solution.py:389
  (1 shorter events, 0.0 us)
Async XLA Ops:
  1.8 11.1 %collective-permute-start.4 = (bf16[64,2048]{1,0:T(8,128)(2,1)S(1)}, bf16[64,2048]{1,0:T(8,128)(2,1)S(1)}, u32[]{:S(2)}, u32[]{:S(2)}) collective-permute-start(bf16[64,2048]{1,0:T(8,128)(2,1)S(1)} %get-tuple-element.32.refs_3_), channel_id=1, source_target_pairs={{0,1},{1,0},{2,3},{3,2},{4,8},{5,9},{6,10},{7,11},{8,4},{9,5},{10,... | collective-permute-start | bytes 786440 | tf_op jit(solution)/shard_map/ppermute | solution.py:78
  4.2 8.7 %collective-permute-start.5 = (bf16[64,2048]{1,0:T(8,128)(2,1)S(1)}, bf16[64,2048]{1,0:T(8,128)(2,1)S(1)}, u32[]{:S(2)}, u32[]{:S(2)}) collective-permute-start(bf16[64,2048]{1,0:T(8,128)(2,1)S(1)} %get-tuple-element.32.refs_3_), channel_id=1, source_target_pairs={{0,4},{1,5},{2,6},{3,7},{4,0},{5,1},{6,2},{7,3},{8,12},{9,13},{10,... | collective-permute-start | bytes 786440 | tf_op jit(solution)/shard_map/ppermute | solution.py:68
  4.2 6.1 %collective-permute-start = (f32[64,128]{1,0:T(8,128)S(1)}, f32[64,128]{1,0:T(8,128)S(1)}, u32[]{:S(2)}, u32[]{:S(2)}) collective-permute-start(f32[64,128]{1,0:T(8,128)S(1)} %get-tuple-element.29.refs_0_), channel_id=1, source_target_pairs={{0,2},{1,3},{2,0},{3,1},{4,6},{5,7},{6,4},{7,5},{8,10},{9,11},{10,... | collective-permute-start | bytes 98312 | tf_op jit(solution)/shard_map/ppermute | solution.py:68
  5.7 4.5 %collective-permute-start.1 = (f32[64,128]{1,0:T(8,128)S(1)}, f32[64,128]{1,0:T(8,128)S(1)}, u32[]{:S(2)}, u32[]{:S(2)}) collective-permute-start(f32[64,128]{1,0:T(8,128)S(1)} %get-tuple-element.29.refs_0_), channel_id=1, source_target_pairs={{0,1},{1,0},{2,3},{3,2},{4,5},{5,4},{6,7},{7,6},{8,9},{9,8},{10,11... | collective-permute-start | bytes 98312 | tf_op jit(solution)/shard_map/ppermute | solution.py:68
  7.2 3.9 %collective-permute-start.2 = (f32[64,128]{1,0:T(8,128)S(1)}, f32[64,128]{1,0:T(8,128)S(1)}, u32[]{:S(2)}, u32[]{:S(2)}) collective-permute-start(f32[64,128]{1,0:T(8,128)S(1)} %get-tuple-element.29.refs_0_), channel_id=1, source_target_pairs={{0,3},{1,2},{2,1},{3,0},{4,7},{5,6},{6,5},{7,4},{8,11},{9,10},{10,... | collective-permute-start | bytes 98312 | tf_op jit(solution)/shard_map/ppermute | solution.py:68
  11.6 1.3 %collective-permute-start.3 = (f32[64,128]{1,0:T(8,128)S(1)}, f32[64,128]{1,0:T(8,128)S(1)}, u32[]{:S(2)}, u32[]{:S(2)}) collective-permute-start(f32[64,128]{1,0:T(8,128)S(1)} %get-tuple-element.31.refs_0_), channel_id=1, source_target_pairs={{0,4},{1,5},{2,6},{3,7},{4,0},{5,1},{6,2},{7,3},{8,12},{9,13},{10,... | collective-permute-start | bytes 98312 | tf_op jit(solution)/shard_map/ppermute | solution.py:68
  13.2 18.6 %collective-permute-start.9 = (bf16[2,64,2048]{2,1,0:T(8,128)(2,1)S(1)}, bf16[2,64,2048]{2,1,0:T(8,128)(2,1)S(1)}, u32[]{:S(2)}, u32[]{:S(2)}) collective-permute-start(bf16[2,64,2048]{2,1,0:T(8,128)(2,1)S(1)} %get-tuple-element.40), channel_id=1, source_target_pairs={{0,1},{1,2},{2,3},{3,0},{4,7},{5,4},{6,5},{7,6},{8,9},{9,10},{10,1... | collective-permute-start | bytes 1572872 | tf_op jit(solution)/shard_map/ppermute | solution.py:84
  14.4 5.4 %collective-permute-start.6 = (f32[64,128]{1,0:T(8,128)S(1)}, f32[64,128]{1,0:T(8,128)S(1)}, u32[]{:S(2)}, u32[]{:S(2)}) collective-permute-start(f32[64,128]{1,0:T(8,128)S(1)} %get-tuple-element.33.behind.refs_0_), channel_id=1, source_target_pairs={{0,16},{1,17},{2,18},{3,19},{4,20},{5,21},{6,22},{7,23},{8,24},{9,... | collective-permute-start | bytes 98312 | tf_op jit(solution)/shard_map/ppermute | solution.py:68
  16.7 4.1 %collective-permute-start.7 = (f32[64,128]{1,0:T(8,128)S(1)}, f32[64,128]{1,0:T(8,128)S(1)}, u32[]{:S(2)}, u32[]{:S(2)}) collective-permute-start(f32[64,128]{1,0:T(8,128)S(1)} %get-tuple-element.33.behind.refs_0_), channel_id=1, source_target_pairs={{0,8},{1,9},{2,10},{3,11},{4,12},{5,13},{6,14},{7,15},{8,0},{9,1},... | collective-permute-start | bytes 98312 | tf_op jit(solution)/shard_map/ppermute | solution.py:68
  17.7 5.1 %collective-permute-start.8 = (f32[64,128]{1,0:T(8,128)S(1)}, f32[64,128]{1,0:T(8,128)S(1)}, u32[]{:S(2)}, u32[]{:S(2)}) collective-permute-start(f32[64,128]{1,0:T(8,128)S(1)} %get-tuple-element.33.behind.refs_0_), channel_id=1, source_target_pairs={{0,24},{1,25},{2,26},{3,27},{4,28},{5,29},{6,30},{7,31},{8,16},{9,... | collective-permute-start | bytes 98312 | tf_op jit(solution)/shard_map/ppermute | solution.py:68
  24.0 19.7 %all-to-all-start = ((f32[8,64,128]{2,1,0:T(8,128)}), f32[8,64,128]{2,1,0:T(8,128)S(1)}, u32[]{:S(2)}, u32[]{:S(2)}) async-start(f32[8,64,128]{2,1,0:T(8,128)} %get-tuple-element.37), calls=%async_computation | async-start | bytes 524288 | tf_op jit(solution)/shard_map/all_to_all | solution.py:366
  31.8 3.8 %collective-permute-start.10 = (bf16[64,2048]{1,0:T(8,128)(2,1)S(1)}, bf16[64,2048]{1,0:T(8,128)(2,1)S(1)}, u32[]{:S(2)}, u32[]{:S(2)}) collective-permute-start(bf16[64,2048]{1,0:T(8,128)(2,1)S(1)} %slice_bitcast_fusion), channel_id=1, source_target_pairs={{0,4},{1,5},{2,6},{3,7},{4,0},{5,1},{6,2},{7,3},{8,12},{9,13},{10,... | collective-permute-start | bytes 786440 | tf_op jit(solution)/shard_map/ppermute | solution.py:68
